TPU v7x, 32 devices: a whole 2x2x4 slice. The times are simulated.
32 devices in a mesh: ctx: 8 (over z, y), fsdp: 4 (over x, core).
Axes of the slice: x: 2, y: 2, z: 4, core: 2. Of those that a mesh axis runs over, the one named last changes fastest.
Arguments:
- tokens: bfloat16 [8192, 1024], P(('fsdp', 'ctx')), may hold values from -6 to 6
- cotangent: bfloat16 [8192, 1024], P(('fsdp', 'ctx')), may hold values from -6 to 6
- gain_attn: bfloat16 [1024], P('fsdp'), may hold values from 0.5 to 1.5
- w_qkv: bfloat16 [1024, 3072], P('fsdp'), may hold values from -0.25 to 0.25
- w_out: bfloat16 [1024, 1024], P('fsdp'), may hold values from -0.75 to 0.75
- gain_ffn: bfloat16 [1024], P('fsdp'), may hold values from 0.5 to 1.5
- w_gate_up: bfloat16 [1024, 5632], P('fsdp'), may hold values from -0.1875 to 0.1875
- w_down: bfloat16 [2816, 1024], P('fsdp'), may hold values from -0.109375 to 0.109375
- lengths: int32 [4, 4], P('fsdp'), may hold values from 1 to 1024, 2048 in all within a row
- block_order: int32 [4, 32], P('fsdp'), may hold values from 0 to 31, each once within a row
Outputs:
- output: bfloat16 [8192, 1024], P(('fsdp', 'ctx'))
- grad_tokens: bfloat16 [8192, 1024], P(('fsdp', 'ctx'))
- grad_gain_attn: float32 [1024], P('fsdp')
- grad_w_qkv: float32 [1024, 3072], P('fsdp')
- grad_w_out: float32 [1024, 1024], P('fsdp')
- grad_gain_ffn: float32 [1024], P('fsdp')
- grad_w_gate_up: float32 [1024, 5632], P('fsdp')
- grad_w_down: float32 [2816, 1024], P('fsdp')
Inputs may be any that keep to these rules, and one draw needn't show every extreme that they name: Each row gives the lengths of the 4 sequences that fill one group's 2048 tokens, in sequence order; the longest is exactly 1024. `block_order`: each row is a permutation of the 32 blocks of one group.
All inputs are finite; a program needn't handle non-finite values.
Results may differ from a plain program's by a relative error of at most 0.024.
Values may be sent and summed in bfloat16 or wider, within the bound.
No kernel may reach another device: no remote copies, remote signals or barrier semaphores. Data moves between devices by JAX's collectives and lax.ppermute only.
A program may use at most 256 MiB of HBM per device.

v0:
```python
import math

import jax
import jax.numpy as jnp
from jax import lax
from jax.sharding import PartitionSpec as P

HEADS = 16


EPS = 1e-05
MASKED = -1e30


def contract_rows(left, right):
    return lax.dot_general(
        left, right, (((0,), (0,)), ((), ())), preferred_element_type=jnp.float32
    )


def against_rows(left, right):
    return lax.dot_general(
        left, right, (((1,), (1,)), ((), ())), preferred_element_type=jnp.float32
    )


def rms_forward(rows):
    inverse = lax.rsqrt(jnp.mean(rows * rows, axis=1, keepdims=True) + EPS)
    return (rows * inverse, inverse)


def rms_backward(normed, inverse, gain, grad_out):
    scaled = grad_out * gain
    inner = jnp.mean(scaled * normed, axis=1, keepdims=True)
    return (inverse * (scaled - normed * inner), jnp.sum(grad_out * normed, axis=0))


def visible(pos_query, seg_query, pos_keys, seg_keys):
    return (seg_query[:, None] == seg_keys[None, :]) & (pos_keys[None, :] <= pos_query[:, None])


def key_block(kv_all, pos_all, seg_all, start, block_rows, heads, depth):
    width = heads * depth
    kv_block = lax.dynamic_slice_in_dim(kv_all, start, block_rows, 0)
    key_heads = kv_block[:, :width].reshape(block_rows, heads, depth)
    value_heads = kv_block[:, width:].reshape(block_rows, heads, depth)
    pos_block = lax.dynamic_slice_in_dim(pos_all, start, block_rows, 0)
    seg_block = lax.dynamic_slice_in_dim(seg_all, start, block_rows, 0)
    return (key_heads, value_heads, pos_block, seg_block)


def attend_forward(query_heads, kv_all, pos_query, seg_query, pos_all, seg_all, scale):
    rows, heads, depth = query_heads.shape
    total_keys = kv_all.shape[0]
    block_rows = min(512, total_keys)

    def one_step(carry, number):
        run_max, run_sum, accum = carry
        key_heads, value_heads, pos_block, seg_block = key_block(
            kv_all, pos_all, seg_all, number * block_rows, block_rows, heads, depth
        )
        allowed = visible(pos_query, seg_query, pos_block, seg_block)[:, None, :]
        scores = (
            jnp.einsum("qhd,khd->qhk", query_heads, key_heads, preferred_element_type=jnp.float32)
            * scale
        )
        scores = jnp.where(allowed, scores, MASKED)
        new_max = jnp.maximum(run_max, jnp.max(scores, axis=2))
        expo = jnp.where(allowed, jnp.exp(scores - new_max[:, :, None]), 0.0)
        factor = jnp.exp(run_max - new_max)
        run_sum = run_sum * factor + jnp.sum(expo, axis=2)
        accum = accum * factor[:, :, None] + jnp.einsum(
            "qhk,khd->qhd",
            expo.astype(jnp.bfloat16),
            value_heads,
            preferred_element_type=jnp.float32,
        )
        return ((new_max, run_sum, accum), None)

    start_state = (
        jnp.full((rows, heads), MASKED, jnp.float32),
        jnp.zeros((rows, heads), jnp.float32),
        jnp.zeros((rows, heads, depth), jnp.float32),
    )
    final_state, unused = lax.scan(
        one_step, start_state, jnp.arange(total_keys // block_rows, dtype=jnp.int32)
    )
    run_max, run_sum, accum = final_state
    return (accum / run_sum[:, :, None], run_max + jnp.log(run_sum))


def attend_backward(
    query_heads, kv_all, grad_heads, delta, log_total, pos_query, seg_query, pos_all, seg_all, scale
):
    rows, heads, depth = query_heads.shape
    width = heads * depth
    total_keys = kv_all.shape[0]
    block_rows = min(512, total_keys)

    def one_step(grad_query, number):
        key_heads, value_heads, pos_block, seg_block = key_block(
            kv_all, pos_all, seg_all, number * block_rows, block_rows, heads, depth
        )
        allowed = visible(pos_query, seg_query, pos_block, seg_block)[:, None, :]
        scores = (
            jnp.einsum("qhd,khd->qhk", query_heads, key_heads, preferred_element_type=jnp.float32)
            * scale
        )
        probs = jnp.where(allowed, jnp.exp(scores - log_total[:, :, None]), 0.0)
        dprob = jnp.einsum(
            "qhd,khd->qhk", grad_heads, value_heads, preferred_element_type=jnp.float32
        )
        grad_scores = (probs * (dprob - delta[:, :, None])).astype(jnp.bfloat16)
        grad_query = grad_query + jnp.einsum(
            "qhk,khd->qhd", grad_scores, key_heads, preferred_element_type=jnp.float32
        )
        grad_keys = (
            jnp.einsum("qhk,qhd->khd", grad_scores, query_heads, preferred_element_type=jnp.float32)
            * scale
        )
        grad_values = jnp.einsum(
            "qhk,qhd->khd",
            probs.astype(jnp.bfloat16),
            grad_heads,
            preferred_element_type=jnp.float32,
        )
        return (
            grad_query,
            jnp.concatenate(
                [grad_keys.reshape(block_rows, width), grad_values.reshape(block_rows, width)],
                axis=1,
            ),
        )

    grad_query, grad_pairs = lax.scan(
        one_step,
        jnp.zeros((rows, heads, depth), jnp.float32),
        jnp.arange(total_keys // block_rows, dtype=jnp.int32),
    )
    return (grad_query * scale, grad_pairs.reshape(total_keys, 2 * width))


def body(
    tokens, cotangent, gain_attn, w_qkv, w_out, gain_ffn, w_gate_up, w_down, lengths, block_order
):
    rows, width = tokens.shape
    heads = HEADS
    depth = width // heads
    scale = depth ** (-0.5)
    ctx_count = lax.axis_size("ctx")
    fsdp_count = lax.axis_size("fsdp")
    group_rows = rows * ctx_count
    factor = 1.0 / math.sqrt(rows * ctx_count * fsdp_count)
    gathered = (
        lax.all_gather(gain_attn, "fsdp", axis=0, tiled=True),
        lax.all_gather(w_qkv, "fsdp", axis=0, tiled=True),
        lax.all_gather(w_out, "fsdp", axis=0, tiled=True),
        lax.all_gather(gain_ffn, "fsdp", axis=0, tiled=True),
        lax.all_gather(w_gate_up, "fsdp", axis=0, tiled=True),
        lax.all_gather(w_down, "fsdp", axis=0, tiled=True),
    )
    gain_one, weight_qkv, weight_out, gain_two, weight_gu, weight_down = gathered
    gain_one = gain_one.astype(jnp.float32)
    gain_two = gain_two.astype(jnp.float32)
    hidden_width = weight_down.shape[0]
    block_size = group_rows // block_order.shape[1]
    pos_all = (
        block_order[0][:, None] * block_size + jnp.arange(block_size, dtype=jnp.int32)[None, :]
    ).reshape(group_rows)
    ends = jnp.cumsum(lengths[0])
    seg_all = jnp.sum((pos_all[:, None] >= ends[None, :]).astype(jnp.int32), axis=1)
    offset = lax.axis_index("ctx") * rows
    pos_query = lax.dynamic_slice_in_dim(pos_all, offset, rows, 0)
    seg_query = lax.dynamic_slice_in_dim(seg_all, offset, rows, 0)
    inputs = tokens.astype(jnp.float32)
    normed_one, inverse_one = rms_forward(inputs)
    attn_in = (normed_one * gain_one).astype(jnp.bfloat16)
    qkv = jnp.dot(attn_in, weight_qkv, preferred_element_type=jnp.float32).astype(jnp.bfloat16)
    query_flat = qkv[:, :width]
    query_heads = query_flat.reshape(rows, heads, depth)
    key_value = qkv[:, width:]
    kv_all = lax.all_gather(key_value, "ctx", axis=0, tiled=True)
    out_heads, log_total = attend_forward(
        query_heads, kv_all, pos_query, seg_query, pos_all, seg_all, scale
    )
    attn_low = out_heads.reshape(rows, width).astype(jnp.bfloat16)
    resid = inputs + jnp.dot(attn_low, weight_out, preferred_element_type=jnp.float32)
    normed_two, inverse_two = rms_forward(resid)
    ffn_in = (normed_two * gain_two).astype(jnp.bfloat16)
    gate_up = jnp.dot(ffn_in, weight_gu, preferred_element_type=jnp.float32)
    gate = gate_up[:, :hidden_width]
    upward = gate_up[:, hidden_width:]
    sigma = jax.nn.sigmoid(gate)
    active = gate * sigma
    hidden = (active * upward).astype(jnp.bfloat16)
    output = (resid + jnp.dot(hidden, weight_down, preferred_element_type=jnp.float32)).astype(
        jnp.bfloat16
    )
    grad_hidden = against_rows(cotangent, weight_down)
    grad_gate = grad_hidden * upward * (sigma + gate * sigma * (1.0 - sigma))
    grad_up = grad_hidden * active
    grad_gu = jnp.concatenate([grad_gate, grad_up], axis=1).astype(jnp.bfloat16)
    grad_ffn_in = against_rows(grad_gu, weight_gu)
    grad_norm_two, grad_gain_two = rms_backward(normed_two, inverse_two, gain_two, grad_ffn_in)
    grad_resid = cotangent.astype(jnp.float32) + grad_norm_two
    grad_branch = grad_resid.astype(jnp.bfloat16)
    grad_attn = against_rows(grad_branch, weight_out).astype(jnp.bfloat16)
    grad_heads = grad_attn.reshape(rows, heads, depth)
    delta = jnp.sum(grad_heads.astype(jnp.float32) * out_heads, axis=2)
    kv_back = lax.all_gather(key_value, "ctx", axis=0, tiled=True)
    grad_query, grad_pair_terms = attend_backward(
        query_heads,
        kv_back,
        grad_heads,
        delta,
        log_total,
        pos_query,
        seg_query,
        pos_all,
        seg_all,
        scale,
    )
    grad_pairs = lax.psum_scatter(
        grad_pair_terms.astype(jnp.bfloat16), "ctx", scatter_dimension=0, tiled=True
    )
    grad_qkv = jnp.concatenate(
        [grad_query.reshape(rows, width).astype(jnp.bfloat16), grad_pairs], axis=1
    )
    grad_attn_in = against_rows(grad_qkv, weight_qkv)
    grad_norm_one, grad_gain_one = rms_backward(normed_one, inverse_one, gain_one, grad_attn_in)
    grad_tokens = (grad_resid + grad_norm_one).astype(jnp.bfloat16)
    terms = (
        grad_gain_one,
        contract_rows(attn_in, grad_qkv),
        contract_rows(attn_low, grad_branch),
        grad_gain_two,
        contract_rows(ffn_in, grad_gu),
        contract_rows(hidden, cotangent),
    )
    partial_shards = (
        lax.psum_scatter(
            terms[0].astype(jnp.bfloat16), "fsdp", scatter_dimension=0, tiled=True
        ).astype(jnp.float32),
        lax.psum_scatter(
            terms[1].astype(jnp.bfloat16), "fsdp", scatter_dimension=0, tiled=True
        ).astype(jnp.float32),
        lax.psum_scatter(
            terms[2].astype(jnp.bfloat16), "fsdp", scatter_dimension=0, tiled=True
        ).astype(jnp.float32),
        lax.psum_scatter(
            terms[3].astype(jnp.bfloat16), "fsdp", scatter_dimension=0, tiled=True
        ).astype(jnp.float32),
        lax.psum_scatter(
            terms[4].astype(jnp.bfloat16), "fsdp", scatter_dimension=0, tiled=True
        ).astype(jnp.float32),
        lax.psum_scatter(
            terms[5].astype(jnp.bfloat16), "fsdp", scatter_dimension=0, tiled=True
        ).astype(jnp.float32),
    )
    shards = (
        lax.psum(partial_shards[0].astype(jnp.bfloat16), "ctx").astype(jnp.float32),
        lax.psum(partial_shards[1].astype(jnp.bfloat16), "ctx").astype(jnp.float32),
        lax.psum(partial_shards[2].astype(jnp.bfloat16), "ctx").astype(jnp.float32),
        lax.psum(partial_shards[3].astype(jnp.bfloat16), "ctx").astype(jnp.float32),
        lax.psum(partial_shards[4].astype(jnp.bfloat16), "ctx").astype(jnp.float32),
        lax.psum(partial_shards[5].astype(jnp.bfloat16), "ctx").astype(jnp.float32),
    )
    return (
        output,
        grad_tokens,
        shards[0] * factor,
        shards[1] * factor,
        shards[2] * factor,
        shards[3] * factor,
        shards[4] * factor,
        shards[5] * factor,
    )


def solution(mesh):
    in_specs = (
        P(("fsdp", "ctx"), None),
        P(("fsdp", "ctx"), None),
        P("fsdp"),
        P("fsdp", None),
        P("fsdp", None),
        P("fsdp"),
        P("fsdp", None),
        P("fsdp", None),
        P("fsdp", None),
        P("fsdp", None),
    )
    out_specs = (
        P(("fsdp", "ctx"), None),
        P(("fsdp", "ctx"), None),
        P("fsdp"),
        P("fsdp", None),
        P("fsdp", None),
        P("fsdp"),
        P("fsdp", None),
        P("fsdp", None),
    )
    return jax.shard_map(body, mesh=mesh, in_specs=in_specs, out_specs=out_specs, check_vma=False)
```

profile of v0, /device:TPU:0, one launch (start us, length us, event | category | flops | bytes accessed | tf_op | source)
XLA Modules:
  0.0 1096.1 jit_solution(1279736065175315214)
XLA Ops:
  8.6 6.0 all-gather
  15.8 42.8 %all-gather.8.cloned.1.call-done = bf16[1024,3072]{1,0:T(8,128)(2,1)} async-done(((bf16[256,3072]{1,0:T(8,128)(2,1)}), bf16[1024,3072]{1,0:T(8,128)(2,1)}) %all-gather.8.cloned.1.call-update) | async-done | bytes 6291472 | tf_op jit(solution)/shard_map/all_gather | solution.py:156
  58.7 4.8 convolution_convert_fusion.3
  67.3 5.2 all-gather.1
  72.8 117.0 %all-gather.10.cloned.1.call-done = bf16[2048,2048]{1,0:T(8,128)(2,1)} async-done(((bf16[256,2048]{1,0:T(8,128)(2,1)}), bf16[2048,2048]{1,0:T(8,128)(2,1)}) %all-gather.10.cloned.1.call-update) | async-done | bytes 8388624 | tf_op jit(solution)/shard_map/all_gather | solution.py:182
  189.8 12.4 %copy.64 = bf16[2048,2048]{0,1:T(8,128)(2,1)} copy(bf16[2048,2048]{1,0:T(8,128)(2,1)} %all-gather.10.cloned.1.call-done) | data formatting | bytes 16777216
  202.1 73.7 %while.28 = (s32[]{:T(128)}, f32[256,16]{0,1:T(8,128)S(1)}, f32[256,16]{0,1:T(8,128)S(1)}, f32[256,16,64]{0,2,1:T(8,128)}, s32[256]{0:T(256)S(1)}, /*index=5*/s3...) while((s32[]{:T(128)}, f32[256,16]{0,1:T(8,128)S(1)}, ...), condition=%wide.region_6.7_spmd.clone, body=%wide.region_3.6_spmd.clone.sunk | while | flops 565334016 | bytes 68434200 | solution.py:85
  205.4 4.8 fusion.113
  210.2 4.6 fusion.114
  222.9 6.1 fusion.113
  229.0 4.6 fusion.114
  234.8 4.4 fusion.116
  242.5 4.8 fusion.113
  247.2 4.6 fusion.114
  253.2 4.4 fusion.116
  260.8 4.8 fusion.113
  265.6 4.6 fusion.114
  271.5 4.4 fusion.116
  279.8 9.9 all-gather.14.cloned.1.call-done
  289.7 9.4 fusion.54
  299.1 35.4 %all-gather.16.cloned.1.call-done = bf16[2816,1024]{1,0:T(8,128)(2,1)} async-done(((bf16[704,1024]{1,0:T(8,128)(2,1)}), bf16[2816,1024]{1,0:T(8,128)(2,1)}) %all-gather.16.cloned.1.call-update) | async-done | bytes 5767184 | tf_op jit(solution)/shard_map/all_gather | solution.py:160
  334.6 8.8 multiply_convert_fusion.1
  343.4 7.5 multiply_reduce_fusion
  356.2 102.9 %while.29 = (s32[]{:T(128)}, f32[256,16,64]{0,2,1:T(8,128)}, bf16[4,512,2048]{2,1,0:T(8,128)(2,1)}, s32[4]{0:T(128)S(1)}, bf16[2048,2048]{0,1:T(8,128)(2,1)}, /*...) while((s32[]{:T(128)}, f32[256,16,64]{0,2,1:T(8,128)}, ...), condition=%wide.region_11.12_spmd.clone, body=%wide.region_10.11_spmd.clone.sunk | while | flops 1369309184 | bytes 118946184 | solution.py:135
  360.8 4.3 fusion.129
  369.2 5.2 fusion.131
  386.3 4.3 fusion.129
  390.6 4.3 fusion.130
  395.0 5.2 fusion.131
  412.1 4.3 fusion.129
  416.4 4.3 fusion.130
  420.8 5.2 fusion.131
  438.0 4.3 fusion.129
  442.3 4.3 fusion.130
  446.6 5.2 fusion.131
  462.5 5.6 convolution_convert_fusion.1
  469.4 7.9 convolution_convert_fusion
  480.8 127.4 %reduce-scatter.6.cloned.1.call-done = bf16[256,2048]{1,0:T(8,128)(2,1)} async-done(((bf16[2048,2048]{1,0:T(8,128)(2,1)}), bf16[256,2048]{1,0:T(8,128)(2,1)}) %reduce-scatter.6.cloned.1.call-update) | async-done | bytes 1048592 | tf_op jit(solution)/shard_map/reduce_scatter | solution.py:223
  608.2 5.8 convolution_convert_fusion.2
  614.1 27.8 %reduce-scatter.10.cloned.1.call-done = bf16[256,1024]{1,0:T(8,128)(2,1)} async-done(((bf16[1024,1024]{1,0:T(8,128)(2,1)}), bf16[256,1024]{1,0:T(8,128)(2,1)}) %reduce-scatter.10.cloned.1.call-update) | async-done | bytes 524304 | tf_op jit(solution)/shard_map/reduce_scatter | solution.py:247
  641.9 58.0 %reduce-scatter.14.cloned.1.call-done = bf16[704,1024]{1,0:T(8,128)(2,1)} async-done(((bf16[2816,1024]{1,0:T(8,128)(2,1)}), bf16[704,1024]{1,0:T(8,128)(2,1)}) %reduce-scatter.14.cloned.1.call-update) | async-done | bytes 1441808 | tf_op jit(solution)/shard_map/reduce_scatter | solution.py:256
  699.9 95.0 %reduce-scatter.12.cloned.1.call-done = bf16[256,5632]{1,0:T(8,128)(2,1)} async-done(((bf16[1024,5632]{1,0:T(8,128)(2,1)}), bf16[256,5632]{1,0:T(8,128)(2,1)}) %reduce-scatter.12.cloned.1.call-update) | async-done | bytes 2883600 | tf_op jit(solution)/shard_map/reduce_scatter | solution.py:253
  794.9 61.0 %reduce-scatter.8.cloned.1.call-done = bf16[256,3072]{1,0:T(8,128)(2,1)} async-done(((bf16[1024,3072]{1,0:T(8,128)(2,1)}), bf16[256,3072]{1,0:T(8,128)(2,1)}) %reduce-scatter.8.cloned.1.call-update) | async-done | bytes 1572880 | tf_op jit(solution)/shard_map/reduce_scatter | solution.py:244
  857.1 5.6 fusion.35
  862.8 4.8 fusion.42
  867.6 6.1 all-reduce.4
  873.8 22.6 %all-reduce.2 = (bf16[256]{0:T(256)(128)(2,1)S(1)}, bf16[256]{0:T(256)(128)(2,1)S(1)}) all-reduce(bf16[256]{0:T(256)(128)(2,1)S(1)} %dynamic-slice.1, bf16[256]{0:T(256)(128)(2,1)S(1)} %dynamic-slice.3), channel_id=1, replica_groups=mesh['ctx'=8,'fsdp'=4] {'ctx'}, use_global_device_ids=true, to_apply=%region_16.17 | all-reduce | flops 512 | bytes 2048 | tf_op jit(solution)/shard_map/psum | solution.py:261
  898.1 181.6 %all-reduce.7.cloned.1.call-done = (bf16[256,3072]{1,0:T(8,128)(2,1)}, bf16[256,1024]{1,0:T(8,128)(2,1)}, bf16[256,5632]{1,0:T(8,128)(2,1)}, bf16[704,1024]{1,0:T(8,128)(2,1)}) async-done(((bf16[256,3072]{1,0:T(8,128)(2,1)}, bf16[256,1024]{1,0:T(8,128)(2,1)}, bf16[256,5632]{1,0:T(8,128)(2,1)}, bf16[704,1024]{1,0:T(8,128)(2,1)}), (bf16[256,3072]{1,0:T(8,128)(2,1)}, bf16[256,1024]{1,0:T(8,128)(2,1)}, ...) | async-done | bytes 6422544 | tf_op jit(solution)/shard_map/psum | solution.py:262
  (234 shorter events, 104.0 us)
Async XLA Ops:
  7.2 51.5 %all-gather.8.cloned.1.call-start = ((), (), s32[]{:S(2)}) async-start(), calls=%async_computation.5 | async-start | bytes 7864320 | tf_op jit(solution)/shard_map/all_gather | solution.py:156
  7.9 181.9 %all-gather.10.cloned.1.call-start = ((), (), s32[]{:S(2)}) async-start(), calls=%async_computation.6 | async-start | bytes 9437184 | tf_op jit(solution)/shard_map/all_gather | solution.py:182
  14.6 48.9 %copy-start.23 = (f32[4,1,256]{2,1,0:T(1,128)}, f32[4,1,256]{2,1,0:T(1,128)S(1)}, u32[]{:S(2)}) copy-start(f32[4,1,256]{2,1,0:T(1,128)S(1)} %convert_element_type.150) | copy-start | bytes 12292
  15.8 47.7 %copy-start.25 = (f32[256]{0:T(256)}, f32[256]{0:T(256)S(1)}, u32[]{:S(2)}) copy-start(f32[256]{0:T(256)S(1)} %add_rsqrt_fusion.1) | copy-start | bytes 3076
  63.6 3.3 copy-start.28
  63.6 3.7 copy-start.29
  64.7 212.5 %all-gather.12.cloned.1.call-start = ((), (), s32[]{:S(2)}) async-start(), calls=%async_computation.7 | async-start | bytes 2621440 | tf_op jit(solution)/shard_map/all_gather | solution.py:157
  65.4 224.3 %all-gather.14.cloned.1.call-start = ((), (), s32[]{:S(2)}) async-start(), calls=%async_computation.8 | async-start | bytes 14417920 | tf_op jit(solution)/shard_map/all_gather | solution.py:159
  66.0 268.6 %all-gather.16.cloned.1.call-start = ((), (), s32[]{:S(2)}) async-start(), calls=%async_computation.9 | async-start | bytes 7208960 | tf_op jit(solution)/shard_map/all_gather | solution.py:160
  66.6 541.7 %reduce-scatter.6.cloned.1.call-start = ((), (), s32[]{:S(2)}) async-start(), calls=%async_computation.10 | async-start | bytes 9437184 | tf_op jit(solution)/shard_map/reduce_scatter | solution.py:223
  202.1 75.1 %copy-start.8 = (bf16[256,1024]{1,0:T(8,128)(2,1)S(1)}, bf16[256,1024]{1,0:T(8,128)(2,1)}, u32[]{:S(2)}) copy-start(bf16[256,1024]{1,0:T(8,128)(2,1)} %param.14) | copy-start | bytes 1572868
  210.2 5.9 copy-start
  229.0 5.8 copy-start
  247.2 6.0 copy-start
  265.6 5.9 copy-start
  277.2 22.0 %copy-start.9 = (bf16[256,16,64]{0,2,1:T(8,128)(2,1)}, bf16[256,16,64]{0,2,1:T(8,128)(2,1)S(1)}, u32[]{:S(2)}) copy-start(bf16[256,16,64]{0,2,1:T(8,128)(2,1)S(1)} %fusion.45) | copy-start | bytes 1572868
  279.8 71.2 %copy-start.3 = (f32[256,1024]{1,0:T(8,128)}, f32[256,1024]{1,0:T(8,128)S(1)}, u32[]{:S(2)}) copy-start(f32[256,1024]{1,0:T(8,128)S(1)} %get-tuple-element.410) | copy-start | bytes 3145732
  289.7 44.9 %copy-start.15 = (bf16[256,1024]{1,0:T(8,128)(2,1)S(1)}, bf16[256,1024]{1,0:T(8,128)(2,1)}, u32[]{:S(2)}) copy-start(bf16[256,1024]{1,0:T(8,128)(2,1)} %param.15) | copy-start | bytes 1572868
  343.4 7.6 copy-start.19
  343.4 7.6 copy-start.20
  343.4 7.6 copy-start.16
  343.4 7.9 copy-start.7
  351.3 4.8 copy-start.5
  351.3 3.6 copy-start.11
  360.4 4.7 copy-start.2
  365.1 4.0 copy-start.14
  369.2 5.2 copy-start.1
  385.9 4.7 copy-start.2
  390.6 4.3 copy-start.14
  395.0 5.2 copy-start.1
  411.7 4.7 copy-start.2
  416.4 4.3 copy-start.14
  420.8 5.2 copy-start.1
  437.6 4.7 copy-start.2
  442.3 4.3 copy-start.14
  446.6 5.2 copy-start.1
  459.1 3.4 copy-start.17
  459.1 182.8 %reduce-scatter.10.cloned.1.call-start = ((), (), s32[]{:S(2)}) async-start(), calls=%async_computation.12 | async-start | bytes 2621440 | tf_op jit(solution)/shard_map/reduce_scatter | solution.py:247
  462.5 237.5 %reduce-scatter.14.cloned.1.call-start = ((), (), s32[]{:S(2)}) async-start(), calls=%async_computation.14 | async-start | bytes 7208960 | tf_op jit(solution)/shard_map/reduce_scatter | solution.py:256
  468.2 326.7 %reduce-scatter.12.cloned.1.call-start = ((), (), s32[]{:S(2)}) async-start(), calls=%async_computation.13 | async-start | bytes 14417920 | tf_op jit(solution)/shard_map/reduce_scatter | solution.py:253
  477.3 130.9 %copy-start.24 = (f32[4,1,256]{2,1,0:T(1,128)S(1)}, f32[4,1,256]{2,1,0:T(1,128)}, u32[]{:S(2)}) copy-start(f32[4,1,256]{2,1,0:T(1,128)} %copy-done.23) | copy-start | bytes 12292
  477.3 130.9 %copy-start.26 = (f32[256]{0:T(256)S(1)}, f32[256]{0:T(256)}, u32[]{:S(2)}) copy-start(f32[256]{0:T(256)} %copy-done.25) | copy-start | bytes 3076
  477.3 378.5 %reduce-scatter.8.cloned.1.call-start = ((), (), s32[]{:S(2)}) async-start(), calls=%async_computation.11 | async-start | bytes 7864320 | tf_op jit(solution)/shard_map/reduce_scatter | solution.py:244
  614.1 241.8 %copy-start.30 = (u32[32]{0:T(128)S(1)}, u32[32]{0:T(128)}, u32[]{:S(2)}) copy-start(u32[32]{0:T(128)} %constant.83) | copy-start | bytes 388
  614.1 465.5 %all-reduce.7.cloned.1.call-start = ((), (), s32[]{:S(2)}) async-start(), calls=%async_computation.15 | async-start | bytes 12845056 | tf_op jit(solution)/shard_map/psum | solution.py:262
  857.1 5.6 copy-start.21
  1079.6 3.6 copy-start.22
  1079.6 4.7 copy-start.12
  (9 other events, 17.0 us)
Sparse Core Ops, SparseCore 0:
  9.6 49.0 all-gather.7
  64.8 124.9 all-gather.9
  191.3 20.7 all-gather.11
  213.5 76.1 all-gather.13
  291.1 43.3 all-gather.15
  459.2 148.9 reduce-scatter.5
  611.5 30.4 reduce-scatter.9
  645.0 54.8 reduce-scatter.13
  702.7 92.1 reduce-scatter.11
  797.5 58.3 reduce-scatter.7
  860.5 219.0 all-reduce.6
where the time goes:
time: 1100 us
  waiting for transfers between devices  758 us (69%)
  matrix products  169 us (15%)
  local copies, waits for them, and re-layouts  63.6 us (6%)
  other arithmetic  44.1 us (4%)
  blocking collectives  39.9 us (4%)
  between operations  14.9 us (1%)
    psum x1, waiting for transfers between devices, body(): lax.psum(partial_shards[1].astype(jnp.bfloat16), 'ctx').astype(jnp.float32)  182 us
    reduce_scatter x1, waiting for transfers between devices, body(): lax.psum_scatter(grad_pair_terms.astype(jnp.bfloat16), 'ctx', scatter_dim...  127 us
    all_gather x1, waiting for transfers between devices, body(): kv_all = lax.all_gather(key_value, 'ctx', axis=0, tiled=True)  117 us
    reduce_scatter x1, waiting for transfers between devices, body(): lax.psum_scatter(terms[4].astype(jnp.bfloat16), 'fsdp', scatter_dimension...  95 us
    reduce_scatter x1, waiting for transfers between devices, body(): lax.psum_scatter(terms[1].astype(jnp.bfloat16), 'fsdp', scatter_dimension...  61 us
    reduce_scatter x1, waiting for transfers between devices, body(): lax.psum_scatter(terms[5].astype(jnp.bfloat16), 'fsdp', scatter_dimension...  58 us
    all_gather x1, waiting for transfers between devices, body(): lax.all_gather(w_qkv, 'fsdp', axis=0, tiled=True)  42.8 us
    all_gather x1, waiting for transfers between devices, body(): lax.all_gather(w_down, 'fsdp', axis=0, tiled=True)  35.4 us
  transfers between devices with their start and end apart: 11, of which 10 were waited for; matrix products, arithmetic and copies ran while one was open for 12% of the time, Pallas kernels for 0%

commit v1 on v0

v1 whole, which is shorter than its diff:
```python
import functools
import math

import jax
import jax.numpy as jnp
from jax import lax
from jax.experimental import pallas as pl
from jax.experimental.pallas import tpu as pltpu
from jax.sharding import PartitionSpec as P

HEADS = 16
TILE = 256


EPS = 1e-05
MASKED=-1e30
def nt(a,b): return lax.dot_general(a,b,(((1,),(1,)),((),())),preferred_element_type=jnp.float32)
def nn(a,b): return lax.dot_general(a,b,(((1,),(0,)),((),())),preferred_element_type=jnp.float32)

def first_tile(ends_ref, nseq, position, tile):
    start = jnp.int32(0)
    for i in range(nseq - 1):
        start = jnp.where(ends_ref[i] <= position, ends_ref[i], start)
    return start // tile

def last_tile(ends_ref, nseq, position, tile):
    end = ends_ref[nseq - 1]
    for i in range(nseq - 2, -1, -1):
        end = jnp.where(ends_ref[i] > position, ends_ref[i], end)
    return (end - 1) // tile

def seen(ends_ref, nseq, query_start, key_start, tile):
    pos_query = query_start + lax.broadcasted_iota(jnp.int32, (1, tile), 1)
    start = jnp.zeros((1, tile), jnp.int32)
    for i in range(nseq - 1):
        start = jnp.where(pos_query >= ends_ref[i], ends_ref[i], start)
    pos_key = key_start + lax.broadcasted_iota(jnp.int32, (tile, tile), 0)
    return (pos_key <= pos_query) & (pos_key >= start)

def head_lanes(x, head, heads, depth):
    if heads == 1:
        return x
    lane = lax.broadcasted_iota(jnp.int32, x.shape, 1)
    return jnp.where((lane >= head * depth) & (lane < (head + 1) * depth), x, jnp.zeros_like(x))

def fwd_kernel(meta, ends_ref, place_ref, *refs):
    n, heads, depth, tile, block, nseq = meta
    qkv_refs, out_refs = refs[:n], refs[n:2*n]
    out_t_ref, lse_ref = refs[2*n], refs[2*n+1]
    q_ref, k_ref, v_ref, o_ref = refs[2*n+2:]
    width = heads*depth
    scale = depth ** (-0.5)
    per = qkv_refs[0].shape[0] // block
    for s in range(n):
        for b in range(per):
            dst = pl.ds(pl.multiple_of(place_ref[s*per+b]*block, block), block)
            src = pl.ds(b*block, block)
            q = qkv_refs[s][src, 0:width].astype(jnp.float32)*scale
            for h in range(heads):
                q_ref[h, dst, :] = head_lanes(q, h, heads, depth).astype(jnp.bfloat16)
            k_ref[dst, :] = qkv_refs[s][src, width:2*width]
            v_ref[dst, :] = qkv_refs[s][src, 2*width:]
    tiles = q_ref.shape[1] // tile
    def one_query(t, _):
        rows = pl.ds(pl.multiple_of(t*tile, tile), tile)
        qs = [q_ref[h, rows, :] for h in range(heads)]
        def one_key(j, carry):
            keys = pl.ds(pl.multiple_of(j*tile, tile), tile)
            k = k_ref[keys, :]
            v_t = jnp.transpose(v_ref[keys, :].astype(jnp.float32)).astype(jnp.bfloat16)
            mask = seen(ends_ref, nseq, t*tile, j*tile, tile)
            new = []
            for h in range(heads):
                m, l, acc = carry[h]
                s = jnp.where(mask, nt(k, qs[h]), MASKED)
                m_new = jnp.maximum(m, jnp.max(s, axis=0, keepdims=True))
                e = jnp.exp(s - m_new)
                alpha = jnp.exp(m - m_new)
                l = l*alpha + jnp.sum(e, axis=0, keepdims=True)
                acc = acc*alpha + nn(v_t[h*depth:(h+1)*depth], e.astype(jnp.bfloat16))
                new.append((m_new, l, acc))
            return tuple(new)
        init = tuple((jnp.full((1,tile),MASKED,jnp.float32), jnp.zeros((1,tile),jnp.float32), jnp.zeros((depth,tile),jnp.float32)) for _ in range(heads))
        final = lax.fori_loop(first_tile(ends_ref, nseq, t*tile, tile), t+1, one_key, init)
        outs = []
        for h in range(heads):
            m, l, acc = final[h]
            outs.append(acc / l)
            lse_ref[h:h+1, rows] = m + jnp.log(l)
        out_t = jnp.concatenate(outs, axis=0) if heads > 1 else outs[0]
        out_t_ref[:, rows] = out_t
        o_ref[rows, :] = jnp.transpose(out_t).astype(jnp.bfloat16)
        return 0
    lax.fori_loop(0, tiles, one_query, 0)
    for s in range(n):
        for b in range(per):
            src = pl.ds(pl.multiple_of(place_ref[s*per+b]*block, block), block)
            out_refs[s][pl.ds(b*block, block), :] = o_ref[src, :]

def bwd_kernel(meta, ends_ref, place_ref, *refs):
    n, heads, depth, tile, block, nseq = meta
    qkv_refs, grad_refs = refs[:n], refs[n:2*n]
    out_t_ref, lse_ref = refs[2*n], refs[2*n+1]
    dqkv_refs = refs[2*n+2:3*n+2]
    q_ref, k_ref, v_ref, g_ref, k_t_ref, delta_ref, dq_t_ref, dq_ref, dk_ref, dv_ref = refs[3*n+2:]
    width = heads*depth
    scale = depth ** (-0.5)
    per = qkv_refs[0].shape[0] // block
    total = k_ref.shape[0]
    for s in range(n):
        for b in range(per):
            dst = pl.ds(pl.multiple_of(place_ref[s*per+b]*block, block), block)
            src = pl.ds(b*block, block)
            q = qkv_refs[s][src, 0:width].astype(jnp.float32)*scale
            g = grad_refs[s][src, :]
            for h in range(heads):
                q_ref[h, dst, :] = head_lanes(q, h, heads, depth).astype(jnp.bfloat16)
                g_ref[h, dst, :] = head_lanes(g.astype(jnp.float32), h, heads, depth).astype(jnp.bfloat16)
            k_ref[dst, :] = qkv_refs[s][src, width:2*width]
            v_ref[dst, :] = qkv_refs[s][src, 2*width:]
    tiles = total // tile
    def prepare(t, _):
        rows = pl.ds(pl.multiple_of(t*tile, tile), tile)
        k_t_ref[:, rows] = jnp.transpose(k_ref[rows, :].astype(jnp.float32)).astype(jnp.bfloat16)
        g = g_ref[0, rows, :].astype(jnp.float32)
        for h in range(1, heads):
            g = g + g_ref[h, rows, :].astype(jnp.float32)
        prod = jnp.transpose(g) * out_t_ref[:, rows]
        for h in range(heads):
            delta_ref[h:h+1, rows] = jnp.sum(prod[h*depth:(h+1)*depth], axis=0, keepdims=True)
        dq_t_ref[:, rows] = jnp.zeros((width, tile), jnp.float32)
        return 0
    lax.fori_loop(0, tiles, prepare, 0)
    def one_key(j, _):
        keys = pl.ds(pl.multiple_of(j*tile, tile), tile)
        k = k_ref[keys, :]
        v = v_ref[keys, :]
        k_t = k_t_ref[:, keys]
        dk_ref[keys, :] = jnp.zeros((tile, width), jnp.float32)
        dv_ref[keys, :] = jnp.zeros((tile, width), jnp.float32)
        def one_query(t, _):
            rows = pl.ds(pl.multiple_of(t*tile, tile), tile)
            mask = seen(ends_ref, nseq, t*tile, j*tile, tile)
            dk = dk_ref[keys, :]
            dv = dv_ref[keys, :]
            for h in range(heads):
                q = q_ref[h, rows, :]
                g = g_ref[h, rows, :]
                s = nt(k, q)
                p = jnp.where(mask, jnp.exp(s - lse_ref[h:h+1, rows]), 0.0)
                dp = nt(v, g)
                ds = (p*(dp - delta_ref[h:h+1, rows])).astype(jnp.bfloat16)
                dv = dv + nn(p.astype(jnp.bfloat16), g)
                dk = dk + nn(ds, q)
                part = pl.ds(h*depth, depth)
                dq_t_ref[part, rows] = dq_t_ref[part, rows] + nn(k_t[h*depth:(h+1)*depth], ds)
            dk_ref[keys, :] = dk
            dv_ref[keys, :] = dv
            return 0
        lax.fori_loop(j, last_tile(ends_ref, nseq, j*tile + tile - 1, tile) + 1, one_query, 0)
        return 0
    lax.fori_loop(0, tiles, one_key, 0)
    def finish(t, _):
        rows = pl.ds(pl.multiple_of(t*tile, tile), tile)
        dq_ref[rows, :] = (jnp.transpose(dq_t_ref[:, rows])*scale).astype(jnp.bfloat16)
        return 0
    lax.fori_loop(0, tiles, finish, 0)
    for s in range(n):
        for b in range(per):
            src = pl.ds(pl.multiple_of(place_ref[s*per+b]*block, block), block)
            dst = pl.ds(b*block, block)
            dqkv_refs[s][dst, 0:width] = dq_ref[src, :]
            dqkv_refs[s][dst, width:2*width] = dk_ref[src, :].astype(jnp.bfloat16)
            dqkv_refs[s][dst, 2*width:] = dv_ref[src, :].astype(jnp.bfloat16)

SM=pl.BlockSpec(memory_space=pltpu.SMEM)
VM=pl.BlockSpec(memory_space=pltpu.VMEM)
def attention_forward(ends, place, qkv, heads, depth, block, tile):
    n=len(qkv); rows=qkv[0].shape[0]; total=n*rows; width=heads*depth
    meta=(n,heads,depth,tile,block,ends.shape[0])
    pairs=total*total//4
    res=pl.pallas_call(functools.partial(fwd_kernel,meta),
        out_shape=[jax.ShapeDtypeStruct((rows,width),jnp.bfloat16)]*n+[jax.ShapeDtypeStruct((width,total),jnp.float32),jax.ShapeDtypeStruct((heads,total),jnp.float32)],
        in_specs=[SM,SM]+[VM]*n, out_specs=[VM]*(n+2),
        scratch_shapes=[pltpu.VMEM((heads,total,width),jnp.bfloat16)]+[pltpu.VMEM((total,width),jnp.bfloat16)]*3,
        cost_estimate=pl.CostEstimate(flops=4*pairs*width,bytes_accessed=10*total*width,transcendentals=pairs*heads),
        name="attention_forward")(ends,place,*qkv)
    return list(res[:n]),res[n],res[n+1]
def attention_backward(ends, place, qkv, grads, out_t, lse, heads, depth, block, tile):
    n=len(qkv); rows=qkv[0].shape[0]; total=n*rows; width=heads*depth
    meta=(n,heads,depth,tile,block,ends.shape[0])
    pairs=total*total//4
    f32=jnp.float32; b16=jnp.bfloat16
    return pl.pallas_call(functools.partial(bwd_kernel,meta),
        out_shape=[jax.ShapeDtypeStruct((rows,3*width),b16)]*n,
        in_specs=[SM,SM]+[VM]*(2*n+2), out_specs=[VM]*n,
        scratch_shapes=[pltpu.VMEM((heads,total,width),b16),pltpu.VMEM((total,width),b16),pltpu.VMEM((total,width),b16),pltpu.VMEM((heads,total,width),b16),
          pltpu.VMEM((width,total),b16),pltpu.VMEM((heads,total),f32),pltpu.VMEM((width,total),f32),pltpu.VMEM((total,width),b16),pltpu.VMEM((total,width),f32),pltpu.VMEM((total,width),f32)],
        cost_estimate=pl.CostEstimate(flops=10*pairs*width,bytes_accessed=20*total*width,transcendentals=pairs*heads),
        name="attention_backward")(ends,place,*qkv,*grads,out_t,lse)


def contract_rows(left, right):
    return lax.dot_general(
        left, right, (((0,), (0,)), ((), ())), preferred_element_type=jnp.float32
    )


def against_rows(left, right):
    return lax.dot_general(
        left, right, (((1,), (1,)), ((), ())), preferred_element_type=jnp.float32
    )


def rms_forward(rows):
    inverse = lax.rsqrt(jnp.mean(rows * rows, axis=1, keepdims=True) + EPS)
    return (rows * inverse, inverse)


def ring_of(count):
    if count % 4 or count < 8:
        return list(range(count))
    across = count // 4
    order = []
    for along in range(4):
        columns = range(1, across) if along % 2 == 0 else range(across - 1, 0, -1)
        order += [along * across + column for column in columns]
    return order + [along * across for along in reversed(range(4))]


def ring_shift(value, ring, step):
    count = len(ring)
    return lax.ppermute(
        value, "ctx", [(ring[i], ring[(i + step) % count]) for i in range(count)]
    )


def ring_gather(value, ring):
    count = len(ring)
    half = count // 2
    slots = [None] * count
    slots[0] = value
    up = down = value
    for step in range(1, half):
        up = ring_shift(up, ring, 1)
        down = ring_shift(down, ring, -1)
        slots[count - step] = up
        slots[step] = down
    cut = value.shape[0] // 2
    slots[half] = (ring_shift(up[:cut], ring, 1), ring_shift(down[cut:], ring, -1))
    return slots


def ring_scatter(chunk, ring):
    count = len(ring)
    half = count // 2
    far = chunk(half)
    cut = far.shape[0] // 2
    up = ring_shift(far[:cut], ring, 1)
    down = ring_shift(far[cut:], ring, -1)
    for step in range(half - 1, 0, -1):
        mine_up, mine_down = chunk(step), chunk(count - step)
        if step == half - 1:
            mine_up = jnp.concatenate([add_low(mine_up[:cut], up), mine_up[cut:]], axis=0)
            mine_down = jnp.concatenate([mine_down[:cut], add_low(mine_down[cut:], down)], axis=0)
        else:
            mine_up, mine_down = add_low(mine_up, up), add_low(mine_down, down)
        up = ring_shift(mine_up, ring, 1)
        down = ring_shift(mine_down, ring, -1)
    return chunk(0).astype(jnp.float32) + up.astype(jnp.float32) + down.astype(jnp.float32)


def add_low(left, right):
    return (left.astype(jnp.float32) + right.astype(jnp.float32)).astype(jnp.bfloat16)


def partner(value, fsdp_count):
    return lax.ppermute(value, "fsdp", [(i, i ^ 1) for i in range(fsdp_count)])


def chip_shift(value, fsdp_count, step):
    return lax.ppermute(
        value, "fsdp", [(i, (i + 2 * step) % fsdp_count) for i in range(fsdp_count)]
    )


def side_gather(value, fsdp_count):
    slots = []
    for step in range(fsdp_count // 2):
        near = value if step == 0 else chip_shift(value, fsdp_count, -step)
        slots += [near, partner(near, fsdp_count)]
    return slots


def side_scatter(terms, fsdp_count):
    total = None
    for step in reversed(range(fsdp_count // 2)):
        near = terms[2 * step].astype(jnp.float32) + partner(
            terms[2 * step + 1], fsdp_count
        ).astype(jnp.float32)
        if step:
            near = chip_shift(near.astype(jnp.bfloat16), fsdp_count, step).astype(jnp.float32)
        total = near if total is None else total + near
    return total


def side_exchange(pieces, fsdp_count):
    received = []
    for step in range(fsdp_count // 2):
        for flip in (0, 1):
            piece = pieces[2 * step + flip]
            if step or flip:
                piece = lax.ppermute(
                    piece,
                    "fsdp",
                    [(i, ((i + 2 * step) % fsdp_count) ^ flip) for i in range(fsdp_count)],
                )
            received.append(piece)
    chips = fsdp_count // 2
    return [received[2 * ((chips - step) % chips) + flip] for step in range(chips) for flip in (0, 1)]


def pick(array, index):
    return lax.dynamic_index_in_dim(array, index, 0, keepdims=False)


def body(
    tokens, cotangent, gain_attn, w_qkv, w_out, gain_ffn, w_gate_up, w_down, lengths, block_order
):
    rows, width = tokens.shape
    heads = HEADS
    depth = width // heads
    ctx_count = lax.axis_size("ctx")
    fsdp_count = lax.axis_size("fsdp")
    group_rows = rows * ctx_count
    factor = 1.0 / math.sqrt(rows * ctx_count * fsdp_count)
    shard = width // fsdp_count
    hidden = w_down.shape[0]
    own_heads = heads // ctx_count
    own_width = own_heads * depth
    ring = ring_of(ctx_count)
    place_in_ring = [ring.index(i) for i in range(ctx_count)]
    me = jnp.asarray(place_in_ring, jnp.int32)[lax.axis_index("ctx")]
    owner = jnp.asarray(ring, jnp.int32)[(me + jnp.arange(ctx_count, dtype=jnp.int32)) % ctx_count]
    owners = [owner[k] for k in range(ctx_count)]
    my_chip, my_core = lax.axis_index("fsdp") // 2, lax.axis_index("fsdp") % 2
    sides = [
        ((my_chip + step) % (fsdp_count // 2)) * 2 + (my_core ^ flip)
        for step in range(fsdp_count // 2)
        for flip in (0, 1)
    ]
    block_size = group_rows // block_order.shape[1]
    per_shard = rows // block_size
    ends = jnp.cumsum(lengths[0]).astype(jnp.int32)
    place = block_order[0].reshape(ctx_count, per_shard)[owner].reshape(-1)

    gains = side_gather(jnp.stack([gain_attn, gain_ffn]), fsdp_count)
    gain_pair = jnp.zeros((2, fsdp_count, shard), jnp.bfloat16)
    for slot, side in zip(gains, sides):
        gain_pair = lax.dynamic_update_slice(gain_pair, slot[:, None, :], (0, side, 0))
    gain_pair = gain_pair.reshape(2, width).astype(jnp.float32)
    gain_one, gain_two = gain_pair[0], gain_pair[1]

    inputs = tokens.astype(jnp.float32)
    normed_one, inverse_one = rms_forward(inputs)
    attn_in = (normed_one * gain_one).astype(jnp.bfloat16)
    attn_slots = ring_gather(attn_in, ring)

    def stack_sides(slots):
        whole = jnp.zeros((fsdp_count,) + slots[0].shape, slots[0].dtype)
        for slot, side in zip(slots, sides):
            whole = lax.dynamic_update_slice_in_dim(whole, slot[None], side, 0)
        return whole

    columns = w_qkv.reshape(shard, 3, ctx_count, own_width)
    slice_mine = lax.dynamic_index_in_dim(columns, owners[0], 2, keepdims=False).reshape(shard, 3 * own_width)
    weight_mine = stack_sides(side_gather(slice_mine, fsdp_count)).reshape(width, 3 * own_width)

    gate_parts = w_gate_up.reshape(shard, 2, fsdp_count, hidden)
    gate_pieces = [
        lax.dynamic_index_in_dim(gate_parts, side, 2, keepdims=False).reshape(shard, 2 * hidden)
        for side in sides
    ]
    weight_gu = stack_sides(side_exchange(gate_pieces, fsdp_count)).reshape(width, 2 * hidden)
    weight_out = stack_sides(side_gather(w_out, fsdp_count)).reshape(ctx_count, own_width, width)
    weight_out = jnp.concatenate([pick(weight_out, owners[k]) for k in range(ctx_count)], axis=0)
    cot_all = jnp.concatenate(side_gather(cotangent, fsdp_count), axis=0)
    weight_qkv = stack_sides(side_gather(w_qkv, fsdp_count)).reshape(width, 3 * width)

    def project(value):
        return jnp.dot(value, weight_mine, preferred_element_type=jnp.float32).astype(jnp.bfloat16)

    half = ctx_count // 2
    attn_slots[half] = jnp.concatenate(attn_slots[half], axis=0)
    qkv = [project(slot) for slot in attn_slots]
    out_slots, out_t, log_total = attention_forward(
        ends, place, qkv, own_heads, depth, block_size, TILE
    )
    attn_parts = [out_slots[0]] + [None] * (ctx_count - 1)
    for k in range(1, ctx_count):
        attn_parts[ctx_count - k] = ring_shift(out_slots[k], ring, k)
    attn_low = jnp.concatenate(attn_parts, axis=1)
    resid = inputs + jnp.dot(attn_low, weight_out, preferred_element_type=jnp.float32)
    normed_two, inverse_two = rms_forward(resid)
    ffn_in = (normed_two * gain_two).astype(jnp.bfloat16)
    ffn_all = jnp.concatenate(side_gather(ffn_in, fsdp_count), axis=0)

    gate_up = jnp.dot(ffn_all, weight_gu, preferred_element_type=jnp.float32)
    gate = gate_up[:, :hidden]
    upward = gate_up[:, hidden:]
    sigma = jax.nn.sigmoid(gate)
    active = gate * sigma
    hidden_low = (active * upward).astype(jnp.bfloat16)
    grad_hidden = against_rows(cot_all, w_down)
    grad_gate = grad_hidden * upward * (sigma + gate * sigma * (1.0 - sigma))
    grad_up = grad_hidden * active
    grad_gu = jnp.concatenate([grad_gate, grad_up], axis=1).astype(jnp.bfloat16)
    grad_ffn_terms = against_rows(grad_gu, weight_gu).astype(jnp.bfloat16).reshape(fsdp_count, rows, width)
    grad_ffn_in = side_scatter([grad_ffn_terms[i] for i in range(fsdp_count)], fsdp_count)
    out_terms = jnp.dot(hidden_low, w_down, preferred_element_type=jnp.float32)
    out_terms = out_terms.astype(jnp.bfloat16).reshape(fsdp_count, rows, width)
    output = (
        resid + side_scatter([out_terms[i] for i in range(fsdp_count)], fsdp_count)
    ).astype(jnp.bfloat16)

    scaled_two = grad_ffn_in * gain_two
    inner_two = jnp.mean(scaled_two * normed_two, axis=1, keepdims=True)
    grad_resid = cotangent.astype(jnp.float32) + inverse_two * (scaled_two - normed_two * inner_two)
    grad_branch = grad_resid.astype(jnp.bfloat16)
    grad_attn = against_rows(grad_branch, weight_out).astype(jnp.bfloat16)
    grad_slots = [grad_attn[:, :own_width]] + [None] * (ctx_count - 1)
    for k in range(1, ctx_count):
        grad_slots[ctx_count - k] = ring_shift(grad_attn[:, k * own_width : (k + 1) * own_width], ring, k)
    grad_qkv = attention_backward(
        ends, place, qkv, grad_slots, out_t, log_total, own_heads, depth, block_size, TILE
    )
    grad_parts = [grad_qkv[0]] + [None] * (ctx_count - 1)
    for k in range(1, ctx_count):
        grad_parts[ctx_count - k] = ring_shift(grad_qkv[k], ring, k)
    by_owner = weight_qkv.reshape(width, 3, ctx_count, own_width)
    weight_rel = jnp.concatenate(
        [
            lax.dynamic_index_in_dim(by_owner, owners[k], 2, keepdims=False).reshape(width, 3 * own_width)
            for k in range(ctx_count)
        ],
        axis=1,
    )
    grad_attn_in = against_rows(jnp.concatenate(grad_parts, axis=1), weight_rel)
    scaled_one = grad_attn_in * gain_one
    inner_one = jnp.mean(scaled_one * normed_one, axis=1, keepdims=True)
    grad_tokens = (grad_resid + inverse_one * (scaled_one - normed_one * inner_one)).astype(jnp.bfloat16)

    sub = shard // ctx_count
    terms_gu = contract_rows(ffn_all, grad_gu).astype(jnp.bfloat16).reshape(fsdp_count, ctx_count, sub, 2 * hidden)
    terms_down = contract_rows(hidden_low, cot_all).astype(jnp.bfloat16).reshape(ctx_count, hidden // ctx_count, width)
    chunk_gu = ring_scatter(
        lambda k: lax.dynamic_index_in_dim(terms_gu, owners[k], 1, keepdims=False).reshape(
            fsdp_count * sub, 2 * hidden
        ),
        ring,
    ).astype(jnp.bfloat16)
    chunk_down = ring_scatter(lambda k: pick(terms_down, owners[k]), ring).astype(jnp.bfloat16)
    chunk_gu = chunk_gu.reshape(fsdp_count, sub, 2 * hidden)
    chunk_gu = side_exchange([pick(chunk_gu, side) for side in sides], fsdp_count)
    chunk_gu = stack_sides(chunk_gu).reshape(fsdp_count, sub, 2, hidden)
    chunk_gu = chunk_gu.transpose(1, 2, 0, 3).reshape(sub, 2 * fsdp_count * hidden)

    terms_out = contract_rows(attn_low, grad_branch).astype(jnp.bfloat16).reshape(ctx_count, own_width, width)
    ordered_out = jnp.zeros_like(terms_out)
    for k in range(ctx_count):
        ordered_out = lax.dynamic_update_slice_in_dim(ordered_out, terms_out[k : k + 1], owners[k], 0)
    ordered_out = ordered_out.reshape(fsdp_count, shard, width)
    part_out = side_scatter([pick(ordered_out, side) for side in sides], fsdp_count).astype(jnp.bfloat16)
    part_out = part_out.reshape(ctx_count, sub, width)
    chunk_out = ring_scatter(lambda k: pick(part_out, owners[k]), ring).astype(jnp.bfloat16)

    attn_all = jnp.concatenate(attn_slots, axis=0)
    terms_qkv = contract_rows(attn_all, jnp.concatenate(grad_qkv, axis=0)).astype(jnp.bfloat16)
    terms_qkv = terms_qkv.reshape(fsdp_count, shard, 3 * own_width)
    chunk_qkv = side_scatter([pick(terms_qkv, side) for side in sides], fsdp_count).astype(jnp.bfloat16)

    def gather_rows(chunk):
        slots = ring_gather(chunk, ring)
        whole = jnp.zeros((ctx_count,) + chunk.shape, jnp.float32)
        cut = chunk.shape[0] // 2
        for k in range(ctx_count):
            if k == half:
                for piece, start in zip(slots[k], (0, cut)):
                    whole = lax.dynamic_update_slice(
                        whole, (piece.astype(jnp.float32) * factor)[None], (owners[k], start, 0)
                    )
            else:
                whole = lax.dynamic_update_slice(
                    whole, (slots[k].astype(jnp.float32) * factor)[None], (owners[k], 0, 0)
                )
        return whole.reshape(-1, chunk.shape[1])

    grad_w_gate_up = gather_rows(chunk_gu)
    grad_w_down = gather_rows(chunk_down)
    grad_w_out = gather_rows(chunk_out)
    qkv_slots = ring_gather(chunk_qkv, ring)
    grad_w_qkv = jnp.zeros((shard, 3, ctx_count * own_width), jnp.float32)
    cut = shard // 2
    for k in range(ctx_count):
        pieces = zip(qkv_slots[k], (0, cut)) if k == half else ((qkv_slots[k], 0),)
        for piece, start in pieces:
            piece = (piece.astype(jnp.float32) * factor).reshape(-1, 3, own_width)
            grad_w_qkv = lax.dynamic_update_slice(grad_w_qkv, piece, (start, 0, owners[k] * own_width))
    grad_w_qkv = grad_w_qkv.reshape(shard, 3 * width)

    def gain_gradient(weight, grad_weight, gain):
        return jnp.sum(weight.astype(jnp.float32) * grad_weight, axis=1) / gain.astype(jnp.float32)

    return (
        output,
        grad_tokens,
        gain_gradient(w_qkv, grad_w_qkv, gain_attn),
        grad_w_qkv,
        grad_w_out,
        gain_gradient(w_gate_up, grad_w_gate_up, gain_ffn),
        grad_w_gate_up,
        grad_w_down,
    )


def solution(mesh):
    in_specs = (
        P(("fsdp", "ctx"), None),
        P(("fsdp", "ctx"), None),
        P("fsdp"),
        P("fsdp", None),
        P("fsdp", None),
        P("fsdp"),
        P("fsdp", None),
        P("fsdp", None),
        P("fsdp", None),
        P("fsdp", None),
    )
    out_specs = (
        P(("fsdp", "ctx"), None),
        P(("fsdp", "ctx"), None),
        P("fsdp"),
        P("fsdp", None),
        P("fsdp", None),
        P("fsdp"),
        P("fsdp", None),
        P("fsdp", None),
    )
    return jax.shard_map(body, mesh=mesh, in_specs=in_specs, out_specs=out_specs, check_vma=False)
```

time: 1100 us -> 629 us (0.57)
  waiting for transfers between devices: 758 us -> 140 us
  starting transfers between devices: 0.44 us -> 132 us
  local copies, waits for them, and re-layouts: 63.6 us -> 187 us
  matrix products: 169 us -> 46.7 us
  Pallas kernels: 0 us -> 39.9 us
  blocking collectives: 39.9 us -> 0 us
    reduce_scatter x5 -> x0, waiting for transfers between devices: 369 us -> none  [the longest x1 127 us: body(): lax.psum_scatter(grad_pair_terms.astype(jnp.bfloat16), 'ctx', scatter_dim...]
    all_gather x5 -> x0, waiting for transfers between devices: 205 us -> none  [the longest x1 117 us: body(): kv_all = lax.all_gather(key_value, 'ctx', axis=0, tiled=True)]
    psum x1 -> x0, waiting for transfers between devices: 182 us -> none  [body(): lax.psum(partial_shards[1].astype(jnp.bfloat16), 'ctx').astype(jnp.float32)]
    ppermute x0 -> x121, waiting for transfers between devices: none -> 140 us  [the longest x85 115 us: ring_shift(): lax.ppermute(value, 'ctx', [(ring[i], ring[(i + step) % count]) for i in...]
    ppermute x0 -> x121, starting transfers between devices: none -> 132 us  [the longest x85 109 us: ring_shift(): lax.ppermute(value, 'ctx', [(ring[i], ring[(i + step) % count]) for i in...]
    dot_general x31 -> x10, matrix products: 122 us -> 18.3 us  [the longest x8 11.1 us: project(): jnp.dot(value, weight_mine, preferred_element_type=jnp.float32)]
    dynamic_slice x26 -> x16, local copies, waits for them, and re-layouts: 6.04 us -> 55.6 us  [the longest x9 47.2 us: body(): lax.dynamic_index_in_dim(by_owner, owners[k], 2, keepdims=False)]
    unnamed x58 -> x175, local copies, waits for them, and re-layouts: 16.3 us -> 58.1 us
  transfers between devices with their start and end apart: 11 -> 121, of which waited for: 10 -> 43; matrix products, arithmetic and copies ran while one was open for 12% -> 46% of each run, Pallas kernels for 0% -> 6%
where the time goes in v1:
time: 629 us; the launch traced here: 621 us
  local copies, waits for them, and re-layouts  187 us (30%)
  waiting for transfers between devices  140 us (22%)
  starting transfers between devices  132 us (21%)
  other arithmetic  51.8 us (8%)
  matrix products  46.7 us (7%)
  Pallas kernels  39.9 us (6%)
  between operations  22.4 us (4%)
    ppermute x85, waiting for transfers between devices, ring_shift(): lax.ppermute(value, 'ctx', [(ring[i], ring[(i + step) % count]) for i in...  115 us
    ppermute x85, starting transfers between devices, ring_shift(): lax.ppermute(value, 'ctx', [(ring[i], ring[(i + step) % count]) for i in...  109 us
    unnamed x175, local copies, waits for them, and re-layouts  58.1 us
    dynamic_slice x9, local copies, waits for them, and re-layouts, body(): lax.dynamic_index_in_dim(by_owner, owners[k], 2, keepdims=False)  47.2 us
    dynamic_update_slice x19, local copies, waits for them, and re-layouts, stack_sides(): whole = lax.dynamic_update_slice_in_dim(whole, slot[None], side, 0)  25.3 us
    dynamic_update_slice x20, other arithmetic, gather_rows(): lax.dynamic_update_slice(whole, (slots[k].astype(jnp.float32) * factor)[N...  20.6 us
    pallas_call x1, Pallas kernels, attention_backward(): pl.pallas_call(functools.partial(bwd_kernel, meta), out_shape=[jax.ShapeD...  20.3 us
    pallas_call x1, Pallas kernels, attention_forward(): pl.pallas_call(functools.partial(fwd_kernel, meta), out_shape=[jax.ShapeD...  19.6 us
  transfers between devices with their start and end apart: 121, of which 43 were waited for; matrix products, arithmetic and copies ran while one was open for 46% of the time, Pallas kernels for 6%

profile of v1, /device:TPU:0, one launch (start us, length us, event | category | flops | bytes accessed | tf_op | source)
XLA Modules:
  0.0 620.9 jit_solution(15690855851071570693)
XLA Ops:
  35.2 4.5 copy.70
  39.7 3.2 constant_dynamic-slice_fusion.29
  44.9 3.5 broadcast_in_dim.200
  88.8 3.3 collective-permute-done.9
  102.1 11.7 %collective-permute-done.29 = bf16[256,1408]{0,1:T(8,128)(2,1)} collective-permute-done((bf16[256,1408]{0,1:T(8,128)(2,1)}, bf16[256,1408]{0,1:T(8,128)(2,1)}, u32[]{:S(2)}, u32[]{:S(2)}) %collective-permute-start.29) | collective-permute-done | bytes 720928 | tf_op jit(solution)/shard_map/ppermute | solution.py:313
  150.3 3.1 collective-permute-done.11
  158.1 3.1 collective-permute-done.12
  163.9 19.6 %attention_forward.1 = (bf16[256,128]{1,0:T(8,128)(2,1)}, bf16[256,128]{1,0:T(8,128)(2,1)}, bf16[256,128]{1,0:T(8,128)(2,1)}, bf16[256,128]{1,0:T(8,128)(2,1)}, ...) custom-call(s32[4]{0:T(128)} %bitcast.419, ...), custom_call_target="tpu_custom_call" | custom-call | flops 536870912 | bytes 2621440 | tf_op jit(solution)/shard_map/attention_forward/pallas_call | solution.py:182
  192.9 3.5 collective-permute-start.19
  203.8 3.6 collective-permute-start.25
  210.9 5.2 collective-permute-done.25
  221.0 5.4 fusion.33
  235.6 5.5 convolution_convert_fusion.2
  241.1 3.6 convolution_convert_fusion
  259.4 4.7 copy.99
  264.1 14.7 %constant_dynamic-slice_fusion.21 = (bf16[1024,3,1,128]{3,2,1,0:T(2,128)(2,1)}, bf16[1024,3,1,128]{3,2,1,0:T(2,128)(2,1)}, bf16[1024,3,1,128]{3,2,1,0:T(2,128)(2...) fusion(bf16[1024,3,8,128]{3,2,1,0:T(8,128)(2,1)S(1)} %bitcast.3, ...), kind=kLoop, calls=%fused_computation.275 | loop fusion | bytes 12582944 | tf_op jit(solution)/shard_map/jit(dynamic_index_in_dim)/dynamic_slice | solution.py:443
  278.9 3.5 copy.78
  283.3 4.6 copy.79
  287.9 4.7 copy.80
  292.6 4.7 copy.81
  297.2 3.5 copy.82
  306.8 4.7 copy.83
  311.5 3.5 copy.84
  319.9 3.5 copy.85
  336.9 4.8 collective-permute-done.111
  356.5 6.9 %collective-permute-done.92 = bf16[128,1408]{1,0:T(8,128)(2,1)S(1)} collective-permute-done((bf16[128,1408]{1,0:T(8,128)(2,1)S(1)}, bf16[128,1408]{1,0:T(8,128)(2,1)S(1)}, u32[]{:S(2)}, u32[]{:S(2)}) %collective-permute-start.92) | collective-permute-done | bytes 360480 | tf_op jit(solution)/shard_map/ppermute | solution.py:233
  364.8 4.2 collective-permute-done.113
  380.6 3.6 collective-permute-start.41
  386.8 3.2 collective-permute-start.44
  396.9 20.3 %attention_backward.1 = (bf16[256,384]{1,0:T(8,128)(2,1)}, bf16[256,384]{1,0:T(8,128)(2,1)}, bf16[256,384]{1,0:T(8,128)(2,1)}, bf16[256,384]{1,0:T(8,128)(2,1)},...) custom-call(s32[4]{0:T(128)} %bitcast.420, ...), custom_call_target="tpu_custom_call" | custom-call | flops 1342177280 | bytes 5242880 | tf_op jit(solution)/shard_map/attention_backward/pallas_call | solution.py:194
  423.0 4.6 convolution_convert_fusion.5
  435.6 4.5 collective-permute-done.46
  444.1 3.3 collective-permute-start.49
  447.4 13.6 %collective-permute-done.48 = bf16[256,384]{1,0:T(8,128)(2,1)S(1)} collective-permute-done((bf16[256,384]{1,0:T(8,128)(2,1)}, bf16[256,384]{1,0:T(8,128)(2,1)S(1)}, u32[]{:S(2)}, u32[]{:S(2)}) %collective-permute-start.48) | collective-permute-done | bytes 196640 | tf_op jit(solution)/shard_map/ppermute | solution.py:233
  462.4 7.1 %collective-permute-done.50 = bf16[256,384]{1,0:T(8,128)(2,1)S(1)} collective-permute-done((bf16[256,384]{1,0:T(8,128)(2,1)S(1)}, bf16[256,384]{1,0:T(8,128)(2,1)S(1)}, u32[]{:S(2)}, u32[]{:S(2)}) %collective-permute-start.50) | collective-permute-done | bytes 196640 | tf_op jit(solution)/shard_map/ppermute | solution.py:233
  469.4 10.0 %collective-permute-start.52 = (bf16[256,384]{1,0:T(8,128)(2,1)S(1)}, bf16[256,384]{1,0:T(8,128)(2,1)S(1)}, u32[]{:S(2)}, u32[]{:S(2)}) collective-permute-start(bf16[256,384]{1,0:T(8,128)(2,1)S(1)} %copy-done.42), channel_id=1, source_target_pairs={{4,12},{12,20},{20,28},{28,24},{24,16},{16,8},{8,0},{0,4},{5,13},{... | collective-permute-start | bytes 589832 | tf_op jit(solution)/shard_map/ppermute | solution.py:233
  482.2 4.0 collective-permute-done.52
  486.2 4.7 fusion.4
  494.3 4.8 collective-permute-done.115
  502.0 3.4 collective-permute-done.95
  510.0 3.2 broadcast_in_dim.217
  536.3 3.3 collective-permute-done.62
  544.5 2.9 collective-permute-done.60
  549.7 5.4 collective-permute-done.98
  565.1 4.2 collective-permute-done.70
  571.4 3.0 collective-permute-done.71
  604.4 3.5 collective-permute-done.83
  615.2 3.5 multiply_reduce_fusion
  (589 shorter events, 335.9 us)
Async XLA Ops:
  0.6 71.5 %collective-permute-start.21 = (bf16[256,1024]{1,0:T(8,128)(2,1)}, bf16[256,1024]{1,0:T(8,128)(2,1)}, u32[]{:S(2)}, u32[]{:S(2)}) collective-permute-start(bf16[256,1024]{1,0:T(8,128)(2,1)} %param.16), channel_id=1, source_target_pairs={{0,1},{1,0},{2,3},{3,2},{4,5},{5,4},{6,7},{7,6},{8,9},{9,8},{10,11... | collective-permute-start | bytes 1572872 | tf_op jit(solution)/shard_map/ppermute | solution.py:278
  1.2 74.7 %collective-permute-start.22 = (bf16[256,1024]{1,0:T(8,128)(2,1)}, bf16[256,1024]{1,0:T(8,128)(2,1)}, u32[]{:S(2)}, u32[]{:S(2)}) collective-permute-start(bf16[256,1024]{1,0:T(8,128)(2,1)} %param.16), channel_id=1, source_target_pairs={{0,2},{1,3},{2,0},{3,1},{4,6},{5,7},{6,4},{7,5},{8,10},{9,11},{10,... | collective-permute-start | bytes 1572872 | tf_op jit(solution)/shard_map/ppermute | solution.py:282
  5.1 53.1 %collective-permute-start = (bf16[2,256]{1,0:T(2,128)(2,1)S(1)}, bf16[2,256]{1,0:T(2,128)(2,1)S(1)}, u32[]{:S(2)}, u32[]{:S(2)}) collective-permute-start(bf16[2,256]{1,0:T(2,128)(2,1)S(1)} %get-tuple-element.77), channel_id=1, source_target_pairs={{0,1},{1,0},{2,3},{3,2},{4,5},{5,4},{6,7},{7,6},{8,9},{9,8},{10,11... | collective-permute-start | bytes 3080 | tf_op jit(solution)/shard_map/ppermute | solution.py:278
  5.3 54.7 %collective-permute-start.1 = (bf16[2,256]{1,0:T(2,128)(2,1)S(1)}, bf16[2,256]{1,0:T(2,128)(2,1)S(1)}, u32[]{:S(2)}, u32[]{:S(2)}) collective-permute-start(bf16[2,256]{1,0:T(2,128)(2,1)S(1)} %get-tuple-element.77), channel_id=1, source_target_pairs={{0,2},{1,3},{2,0},{3,1},{4,6},{5,7},{6,4},{7,5},{8,10},{9,11},{10,... | collective-permute-start | bytes 3080 | tf_op jit(solution)/shard_map/ppermute | solution.py:282
  15.0 47.5 %collective-permute-start.3 = (bf16[256,384]{0,1:T(8,128)(2,1)S(1)}, bf16[256,384]{0,1:T(8,128)(2,1)}, u32[]{:S(2)}, u32[]{:S(2)}) collective-permute-start(bf16[256,384]{0,1:T(8,128)(2,1)S(1)} %bitcast.402), channel_id=1, source_target_pairs={{0,1},{1,0},{2,3},{3,2},{4,5},{5,4},{6,7},{7,6},{8,9},{9,8},{10,11... | collective-permute-start | bytes 589832 | tf_op jit(solution)/shard_map/ppermute | solution.py:278
  61.1 18.6 %collective-permute-start.34 = (bf16[256,1024]{1,0:T(8,128)(2,1)S(1)}, bf16[256,1024]{1,0:T(8,128)(2,1)}, u32[]{:S(2)}, u32[]{:S(2)}) collective-permute-start(bf16[256,1024]{1,0:T(8,128)(2,1)S(1)} %copy-done.18), channel_id=1, source_target_pairs={{0,2},{1,3},{2,0},{3,1},{4,6},{5,7},{6,4},{7,5},{8,10},{9,11},{10,... | collective-permute-start | bytes 1572872 | tf_op jit(solution)/shard_map/ppermute | solution.py:282
  62.6 15.1 %collective-permute-start.33 = (bf16[256,1024]{1,0:T(8,128)(2,1)S(1)}, bf16[256,1024]{1,0:T(8,128)(2,1)}, u32[]{:S(2)}, u32[]{:S(2)}) collective-permute-start(bf16[256,1024]{1,0:T(8,128)(2,1)S(1)} %copy-done.18), channel_id=1, source_target_pairs={{0,1},{1,0},{2,3},{3,2},{4,5},{5,4},{6,7},{7,6},{8,9},{9,8},{10,11... | collective-permute-start | bytes 1572872 | tf_op jit(solution)/shard_map/ppermute | solution.py:278
  68.1 79.5 %collective-permute-start.53 = (bf16[256,3072]{1,0:T(8,128)(2,1)}, bf16[256,3072]{1,0:T(8,128)(2,1)}, u32[]{:S(2)}, u32[]{:S(2)}) collective-permute-start(bf16[256,3072]{1,0:T(8,128)(2,1)} %param.15), channel_id=1, source_target_pairs={{0,1},{1,0},{2,3},{3,2},{4,5},{5,4},{6,7},{7,6},{8,9},{9,8},{10,11... | collective-permute-start | bytes 4718600 | tf_op jit(solution)/shard_map/ppermute | solution.py:278
  75.8 18.8 %collective-permute-start.27 = (bf16[256,1408]{0,1:T(8,128)(2,1)S(1)}, bf16[256,1408]{0,1:T(8,128)(2,1)S(1)}, u32[]{:S(2)}, u32[]{:S(2)}) collective-permute-start(bf16[256,1408]{0,1:T(8,128)(2,1)S(1)} %bitcast.408), channel_id=1, source_target_pairs={{0,1},{1,0},{2,3},{3,2},{4,5},{5,4},{6,7},{7,6},{8,9},{9,8},{10,11... | collective-permute-start | bytes 2162696 | tf_op jit(solution)/shard_map/ppermute | solution.py:313
  79.8 20.1 %collective-permute-start.28 = (bf16[256,1408]{0,1:T(8,128)(2,1)}, bf16[256,1408]{0,1:T(8,128)(2,1)}, u32[]{:S(2)}, u32[]{:S(2)}) collective-permute-start(bf16[256,1408]{0,1:T(8,128)(2,1)} %bitcast.44), channel_id=1, source_target_pairs={{0,2},{1,3},{2,0},{3,1},{4,6},{5,7},{6,4},{7,5},{8,10},{9,11},{10,... | collective-permute-start | bytes 2162696 | tf_op jit(solution)/shard_map/ppermute | solution.py:313
  86.2 27.6 %collective-permute-start.29 = (bf16[256,1408]{0,1:T(8,128)(2,1)}, bf16[256,1408]{0,1:T(8,128)(2,1)}, u32[]{:S(2)}, u32[]{:S(2)}) collective-permute-start(bf16[256,1408]{0,1:T(8,128)(2,1)} %bitcast.46), channel_id=1, source_target_pairs={{0,3},{1,2},{2,1},{3,0},{4,7},{5,6},{6,5},{7,4},{8,11},{9,10},{10,... | collective-permute-start | bytes 2162696 | tf_op jit(solution)/shard_map/ppermute | solution.py:313
  92.0 55.6 %collective-permute-start.54 = (bf16[256,3072]{1,0:T(8,128)(2,1)}, bf16[256,3072]{1,0:T(8,128)(2,1)}, u32[]{:S(2)}, u32[]{:S(2)}) collective-permute-start(bf16[256,3072]{1,0:T(8,128)(2,1)} %param.15), channel_id=1, source_target_pairs={{0,2},{1,3},{2,0},{3,1},{4,6},{5,7},{6,4},{7,5},{8,10},{9,11},{10,... | collective-permute-start | bytes 4718600 | tf_op jit(solution)/shard_map/ppermute | solution.py:282
  94.7 27.0 %collective-permute-start.23 = (bf16[256,1024]{1,0:T(8,128)(2,1)}, bf16[256,1024]{1,0:T(8,128)(2,1)}, u32[]{:S(2)}, u32[]{:S(2)}) collective-permute-start(bf16[256,1024]{1,0:T(8,128)(2,1)} %collective-permute-done.22), channel_id=1, source_target_pairs={{0,1},{1,0},{2,3},{3,2},{4,5},{5,4},{6,7},{7,6},{8,9},{9,8},{10,11... | collective-permute-start | bytes 1572872 | tf_op jit(solution)/shard_map/ppermute | solution.py:278
  99.8 37.6 %collective-permute-start.35 = (bf16[256,1024]{1,0:T(8,128)(2,1)}, bf16[256,1024]{1,0:T(8,128)(2,1)}, u32[]{:S(2)}, u32[]{:S(2)}) collective-permute-start(bf16[256,1024]{1,0:T(8,128)(2,1)} %collective-permute-done.34), channel_id=1, source_target_pairs={{0,1},{1,0},{2,3},{3,2},{4,5},{5,4},{6,7},{7,6},{8,9},{9,8},{10,11... | collective-permute-start | bytes 1572872 | tf_op jit(solution)/shard_map/ppermute | solution.py:278
  113.8 25.5 %collective-permute-start.10 = (bf16[256,1024]{1,0:T(8,128)(2,1)S(1)}, bf16[256,1024]{1,0:T(8,128)(2,1)}, u32[]{:S(2)}, u32[]{:S(2)}) collective-permute-start(bf16[256,1024]{1,0:T(8,128)(2,1)S(1)} %copy-done.21), channel_id=1, source_target_pairs={{4,12},{12,20},{20,28},{28,24},{24,16},{16,8},{8,0},{0,4},{5,13},{... | collective-permute-start | bytes 1572872 | tf_op jit(solution)/shard_map/ppermute | solution.py:233
  121.6 19.2 %collective-permute-start.7 = (bf16[256,1024]{1,0:T(8,128)(2,1)S(1)}, bf16[256,1024]{1,0:T(8,128)(2,1)S(1)}, u32[]{:S(2)}, u32[]{:S(2)}) collective-permute-start(bf16[256,1024]{1,0:T(8,128)(2,1)S(1)} %copy-done.24), channel_id=1, source_target_pairs={{4,0},{12,4},{20,12},{28,20},{24,28},{16,24},{8,16},{0,8},{5,1},{1... | collective-permute-start | bytes 1572872 | tf_op jit(solution)/shard_map/ppermute | solution.py:233
  147.6 108.5 %collective-permute-start.55 = (bf16[256,3072]{1,0:T(8,128)(2,1)}, bf16[256,3072]{1,0:T(8,128)(2,1)}, u32[]{:S(2)}, u32[]{:S(2)}) collective-permute-start(bf16[256,3072]{1,0:T(8,128)(2,1)} %collective-permute-done.54), channel_id=1, source_target_pairs={{0,1},{1,0},{2,3},{3,2},{4,5},{5,4},{6,7},{7,6},{8,9},{9,8},{10,11... | collective-permute-start | bytes 4718600 | tf_op jit(solution)/shard_map/ppermute | solution.py:278
  232.7 17.5 %collective-permute-start.105 = (bf16[44,1024]{1,0:T(8,128)(2,1)S(1)}, bf16[44,1024]{1,0:T(8,128)(2,1)S(1)}, u32[]{:S(2)}, u32[]{:S(2)}) collective-permute-start(bf16[44,1024]{1,0:T(8,128)(2,1)S(1)} %get-tuple-element.114), channel_id=1, source_target_pairs={{4,12},{12,20},{20,28},{28,24},{24,16},{16,8},{8,0},{0,4},{5,13},{... | collective-permute-start | bytes 270344 | tf_op jit(solution)/shard_map/ppermute | solution.py:233
  232.8 17.4 %collective-permute-start.109 = (bf16[44,1024]{1,0:T(8,128)(2,1)S(1)}, bf16[44,1024]{1,0:T(8,128)(2,1)S(1)}, u32[]{:S(2)}, u32[]{:S(2)}) collective-permute-start(bf16[44,1024]{1,0:T(8,128)(2,1)S(1)} %get-tuple-element.116), channel_id=1, source_target_pairs={{4,0},{12,4},{20,12},{28,20},{24,28},{16,24},{8,16},{0,8},{5,1},{1... | collective-permute-start | bytes 270344 | tf_op jit(solution)/shard_map/ppermute | solution.py:233
  250.3 77.2 %collective-permute-start.30 = (bf16[256,1024]{1,0:T(8,128)(2,1)}, bf16[256,1024]{1,0:T(8,128)(2,1)}, u32[]{:S(2)}, u32[]{:S(2)}) collective-permute-start(bf16[256,1024]{1,0:T(8,128)(2,1)} %get-tuple-element.108), channel_id=1, source_target_pairs={{0,1},{1,0},{2,3},{3,2},{4,5},{5,4},{6,7},{7,6},{8,9},{9,8},{10,11... | collective-permute-start | bytes 1572872 | tf_op jit(solution)/shard_map/ppermute | solution.py:278
  250.3 80.2 %collective-permute-start.36 = (bf16[256,1024]{1,0:T(8,128)(2,1)}, bf16[256,1024]{1,0:T(8,128)(2,1)}, u32[]{:S(2)}, u32[]{:S(2)}) collective-permute-start(bf16[256,1024]{1,0:T(8,128)(2,1)} %get-tuple-element.106), channel_id=1, source_target_pairs={{0,1},{1,0},{2,3},{3,2},{4,5},{5,4},{6,7},{7,6},{8,9},{9,8},{10,11... | collective-permute-start | bytes 1572872 | tf_op jit(solution)/shard_map/ppermute | solution.py:278
  252.8 119.2 %collective-permute-start.38 = (bf16[256,1024]{1,0:T(8,128)(2,1)}, bf16[256,1024]{1,0:T(8,128)(2,1)S(1)}, u32[]{:S(2)}, u32[]{:S(2)}) collective-permute-start(bf16[256,1024]{1,0:T(8,128)(2,1)} %get-tuple-element.107), channel_id=1, source_target_pairs={{0,1},{1,0},{2,3},{3,2},{4,5},{5,4},{6,7},{7,6},{8,9},{9,8},{10,11... | collective-permute-start | bytes 1572872 | tf_op jit(solution)/shard_map/ppermute | solution.py:278
  253.7 70.8 %collective-permute-start.110 = (bf16[88,1024]{1,0:T(8,128)(2,1)}, bf16[88,1024]{1,0:T(8,128)(2,1)}, u32[]{:S(2)}, u32[]{:S(2)}) collective-permute-start(bf16[88,1024]{1,0:T(8,128)(2,1)} %pad_maximum_fusion.9), channel_id=1, source_target_pairs={{4,0},{12,4},{20,12},{28,20},{24,28},{16,24},{8,16},{0,8},{5,1},{1... | collective-permute-start | bytes 540680 | tf_op jit(solution)/shard_map/ppermute | solution.py:233
  256.1 60.9 %collective-permute-start.106 = (bf16[88,1024]{1,0:T(8,128)(2,1)}, bf16[88,1024]{1,0:T(8,128)(2,1)S(1)}, u32[]{:S(2)}, u32[]{:S(2)}) collective-permute-start(bf16[88,1024]{1,0:T(8,128)(2,1)} %pad_maximum_fusion.8), channel_id=1, source_target_pairs={{4,12},{12,20},{20,28},{28,24},{24,16},{16,8},{8,0},{0,4},{5,13},{... | collective-permute-start | bytes 540680 | tf_op jit(solution)/shard_map/ppermute | solution.py:233
  324.4 48.0 %collective-permute-start.32 = (bf16[256,1024]{1,0:T(8,128)(2,1)}, bf16[256,1024]{1,0:T(8,128)(2,1)S(1)}, u32[]{:S(2)}, u32[]{:S(2)}) collective-permute-start(bf16[256,1024]{1,0:T(8,128)(2,1)} %get-tuple-element.109), channel_id=1, source_target_pairs={{0,1},{1,0},{2,3},{3,2},{4,5},{5,4},{6,7},{7,6},{8,9},{9,8},{10,11... | collective-permute-start | bytes 1572872 | tf_op jit(solution)/shard_map/ppermute | solution.py:278
  327.5 16.4 %collective-permute-start.91 = (bf16[128,1408]{1,0:T(8,128)(2,1)}, bf16[128,1408]{1,0:T(8,128)(2,1)S(1)}, u32[]{:S(2)}, u32[]{:S(2)}) collective-permute-start(bf16[128,1408]{1,0:T(8,128)(2,1)} %pad_maximum_fusion.5), channel_id=1, source_target_pairs={{4,0},{12,4},{20,12},{28,20},{24,28},{16,24},{8,16},{0,8},{5,1},{1... | collective-permute-start | bytes 1081352 | tf_op jit(solution)/shard_map/ppermute | solution.py:233
  345.0 27.4 %collective-permute-start.31 = (bf16[256,1024]{1,0:T(8,128)(2,1)S(1)}, bf16[256,1024]{1,0:T(8,128)(2,1)S(1)}, u32[]{:S(2)}, u32[]{:S(2)}) collective-permute-start(bf16[256,1024]{1,0:T(8,128)(2,1)S(1)} %add_convert_fusion.2), channel_id=1, source_target_pairs={{0,2},{1,3},{2,0},{3,1},{4,6},{5,7},{6,4},{7,5},{8,10},{9,11},{10,... | collective-permute-start | bytes 1572872 | tf_op jit(solution)/shard_map/ppermute | solution.py:282
  349.5 22.5 %collective-permute-start.37 = (bf16[256,1024]{1,0:T(8,128)(2,1)S(1)}, bf16[256,1024]{1,0:T(8,128)(2,1)S(1)}, u32[]{:S(2)}, u32[]{:S(2)}) collective-permute-start(bf16[256,1024]{1,0:T(8,128)(2,1)S(1)} %add_convert_fusion), channel_id=1, source_target_pairs={{0,2},{1,3},{2,0},{3,1},{4,6},{5,7},{6,4},{7,5},{8,10},{9,11},{10,... | collective-permute-start | bytes 1572872 | tf_op jit(solution)/shard_map/ppermute | solution.py:282
  369.0 15.5 %collective-permute-start.116 = (bf16[88,1024]{1,0:T(8,128)(2,1)S(1)}, bf16[88,1024]{1,0:T(8,128)(2,1)}, u32[]{:S(2)}, u32[]{:S(2)}) collective-permute-start(bf16[88,1024]{1,0:T(8,128)(2,1)S(1)} %get-tuple-element.69), channel_id=1, source_target_pairs={{4,12},{12,20},{20,28},{28,24},{24,16},{16,8},{8,0},{0,4},{5,13},{... | collective-permute-start | bytes 540680 | tf_op jit(solution)/shard_map/ppermute | solution.py:233
  391.1 40.5 %collective-permute-start.89 = (bf16[128,1408]{1,0:T(8,128)(2,1)}, bf16[128,1408]{1,0:T(8,128)(2,1)}, u32[]{:S(2)}, u32[]{:S(2)}) collective-permute-start(bf16[128,1408]{1,0:T(8,128)(2,1)} %fusion.16), channel_id=1, source_target_pairs={{4,12},{12,20},{20,28},{28,24},{24,16},{16,8},{8,0},{0,4},{5,13},{... | collective-permute-start | bytes 1081352 | tf_op jit(solution)/shard_map/ppermute | solution.py:233
  391.7 40.7 %collective-permute-start.93 = (bf16[128,1408]{1,0:T(8,128)(2,1)}, bf16[128,1408]{1,0:T(8,128)(2,1)}, u32[]{:S(2)}, u32[]{:S(2)}) collective-permute-start(bf16[128,1408]{1,0:T(8,128)(2,1)} %fusion.14), channel_id=1, source_target_pairs={{4,0},{12,4},{20,12},{28,20},{24,28},{16,24},{8,16},{0,8},{5,1},{1... | collective-permute-start | bytes 1081352 | tf_op jit(solution)/shard_map/ppermute | solution.py:233
  393.2 36.5 %collective-permute-start.114 = (bf16[88,1024]{1,0:T(8,128)(2,1)}, bf16[88,1024]{1,0:T(8,128)(2,1)}, u32[]{:S(2)}, u32[]{:S(2)}) collective-permute-start(bf16[88,1024]{1,0:T(8,128)(2,1)} %collective-permute-done.113), channel_id=1, source_target_pairs={{4,0},{12,4},{20,12},{28,20},{24,28},{16,24},{8,16},{0,8},{5,1},{1... | collective-permute-start | bytes 540680 | tf_op jit(solution)/shard_map/ppermute | solution.py:233
  395.1 96.9 %collective-permute-start.117 = (bf16[88,1024]{1,0:T(8,128)(2,1)}, bf16[88,1024]{1,0:T(8,128)(2,1)}, u32[]{:S(2)}, u32[]{:S(2)}) collective-permute-start(bf16[88,1024]{1,0:T(8,128)(2,1)} %collective-permute-done.116), channel_id=1, source_target_pairs={{4,12},{12,20},{20,28},{28,24},{24,16},{16,8},{8,0},{0,4},{5,13},{... | collective-permute-start | bytes 540680 | tf_op jit(solution)/shard_map/ppermute | solution.py:233
  396.3 134.1 %collective-permute-start.67 = (bf16[256,1024]{1,0:T(8,128)(2,1)}, bf16[256,1024]{1,0:T(8,128)(2,1)}, u32[]{:S(2)}, u32[]{:S(2)}) collective-permute-start(bf16[256,1024]{1,0:T(8,128)(2,1)} %get-tuple-element.104), channel_id=1, source_target_pairs={{0,1},{1,0},{2,3},{3,2},{4,5},{5,4},{6,7},{7,6},{8,9},{9,8},{10,11... | collective-permute-start | bytes 1572872 | tf_op jit(solution)/shard_map/ppermute | solution.py:278
  429.7 127.6 %collective-permute-start.69 = (bf16[256,1024]{1,0:T(8,128)(2,1)}, bf16[256,1024]{1,0:T(8,128)(2,1)}, u32[]{:S(2)}, u32[]{:S(2)}) collective-permute-start(bf16[256,1024]{1,0:T(8,128)(2,1)} %get-tuple-element.105), channel_id=1, source_target_pairs={{0,1},{1,0},{2,3},{3,2},{4,5},{5,4},{6,7},{7,6},{8,9},{9,8},{10,11... | collective-permute-start | bytes 1572872 | tf_op jit(solution)/shard_map/ppermute | solution.py:278
  440.1 20.9 %collective-permute-start.48 = (bf16[256,384]{1,0:T(8,128)(2,1)}, bf16[256,384]{1,0:T(8,128)(2,1)S(1)}, u32[]{:S(2)}, u32[]{:S(2)}) collective-permute-start(bf16[256,384]{1,0:T(8,128)(2,1)} %get-tuple-element.39), channel_id=1, source_target_pairs={{4,16},{12,8},{20,0},{28,4},{24,12},{16,20},{8,28},{0,24},{5,17},{... | collective-permute-start | bytes 589832 | tf_op jit(solution)/shard_map/ppermute | solution.py:233
  444.1 17.0 %collective-permute-start.49 = (bf16[256,384]{1,0:T(8,128)(2,1)}, bf16[256,384]{1,0:T(8,128)(2,1)S(1)}, u32[]{:S(2)}, u32[]{:S(2)}) collective-permute-start(bf16[256,384]{1,0:T(8,128)(2,1)} %get-tuple-element.40), channel_id=1, source_target_pairs={{4,24},{12,16},{20,8},{28,0},{24,4},{16,12},{8,20},{0,28},{5,25},{... | collective-permute-start | bytes 589832 | tf_op jit(solution)/shard_map/ppermute | solution.py:233
  461.1 21.1 %collective-permute-start.51 = (bf16[256,384]{1,0:T(8,128)(2,1)S(1)}, bf16[256,384]{1,0:T(8,128)(2,1)S(1)}, u32[]{:S(2)}, u32[]{:S(2)}) collective-permute-start(bf16[256,384]{1,0:T(8,128)(2,1)S(1)} %copy-done.43), channel_id=1, source_target_pairs={{4,20},{12,28},{20,24},{28,16},{24,8},{16,0},{8,4},{0,12},{5,21},{... | collective-permute-start | bytes 589832 | tf_op jit(solution)/shard_map/ppermute | solution.py:233
  469.4 16.8 %collective-permute-start.52 = (bf16[256,384]{1,0:T(8,128)(2,1)S(1)}, bf16[256,384]{1,0:T(8,128)(2,1)S(1)}, u32[]{:S(2)}, u32[]{:S(2)}) collective-permute-start(bf16[256,384]{1,0:T(8,128)(2,1)S(1)} %copy-done.42), channel_id=1, source_target_pairs={{4,12},{12,20},{20,28},{28,24},{24,16},{16,8},{8,0},{0,4},{5,13},{... | collective-permute-start | bytes 589832 | tf_op jit(solution)/shard_map/ppermute | solution.py:233
  486.2 40.8 %collective-permute-start.58 = (bf16[256,384]{0,1:T(8,128)(2,1)}, bf16[256,384]{0,1:T(8,128)(2,1)}, u32[]{:S(2)}, u32[]{:S(2)}) collective-permute-start(bf16[256,384]{0,1:T(8,128)(2,1)} %bitcast.65), channel_id=1, source_target_pairs={{0,1},{1,0},{2,3},{3,2},{4,5},{5,4},{6,7},{7,6},{8,9},{9,8},{10,11... | collective-permute-start | bytes 589832 | tf_op jit(solution)/shard_map/ppermute | solution.py:278
  505.4 22.7 %collective-permute-start.57 = (bf16[256,384]{0,1:T(8,128)(2,1)S(1)}, bf16[256,384]{0,1:T(8,128)(2,1)S(1)}, u32[]{:S(2)}, u32[]{:S(2)}) collective-permute-start(bf16[256,384]{0,1:T(8,128)(2,1)S(1)} %fusion.24), channel_id=1, source_target_pairs={{0,2},{1,3},{2,0},{3,1},{4,6},{5,7},{6,4},{7,5},{8,10},{9,11},{10,... | collective-permute-start | bytes 589832 | tf_op jit(solution)/shard_map/ppermute | solution.py:282
  520.2 20.3 %collective-permute-start.97 = (bf16[32,5632]{1,0:T(8,128)(2,1)}, bf16[32,5632]{1,0:T(8,128)(2,1)}, u32[]{:S(2)}, u32[]{:S(2)}) collective-permute-start(bf16[32,5632]{1,0:T(8,128)(2,1)} %reshape.430), channel_id=1, source_target_pairs={{4,0},{12,4},{20,12},{28,20},{24,28},{16,24},{8,16},{0,8},{5,1},{1... | collective-permute-start | bytes 1081352 | tf_op jit(solution)/shard_map/ppermute | solution.py:233
  527.0 16.7 %collective-permute-start.100 = (bf16[32,5632]{1,0:T(8,128)(2,1)}, bf16[32,5632]{1,0:T(8,128)(2,1)S(1)}, u32[]{:S(2)}, u32[]{:S(2)}) collective-permute-start(bf16[32,5632]{1,0:T(8,128)(2,1)} %reshape.430), channel_id=1, source_target_pairs={{4,12},{12,20},{20,28},{28,24},{24,16},{16,8},{8,0},{0,4},{5,13},{... | collective-permute-start | bytes 1081352 | tf_op jit(solution)/shard_map/ppermute | solution.py:233
  534.8 24.5 %collective-permute-start.68 = (bf16[256,1024]{1,0:T(8,128)(2,1)S(1)}, bf16[256,1024]{1,0:T(8,128)(2,1)S(1)}, u32[]{:S(2)}, u32[]{:S(2)}) collective-permute-start(bf16[256,1024]{1,0:T(8,128)(2,1)S(1)} %fusion.12), channel_id=1, source_target_pairs={{0,2},{1,3},{2,0},{3,1},{4,6},{5,7},{6,4},{7,5},{8,10},{9,11},{10,... | collective-permute-start | bytes 1572872 | tf_op jit(solution)/shard_map/ppermute | solution.py:282
  548.4 15.2 %collective-permute-start.61 = (bf16[256,384]{0,1:T(8,128)(2,1)S(1)}, bf16[256,384]{0,1:T(8,128)(2,1)S(1)}, u32[]{:S(2)}, u32[]{:S(2)}) collective-permute-start(bf16[256,384]{0,1:T(8,128)(2,1)S(1)} %collective-permute-done.60), channel_id=1, source_target_pairs={{4,0},{12,4},{20,12},{28,20},{24,28},{16,24},{8,16},{0,8},{5,1},{1... | collective-permute-start | bytes 589832 | tf_op jit(solution)/shard_map/ppermute | solution.py:233
  557.3 37.7 %collective-permute-start.99 = (bf16[32,5632]{1,0:T(8,128)(2,1)}, bf16[32,5632]{1,0:T(8,128)(2,1)}, u32[]{:S(2)}, u32[]{:S(2)}) collective-permute-start(bf16[32,5632]{1,0:T(8,128)(2,1)} %collective-permute-done.98), channel_id=1, source_target_pairs={{4,0},{12,4},{20,12},{28,20},{24,28},{16,24},{8,16},{0,8},{5,1},{1... | collective-permute-start | bytes 1081352 | tf_op jit(solution)/shard_map/ppermute | solution.py:233
  559.0 34.1 %collective-permute-start.102 = (bf16[32,5632]{1,0:T(8,128)(2,1)}, bf16[32,5632]{1,0:T(8,128)(2,1)S(1)}, u32[]{:S(2)}, u32[]{:S(2)}) collective-permute-start(bf16[32,5632]{1,0:T(8,128)(2,1)} %collective-permute-done.101), channel_id=1, source_target_pairs={{4,12},{12,20},{20,28},{28,24},{24,16},{16,8},{8,0},{0,4},{5,13},{... | collective-permute-start | bytes 1081352 | tf_op jit(solution)/shard_map/ppermute | solution.py:233
  593.1 16.9 %collective-permute-start.103 = (bf16[16,5632]{1,0:T(8,128)(2,1)S(1)}, bf16[16,5632]{1,0:T(8,128)(2,1)S(1)}, u32[]{:S(2)}, u32[]{:S(2)}) collective-permute-start(bf16[16,5632]{1,0:T(8,128)(2,1)S(1)} %slice.390), channel_id=1, source_target_pairs={{4,12},{12,20},{20,28},{28,24},{24,16},{16,8},{8,0},{0,4},{5,13},{... | collective-permute-start | bytes 540680 | tf_op jit(solution)/shard_map/ppermute | solution.py:233
  (135 other events, 1390.8 us)

commit v2 on v1

v2 whole, which is shorter than its diff:
```python
import functools
import math

import jax
import jax.numpy as jnp
from jax import lax
from jax.experimental import pallas as pl
from jax.experimental.pallas import tpu as pltpu
from jax.sharding import PartitionSpec as P

HEADS = 16
TILE = 256


EPS = 1e-05
MASKED=-1e30
def nt(a,b): return lax.dot_general(a,b,(((1,),(1,)),((),())),preferred_element_type=jnp.float32)
def nn(a,b): return lax.dot_general(a,b,(((1,),(0,)),((),())),preferred_element_type=jnp.float32)

def ends_of(lengths_ref):
    ends = [lengths_ref[0, 0]]
    for i in range(1, lengths_ref.shape[1]):
        ends.append(ends[-1] + lengths_ref[0, i])
    return ends

def first_tile(ends, position, tile):
    start = jnp.int32(0)
    for end in ends[:-1]:
        start = jnp.where(end <= position, end, start)
    return start // tile

def last_tile(ends, position, tile):
    last = ends[-1]
    for end in reversed(ends[:-1]):
        last = jnp.where(end > position, end, last)
    return (last - 1) // tile

def seen(ends, query_start, key_start, tile):
    pos_query = query_start + lax.broadcasted_iota(jnp.int32, (1, tile), 1)
    start = jnp.zeros((1, tile), jnp.int32)
    for end in ends[:-1]:
        start = jnp.where(pos_query >= end, end, start)
    pos_key = key_start + lax.broadcasted_iota(jnp.int32, (tile, tile), 0)
    return (pos_key <= pos_query) & (pos_key >= start)

def head_lanes(x, head, heads, depth):
    if heads == 1:
        return x
    lane = lax.broadcasted_iota(jnp.int32, x.shape, 1)
    return jnp.where((lane >= head * depth) & (lane < (head + 1) * depth), x, jnp.zeros_like(x))

def placed(slots, block, table, order_ref, per):
    number = 0
    for slot in slots:
        for row in range(0, slot.shape[0], block):
            position = order_ref[0, table[0, number // per] * per + number % per] * block
            yield slot, pl.ds(row, block), pl.ds(pl.multiple_of(position, block), block)
            number += 1

def fwd_kernel(meta, table, lengths_ref, order_ref, *refs):
    given, n, heads, depth, tile, block = meta
    qkv_refs, out_refs = refs[:given], refs[given:given+n]
    out_t_ref, lse_ref = refs[given+n], refs[given+n+1]
    q_ref, k_ref, v_ref, o_ref = refs[given+n+2:]
    ends = ends_of(lengths_ref)
    width = heads*depth
    scale = depth ** (-0.5)
    per = out_refs[0].shape[0] // block
    for slot, src, dst in placed(qkv_refs, block, table, order_ref, per):
        q = slot[src, 0:width].astype(jnp.float32)*scale
        for h in range(heads):
            q_ref[h, dst, :] = head_lanes(q, h, heads, depth).astype(jnp.bfloat16)
        k_ref[dst, :] = slot[src, width:2*width]
        v_ref[dst, :] = slot[src, 2*width:]
    tiles = q_ref.shape[1] // tile
    def one_query(t, _):
        rows = pl.ds(pl.multiple_of(t*tile, tile), tile)
        qs = [q_ref[h, rows, :] for h in range(heads)]
        def one_key(j, carry):
            keys = pl.ds(pl.multiple_of(j*tile, tile), tile)
            k = k_ref[keys, :]
            v_t = jnp.transpose(v_ref[keys, :].astype(jnp.float32)).astype(jnp.bfloat16)
            mask = seen(ends, t*tile, j*tile, tile)
            new = []
            for h in range(heads):
                m, l, acc = carry[h]
                s = jnp.where(mask, nt(k, qs[h]), MASKED)
                m_new = jnp.maximum(m, jnp.max(s, axis=0, keepdims=True))
                e = jnp.exp(s - m_new)
                alpha = jnp.exp(m - m_new)
                l = l*alpha + jnp.sum(e, axis=0, keepdims=True)
                acc = acc*alpha + nn(v_t[h*depth:(h+1)*depth], e.astype(jnp.bfloat16))
                new.append((m_new, l, acc))
            return tuple(new)
        init = tuple((jnp.full((1,tile),MASKED,jnp.float32), jnp.zeros((1,tile),jnp.float32), jnp.zeros((depth,tile),jnp.float32)) for _ in range(heads))
        final = lax.fori_loop(first_tile(ends, t*tile, tile), t+1, one_key, init)
        outs = []
        for h in range(heads):
            m, l, acc = final[h]
            outs.append(acc / l)
            lse_ref[h:h+1, rows] = m + jnp.log(l)
        out_t = jnp.concatenate(outs, axis=0) if heads > 1 else outs[0]
        out_t_ref[:, rows] = out_t
        o_ref[rows, :] = jnp.transpose(out_t).astype(jnp.bfloat16)
        return 0
    lax.fori_loop(0, tiles, one_query, 0)
    for slot, dst, src in placed(out_refs, block, table, order_ref, per):
        slot[dst, :] = o_ref[src, :]

def bwd_kernel(meta, table, lengths_ref, order_ref, *refs):
    given, n, heads, depth, tile, block = meta
    qkv_refs, grad_refs = refs[:given], refs[given:given+n]
    part_out_ref = refs[given+n]
    refs = refs[given-n:]
    out_t_ref, lse_ref = refs[2*n+1], refs[2*n+2]
    dqkv_refs = refs[2*n+3:3*n+3]
    ends = ends_of(lengths_ref)
    q_ref, k_ref, v_ref, g_ref, k_t_ref, delta_ref, dq_t_ref, dq_ref, dk_ref, dv_ref = refs[3*n+3:]
    width = heads*depth
    scale = depth ** (-0.5)
    per = dqkv_refs[0].shape[0] // block
    total = k_ref.shape[0]
    for slot, src, dst in placed(qkv_refs, block, table, order_ref, per):
        q = slot[src, 0:width].astype(jnp.float32)*scale
        for h in range(heads):
            q_ref[h, dst, :] = head_lanes(q, h, heads, depth).astype(jnp.bfloat16)
        k_ref[dst, :] = slot[src, width:2*width]
        v_ref[dst, :] = slot[src, 2*width:]
    for slot, src, dst in placed(grad_refs, block, table, order_ref, per):
        g = slot[src, :].astype(jnp.float32)
        for h in range(heads):
            g_ref[h, dst, :] = head_lanes(g, h, heads, depth).astype(jnp.bfloat16)
    tiles = total // tile
    def prepare(t, _):
        rows = pl.ds(pl.multiple_of(t*tile, tile), tile)
        k_t_ref[:, rows] = jnp.transpose(k_ref[rows, :].astype(jnp.float32)).astype(jnp.bfloat16)
        g = g_ref[0, rows, :].astype(jnp.float32)
        for h in range(1, heads):
            g = g + g_ref[h, rows, :].astype(jnp.float32)
        prod = jnp.transpose(g) * out_t_ref[:, rows]
        for h in range(heads):
            delta_ref[h:h+1, rows] = jnp.sum(prod[h*depth:(h+1)*depth], axis=0, keepdims=True)
        dq_t_ref[:, rows] = jnp.zeros((width, tile), jnp.float32)
        return 0
    lax.fori_loop(0, tiles, prepare, 0)
    def one_key(j, _):
        keys = pl.ds(pl.multiple_of(j*tile, tile), tile)
        k = k_ref[keys, :]
        v = v_ref[keys, :]
        k_t = k_t_ref[:, keys]
        dk_ref[keys, :] = jnp.zeros((tile, width), jnp.float32)
        dv_ref[keys, :] = jnp.zeros((tile, width), jnp.float32)
        def one_query(t, _):
            rows = pl.ds(pl.multiple_of(t*tile, tile), tile)
            mask = seen(ends, t*tile, j*tile, tile)
            dk = dk_ref[keys, :]
            dv = dv_ref[keys, :]
            for h in range(heads):
                q = q_ref[h, rows, :]
                g = g_ref[h, rows, :]
                s = nt(k, q)
                p = jnp.where(mask, jnp.exp(s - lse_ref[h:h+1, rows]), 0.0)
                dp = nt(v, g)
                ds = (p*(dp - delta_ref[h:h+1, rows])).astype(jnp.bfloat16)
                dv = dv + nn(p.astype(jnp.bfloat16), g)
                dk = dk + nn(ds, q)
                part = pl.ds(h*depth, depth)
                dq_t_ref[part, rows] = dq_t_ref[part, rows] + nn(k_t[h*depth:(h+1)*depth], ds)
            dk_ref[keys, :] = dk
            dv_ref[keys, :] = dv
            return 0
        lax.fori_loop(j, last_tile(ends, j*tile + tile - 1, tile) + 1, one_query, 0)
        return 0
    lax.fori_loop(0, tiles, one_key, 0)
    def finish(t, _):
        rows = pl.ds(pl.multiple_of(t*tile, tile), tile)
        dq_ref[rows, :] = (jnp.transpose(dq_t_ref[:, rows])*scale).astype(jnp.bfloat16)
        return 0
    lax.fori_loop(0, tiles, finish, 0)
    for slot, dst, src in placed(dqkv_refs, block, table, order_ref, per):
        slot[dst, 0:width] = dq_ref[src, :]
        slot[dst, width:2*width] = dk_ref[src, :].astype(jnp.bfloat16)
        slot[dst, 2*width:3*width] = dv_ref[src, :].astype(jnp.bfloat16)
    shard = part_out_ref.shape[1]
    for k in range(n):
        dqkv_refs[k][0:shard, 3*width:] = part_out_ref[k]
        if shard < dqkv_refs[k].shape[0]:
            dqkv_refs[k][shard:, 3*width:] = jnp.zeros((dqkv_refs[k].shape[0]-shard, width), jnp.bfloat16)

SM=pl.BlockSpec(memory_space=pltpu.SMEM)
VM=pl.BlockSpec(memory_space=pltpu.VMEM)
def attention_forward(table, lengths, order, qkv, n, heads, depth, tile):
    total=sum(x.shape[0] for x in qkv); rows=total//n; width=heads*depth
    block=total//order.shape[1]
    meta=(len(qkv),n,heads,depth,tile,block)
    res=pl.pallas_call(functools.partial(fwd_kernel,meta),
        out_shape=[jax.ShapeDtypeStruct((rows,width),jnp.bfloat16)]*n+[jax.ShapeDtypeStruct((width,total),jnp.float32),jax.ShapeDtypeStruct((heads,total),jnp.float32)],
        in_specs=[SM,SM,SM]+[VM]*len(qkv), out_specs=[VM]*(n+2),
        scratch_shapes=[pltpu.VMEM((heads,total,width),jnp.bfloat16)]+[pltpu.VMEM((total,width),jnp.bfloat16)]*3,
        cost_estimate=cost(17),
        name="attention_forward")(table,lengths,order,*qkv)
    return list(res[:n]),res[n],res[n+1]
def attention_backward(table, lengths, order, qkv, grads, part_out, out_t, lse, heads, depth, tile):
    n=len(grads); rows=grads[0].shape[0]; total=n*rows; width=heads*depth
    block=total//order.shape[1]
    meta=(len(qkv),n,heads,depth,tile,block)
    f32=jnp.float32; b16=jnp.bfloat16
    return list(pl.pallas_call(functools.partial(bwd_kernel,meta),
        out_shape=[jax.ShapeDtypeStruct((rows,4*width),b16)]*n,
        in_specs=[SM,SM,SM]+[VM]*(len(qkv)+n+3), out_specs=[VM]*n,
        scratch_shapes=[pltpu.VMEM((heads,total,width),b16),pltpu.VMEM((total,width),b16),pltpu.VMEM((total,width),b16),pltpu.VMEM((heads,total,width),b16),
          pltpu.VMEM((width,total),b16),pltpu.VMEM((heads,total),f32),pltpu.VMEM((width,total),f32),pltpu.VMEM((total,width),b16),pltpu.VMEM((total,width),f32),pltpu.VMEM((total,width),f32)],
        cost_estimate=cost(18),
        name="attention_backward")(table,lengths,order,*qkv,*grads,part_out,out_t,lse))


def tn(left, right):
    return lax.dot_general(left, right, (((0,), (0,)), ((), ())), preferred_element_type=jnp.float32)


def low(value):
    return value.astype(jnp.bfloat16)


def wide(value):
    return value.astype(jnp.float32)


def at(start, size):
    return pl.ds(pl.multiple_of(start, size), size)


def cost(microseconds):
    return pl.CostEstimate(flops=0, bytes_accessed=int(microseconds * 3.4e6), transcendentals=0)


def call(name, kernel, out, inputs, scratch=(), time=2.0):
    return list(
        pl.pallas_call(
            kernel,
            out_shape=list(out),
            in_specs=[SM] + [VM] * (len(inputs) - 1),
            out_specs=[VM] * len(out),
            scratch_shapes=list(scratch),
            cost_estimate=cost(time),
            name=name,
        )(*inputs)
    )


def shape(dims, dtype=jnp.bfloat16):
    return jax.ShapeDtypeStruct(tuple(dims), dtype)


def slice_kernel(own_width, table, w_ref, one_ref, two_ref, out_ref):
    shard, total = w_ref.shape
    for part in range(3):
        out_ref[0:shard, part * own_width : (part + 1) * own_width] = w_ref[
            :, at(part * (total // 3) + table[0, 0] * own_width, own_width)
        ]
    out_ref[shard : shard + 8, :] = gain_rows(wide(one_ref[...]), wide(two_ref[...]), 3 * own_width)


def gain_rows(one, two, lanes):
    shard = one.shape[1]
    if lanes > shard:
        rest = jnp.zeros((1, lanes - shard), jnp.float32)
        one, two = jnp.concatenate([one, rest], axis=1), jnp.concatenate([two, rest], axis=1)
    number = lax.broadcasted_iota(jnp.int32, (8, lanes), 0)
    return low(jnp.where(number == 0, one, jnp.where(number == 1, two, 0.0)))


def full_gain(table, n, pieces, row, gain_ref):
    shard = gain_ref.shape[1] // len(pieces)
    for slot, piece in enumerate(pieces):
        lines = wide(piece[pl.ds(piece.shape[0] - 8, 8), 0:shard])
        gain_ref[0:1, at(table[0, n + slot] * shard, shard)] = lines[row : row + 1]


def split_kernel(n, table, w_ref, *refs):
    outs, parts_ref = refs[:-1], refs[-1]
    count = len(outs)
    hidden = w_ref.shape[1] // (2 * count)
    for part in range(count):
        parts_ref[part, :, 0:hidden] = w_ref[:, part * hidden : (part + 1) * hidden]
        parts_ref[part, :, hidden:] = w_ref[:, (count + part) * hidden : (count + part + 1) * hidden]
    for slot in range(count):
        outs[slot][...] = parts_ref[table[0, n + slot]]


def project_kernel(n, table, rows_ref, *refs):
    pieces, attn_ref, qkv_ref, gain_ref, weight_ref = refs[:-4], refs[-4], refs[-3], refs[-2], refs[-1]
    shard = rows_ref.shape[1] // len(pieces)
    full_gain(table, n, pieces, 0, gain_ref)
    for slot, piece in enumerate(pieces):
        weight_ref[at(table[0, n + slot] * shard, shard), :] = piece[pl.ds(0, shard), :]
    value = wide(rows_ref[...])
    inverse = lax.rsqrt(jnp.mean(value * value, axis=1, keepdims=True) + EPS)
    attn_in = low(value * inverse * gain_ref[0:1, :])
    attn_ref[...] = attn_in
    qkv_ref[...] = low(nn(attn_in, weight_ref[...]))


def stage_rows(table, n, pieces, weight_ref):
    shard = pieces[0].shape[0]
    for slot, piece in enumerate(pieces):
        weight_ref[at(table[0, n + slot] * shard, shard), :] = piece[...]


def leave_kernel(n, count, table, tokens_ref, *refs):
    parts, outs, slices = refs[:n], refs[n : n + count], refs[n + count : n + 2 * count]
    resid_ref, ffn_ref, gain_ref, weight_ref, sum_ref = refs[n + 2 * count :]
    own_width = parts[0].shape[1]
    full_gain(table, n, slices, 1, gain_ref)
    stage_rows(table, n, outs, weight_ref)
    rows = tokens_ref.shape[0]
    attn = jnp.concatenate([parts[k][...] for k in range(n)], axis=1)
    ordered = jnp.concatenate([weight_ref[at(table[0, k] * own_width, own_width), :] for k in range(n)], axis=0)
    resid = wide(tokens_ref[...]) + nn(attn, ordered)
    resid_ref[...] = resid
    inverse = lax.rsqrt(jnp.mean(resid * resid, axis=1, keepdims=True) + EPS)
    ffn_ref[...] = low(resid * inverse * gain_ref[0:1, :])


def ffn_kernel(n, count, slots, table, *refs):
    ffn, cot = refs[:slots], refs[slots : 2 * slots]
    pieces, down_ref = refs[2 * slots : 2 * slots + count], refs[2 * slots + count]
    rest = refs[2 * slots + count + 1 :]
    terms, outs, hidden_ref, grad_ref = rest[:slots], rest[slots : 2 * slots], rest[2 * slots], rest[2 * slots + 1]
    gate_ref, up_ref = rest[2 * slots + 2 :]
    hidden = down_ref.shape[0]
    shard = pieces[0].shape[0]
    rows = ffn[0].shape[0]
    for slot, piece in enumerate(pieces):
        place = at(table[0, n + slot] * shard, shard)
        gate_ref[place, :] = piece[:, 0:hidden]
        up_ref[place, :] = piece[:, hidden:]
    for slot in range(slots):
        value = ffn[slot][...]
        gate = nn(value, gate_ref[...])
        upward = nn(value, up_ref[...])
        grad_hidden = nt(cot[slot][...], down_ref[...])
        sigma = jax.nn.sigmoid(gate)
        active = gate * sigma
        hidden_low = low(active * upward)
        grad_gate = low(grad_hidden * upward * (sigma + active * (1.0 - sigma)))
        grad_up = low(grad_hidden * active)
        terms[slot][...] = low(nt(grad_gate, gate_ref[...]) + nt(grad_up, up_ref[...]))
        outs[slot][...] = low(nn(hidden_low, down_ref[...]))
        place = pl.ds(slot * rows, rows)
        hidden_ref[place, :] = hidden_low
        grad_ref[place, 0:hidden] = grad_gate
        grad_ref[place, hidden:] = grad_up


def ffn_weight_kernel(n, count, table, *refs):
    ffn, cot, rest = refs[:count], refs[count : 2 * count], refs[2 * count :]
    hiddens, grads, rest = rest[: count // 2], rest[count // 2 : count], rest[count:]
    outs, (value_ref, turned_ref) = rest[:-2], rest[-2:]
    hidden = hiddens[0].shape[1]
    half = n // 2
    shard = ffn[0].shape[1] // count
    sub = shard // n
    lines = count * sub
    cut = outs[half].shape[0]
    hidden_all = jnp.concatenate([r[...] for r in hiddens], axis=0)
    grad_all = jnp.concatenate([r[...] for r in grads], axis=0)

    def store(slot, row, lanes, value):
        if slot != half:
            outs[slot if slot < half else slot + 1][row : row + sub, lanes] = value
        elif row < cut:
            outs[half][row : row + sub, lanes] = value
        else:
            outs[half + 1][row - cut : row - cut + sub, lanes] = value

    for f in range(count):
        lanes = slice(f * shard, (f + 1) * shard)
        ffn_all = jnp.concatenate([r[:, lanes] for r in ffn], axis=0)
        value_ref[...] = low(tn(ffn_all, grad_all))
        cot_all = jnp.concatenate([r[:, lanes] for r in cot], axis=0)
        turned_ref[...] = low(tn(cot_all, hidden_all))
        side, line = f // (count // 2), lines + (f % (count // 2)) * sub
        for slot in range(n):
            mine = at(table[0, slot] * sub, sub)
            store(slot, f * sub, slice(0, 2 * hidden), value_ref[mine, :])
            store(slot, line, slice(side * hidden, (side + 1) * hidden), turned_ref[mine, :])


def branch_kernel(n, count, got, table, resid_ref, cot_ref, *refs):
    terms, outs, slices = refs[:got], refs[got : got + count], refs[got + count : got + 2 * count]
    rest = refs[got + 2 * count :]
    grad_ref, branch_ref, parts = rest[0], rest[1], rest[2 : 2 + n]
    gain_ref, weight_ref, scratch_ref = rest[2 + n :]
    own_width = parts[0].shape[1]
    full_gain(table, n, slices, 1, gain_ref)
    stage_rows(table, n, outs, weight_ref)
    resid = resid_ref[...]
    inverse = lax.rsqrt(jnp.mean(resid * resid, axis=1, keepdims=True) + EPS)
    normed = resid * inverse
    grad = wide(terms[0][...])
    for term in terms[1:]:
        grad = grad + wide(term[...])
    scaled = grad * gain_ref[0:1, :]
    inner = jnp.mean(scaled * normed, axis=1, keepdims=True)
    grad_resid = wide(cot_ref[...]) + inverse * (scaled - normed * inner)
    grad_ref[...] = grad_resid
    branch = low(grad_resid)
    branch_ref[...] = branch
    for k in range(n):
        parts[k][...] = low(nt(branch, weight_ref[at(table[0, k] * own_width, own_width), :]))


def out_weight_kernel(n, count, table, branch_ref, *refs):
    parts, outs, whole_ref = refs[:n], refs[n : n + count], refs[-1]
    own_width = parts[0].shape[1]
    shard = outs[0].shape[1]
    branch = branch_ref[...]
    for k in range(n):
        whole_ref[at(table[0, k] * own_width, own_width), :] = low(tn(parts[k][...], branch))
    for slot in range(count):
        lines = at(table[0, n + slot] * shard, shard)
        for k in range(n):
            if own_width % 128 == 0:
                outs[slot][k] = whole_ref[lines, at(table[0, k] * own_width, own_width)]
            else:
                outs[slot][k] = whole_ref[lines, k * own_width : (k + 1) * own_width]


def qkv_weight_kernel(given, n, count, table, *refs):
    attn, grads, outs = refs[:given], refs[given : given + n], refs[given + n :]
    shard = outs[0].shape[0]
    grad_all = jnp.concatenate([r[:, 0 : outs[0].shape[1]] for r in grads], axis=0)
    for slot in range(count):
        lanes = at(table[0, n + slot] * shard, shard)
        attn_all = jnp.concatenate([r[:, lanes] for r in attn], axis=0)
        outs[slot][...] = low(tn(attn_all, grad_all))


def tail_kernel(n, count, aligned, table, tokens_ref, grad_ref, *refs):
    parts, weights, slices = refs[:n], refs[n : -4 - count], refs[-4 - count : -4]
    out_ref, gain_ref, sum_ref, grads_ref = refs[-4:]
    pieces = len(weights) // count
    own_width = parts[0].shape[1] // 4
    width = tokens_ref.shape[1]
    shard = width // count
    full_gain(table, n, slices, 0, gain_ref)
    for k in range(n):
        for part in range(3):
            value = parts[k][:, part * own_width : (part + 1) * own_width]
            if aligned:
                grads_ref[:, at(part * width + table[0, k] * own_width, own_width)] = value
            else:
                start = (k * 3 + part) * own_width
                grads_ref[:, start : start + own_width] = value
    for slot in range(count):
        for piece in range(pieces):
            size = shard // pieces
            place = at(table[0, n + slot] * shard + piece * size, size)
            sum_ref[:, place] = nt(grads_ref[...], weights[slot * pieces + piece][...])
    value = wide(tokens_ref[...])
    inverse = lax.rsqrt(jnp.mean(value * value, axis=1, keepdims=True) + EPS)
    normed = value * inverse
    scaled = sum_ref[...] * gain_ref[0:1, :]
    inner = jnp.mean(scaled * normed, axis=1, keepdims=True)
    out_ref[...] = low(grad_ref[...] + inverse * (scaled - normed * inner))


def row_sums(product):
    rows, lanes = product.shape
    total = product[:, 0:128]
    for i in range(1, lanes // 128):
        total = total + product[:, i * 128 : (i + 1) * 128]
    return jnp.sum(jnp.transpose(total), axis=0, keepdims=True)


def ffn_final_kernel(n, count, factor, table, w_ref, gain_ref, *refs):
    pieces = refs[: n + 1]
    gu_ref, down_ref, gain_out_ref, turned_ref = refs[n + 1 :]
    hidden = down_ref.shape[0]
    sub = gu_ref.shape[0] // n
    half = n // 2
    for k in range(n):
        if k == half:
            piece = jnp.concatenate([wide(pieces[half][...]), wide(pieces[half + 1][...])], axis=0)
        else:
            piece = wide(pieces[k if k < half else k + 1][...])
        piece = piece * factor
        start = table[0, k] * sub
        for part in range(count):
            lines = piece[part * sub : (part + 1) * sub]
            gu_ref[at(start, sub), part * hidden : (part + 1) * hidden] = lines[:, 0:hidden]
            gu_ref[at(start, sub), (count + part) * hidden : (count + part + 1) * hidden] = lines[:, hidden:]
            side, line = part // (count // 2), (count + part % (count // 2)) * sub
            turned_ref[at(part * (n * sub) + start, sub), :] = piece[line : line + sub, side * hidden : (side + 1) * hidden]
    width = turned_ref.shape[0]
    for i in range(width // 128):
        down_ref[:, i * 128 : (i + 1) * 128] = jnp.transpose(turned_ref[i * 128 : (i + 1) * 128, :])
    gain_out_ref[...] = row_sums(wide(w_ref[...]) * gu_ref[...]) / wide(gain_ref[...])


def attn_final_kernel(n, factor, aligned, table, w_ref, gain_ref, *refs):
    pieces = refs[: n + 1]
    qkv_ref, out_ref, gain_out_ref = refs[n + 1 :]
    own_width = pieces[0].shape[1] // 4
    width = out_ref.shape[1]
    half = n // 2
    for k in range(n):
        if k == half:
            piece = jnp.concatenate([wide(pieces[half][...]), wide(pieces[half + 1][...])], axis=0)
        else:
            piece = wide(pieces[k if k < half else k + 1][...])
        piece = piece * factor
        for part in range(4):
            value = piece[:, part * own_width : (part + 1) * own_width]
            target = out_ref if part == 3 else qkv_ref
            base = 0 if part == 3 else part * width
            if aligned:
                target[:, at(base + table[0, k] * own_width, own_width)] = value
            else:
                target[:, base + k * own_width : base + (k + 1) * own_width] = value
    gain_out_ref[...] = row_sums(wide(w_ref[...]) * qkv_ref[...]) / wide(gain_ref[...])


def cut_kernel(n, table, own_ref, up_ref, down_ref, *refs):
    outs, rest_ref, sum_ref = refs[:-2], refs[-2], refs[-1]
    sum_ref[...] = low(wide(own_ref[...]) + wide(up_ref[...]) + wide(down_ref[...]))
    sub = outs[0].shape[0]
    for slot, out in enumerate(outs):
        out[...] = sum_ref[at(table[0, n + slot] * sub, sub), :]
    rest_ref[...] = sum_ref[len(outs) * sub :, :]


def pack_kernel(n, table, rest_ref, *refs):
    pieces, out_ref = refs[:-1], refs[-1]
    sub = pieces[0].shape[0]
    for slot, piece in enumerate(pieces):
        out_ref[at(table[0, n + slot] * sub, sub), :] = piece[...]
    out_ref[len(pieces) * sub :, :] = rest_ref[...]


def join_kernel(terms, table, *refs):
    qkv, back, out_ref = refs[:terms], refs[terms:-1], refs[-1]
    total = wide(qkv[0][...])
    for term in qkv[1:]:
        total = total + wide(term[...])
    start = total.shape[1]
    out_ref[:, 0:start] = low(total)
    shard = out_ref.shape[0]
    other = wide(back[0][0:shard, start:])
    for term in back[1:]:
        other = other + wide(term[0:shard, start:])
    out_ref[:, start:] = low(other)


def ring_of(count):
    if count % 4 or count < 8:
        return list(range(count))
    across = count // 4
    order = []
    for along in range(4):
        columns = range(1, across) if along % 2 == 0 else range(across - 1, 0, -1)
        order += [along * across + column for column in columns]
    return order + [along * across for along in reversed(range(4))]


def ring_shift(value, ring, step):
    count = len(ring)
    return lax.ppermute(
        value, "ctx", [(ring[i], ring[(i + step) % count]) for i in range(count)]
    )


def tie(*values):
    return lax.optimization_barrier(values)


class Gather:
    def __init__(self, value, ring):
        self.ring, self.half, self.step = ring, len(ring) // 2, 1
        self.first, self.ahead, self.behind, self.far = value, [], [], None
        self.up, self.down = tie(ring_shift(value, ring, 1), ring_shift(value, ring, -1))

    def advance(self, *others):
        self.ahead.append(self.down)
        self.behind.append(self.up)
        self.up, self.down, *others = tie(self.up, self.down, *others)
        self.step += 1
        up, down = self.up, self.down
        if self.step == self.half:
            cut = up.shape[0] // 2
            up, down = up[:cut], down[cut:]
        self.up, self.down = tie(ring_shift(up, self.ring, 1), ring_shift(down, self.ring, -1))
        return others

    def slots(self):
        while self.step < self.half:
            self.advance()
        return [self.first] + self.ahead + [self.up, self.down] + self.behind[::-1]


class Scatter:
    def __init__(self, terms, ring):
        self.ring, self.half, self.terms = ring, len(ring) // 2, terms
        self.up, self.down = terms[self.half : self.half + 2]
        self.step = self.half
        self.send()

    def send(self):
        self.up, self.down = tie(ring_shift(self.up, self.ring, 1), ring_shift(self.down, self.ring, -1))

    def advance(self, *others):
        self.up, self.down, *others = tie(self.up, self.down, *others)
        up, down, cut = self.terms[self.step - 1], self.terms[len(self.ring) + 2 - self.step], self.up.shape[0]
        if self.step == self.half:
            rows = up.shape[0]
            self.up = low(wide(up) + jnp.pad(wide(self.up), ((0, rows - cut), (0, 0))))
            self.down = low(wide(down) + jnp.pad(wide(self.down), ((rows - cut, 0), (0, 0))))
        else:
            self.up, self.down = add_low(up, self.up), add_low(down, self.down)
        self.step -= 1
        self.send()
        return others

    def sums(self):
        while self.step > 1:
            self.advance()
        return [self.terms[0], self.up, self.down]


def ring_exchange(slots, ring):
    count = len(ring)
    result = [slots[0]] + [None] * (count - 1)
    for k in range(1, count):
        result[count - k] = ring_shift(slots[k], ring, k)
    return result


def partner(value, count):
    return lax.ppermute(value, "fsdp", [(i, i ^ 1) for i in range(count)])


def chip_shift(value, count, step):
    return lax.ppermute(value, "fsdp", [(i, (i + 2 * step) % count) for i in range(count)])


def far_gather(value, count):
    return [value] + [chip_shift(value, count, -step) for step in range(1, count // 2)]


def near_gather(nears, count):
    slots = []
    for near in nears:
        slots += [near, partner(near, count)]
    return slots


def near_scatter(terms, count):
    return [add_low(terms[i], partner(terms[i + 1], count)) for i in range(0, count, 2)]


def far_scatter(nears, count):
    return [nears[0]] + [chip_shift(nears[step], count, step) for step in range(1, count // 2)]


def side_exchange(pieces, count):
    chips = count // 2
    received = [None] * count
    for step in range(chips):
        for flip in (0, 1):
            piece = pieces[2 * step + flip]
            if step or flip:
                pairs = [(i, ((i + 2 * step) % count) ^ flip) for i in range(count)]
                piece = lax.ppermute(piece, "fsdp", pairs)
            received[2 * ((chips - step) % chips) + flip] = piece
    return received


def add_low(left, right):
    return low(wide(left) + wide(right))


def total_of(terms):
    total = wide(terms[0])
    for term in terms[1:]:
        total = total + wide(term)
    return total


def body(
    tokens, cotangent, gain_attn, w_qkv, w_out, gain_ffn, w_gate_up, w_down, lengths, block_order
):
    rows, width = tokens.shape
    heads = HEADS
    depth = width // heads
    ctx = lax.axis_size("ctx")
    fsdp = lax.axis_size("fsdp")
    factor = 1.0 / math.sqrt(rows * ctx * fsdp)
    shard = width // fsdp
    hidden = w_down.shape[0]
    own_heads = heads // ctx
    own_width = own_heads * depth
    aligned = own_width % 128 == 0
    half = ctx // 2
    sub = shard // ctx
    lines = fsdp * sub
    ring = ring_of(ctx)
    chips = fsdp // 2
    entries = []
    for c in range(ctx):
        me = ring.index(c)
        for f in range(fsdp):
            owners = [ring[(me + k) % ctx] for k in range(ctx)]
            sides = [((f // 2 + s) % chips) * 2 + ((f % 2) ^ k) for s in range(chips) for k in (0, 1)]
            entries.append(owners + sides)
    device = lax.axis_index("ctx") * fsdp + lax.axis_index("fsdp")
    table = lax.dynamic_slice_in_dim(jnp.asarray(entries, jnp.int32), device, 1, 0)
    gain_one, gain_two = gain_attn.reshape(1, shard), gain_ffn.reshape(1, shard)
    f32 = jnp.float32
    gain_scratch = pltpu.VMEM((8, width), f32)
    square_scratch = pltpu.VMEM((width, width), jnp.bfloat16)

    going = Gather(tokens, ring)
    if aligned:
        (piece,) = call(
            "slice", functools.partial(slice_kernel, own_width),
            [shape((shard + 8, 3 * own_width))], [table, w_qkv, gain_one, gain_two],
            time=2.2,
        )
    else:
        mine = [
            lax.dynamic_slice(w_qkv, (0, part * width + table[0, 0] * own_width), (shard, own_width))
            for part in range(3)
        ]
        piece = jnp.concatenate(
            [jnp.concatenate(mine, axis=1), gain_rows(wide(gain_one), wide(gain_two), 3 * own_width)], axis=0
        )
    slices = far_gather(piece, fsdp)
    gate_pieces = call(
        "split", functools.partial(split_kernel, ctx),
        [shape((shard, 2 * hidden))] * fsdp, [table, w_gate_up],
        scratch=[pltpu.VMEM((fsdp, shard, 2 * hidden), jnp.bfloat16)],
        time=4,
    )
    slices, gate_pieces = going.advance(slices, gate_pieces)
    slices = near_gather(slices, fsdp)
    gate_pieces = side_exchange(gate_pieces, fsdp)

    def project(slot):
        return call(
            "project", functools.partial(project_kernel, ctx),
            [shape(slot.shape), shape((slot.shape[0], 3 * own_width))], [table, slot] + slices,
            scratch=[gain_scratch, pltpu.VMEM((width, 3 * own_width), jnp.bfloat16)],
            time=2.6,
        )

    first = project(tokens)
    ahead, behind = [project(going.ahead[0])], [project(going.behind[0])]
    first, ahead[0], behind[0], gate_pieces[1:3] = going.advance(first, ahead[0], behind[0], gate_pieces[1:3])
    for step in range(1, half - 1):
        ahead.append(project(going.ahead[step]))
        behind.append(project(going.behind[step]))
        if going.step < half:
            ahead[step], behind[step], gate_pieces[3:] = going.advance(ahead[step], behind[step], gate_pieces[3:])
    later_out, later_cot, later_qkv, unused = tie(w_out, cotangent, w_qkv, gate_pieces[-1])
    outs = far_gather(later_out, fsdp)
    *far, ahead, behind = tie(going.up, going.down, ahead, behind)
    pairs = [first] + ahead + [project(far[0]), project(far[1])] + behind[::-1]
    attn_slots, qkv = [pair[0] for pair in pairs], [pair[1] for pair in pairs]

    out_slots, out_t, log_total = attention_forward(
        table, lengths, block_order, qkv, ctx, own_heads, depth, TILE
    )
    qkv_halves = [later_qkv[: shard // 2], later_qkv[shard // 2 :]] if aligned else [relative(later_qkv, table, ctx)]
    qkv_nears = [far_gather(qkv_halves[0], fsdp)]
    out_slots, qkv_nears[0], outs = tie(out_slots, qkv_nears[0], outs)
    attn_parts = ring_exchange(out_slots, ring)
    later_cot, unused = tie(later_cot, out_slots[0])
    outs, cots = near_gather(outs, fsdp), near_gather(far_gather(later_cot, fsdp), fsdp)
    attn_parts, outs, cots[2::2] = tie(attn_parts, outs, cots[2::2])
    resid, ffn_in = call(
        "leave", functools.partial(leave_kernel, ctx, fsdp),
        [shape((rows, width), f32), shape((rows, width))],
        [table, tokens] + attn_parts + outs + slices,
        scratch=[gain_scratch, square_scratch, pltpu.VMEM((8, 128), f32)],
        time=4.1,
    )

    nears = far_gather(ffn_in, fsdp)
    ffns, grad_terms, out_terms, hiddens, grads = [], [], [], [], []
    for chip in range(chips):
        ffn_pair = [nears[chip], partner(nears[chip], fsdp)]
        result = call(
            "feed_forward", functools.partial(ffn_kernel, ctx, fsdp, 2),
            [shape((rows, width))] * 4 + [shape((2 * rows, hidden)), shape((2 * rows, 2 * hidden))],
            [table] + ffn_pair + cots[2 * chip : 2 * chip + 2] + gate_pieces + [w_down],
            scratch=[pltpu.VMEM((width, hidden), jnp.bfloat16)] * 2,
            time=9.5,
        )
        if chip == 0:
            result, nears[1:] = tie(result, nears[1:])
        ffns += ffn_pair
        grad_terms += result[0:2]
        out_terms += result[2:4]
        hiddens.append(result[4])
        grads.append(result[5])
    grad_nears = near_scatter(grad_terms, fsdp)
    hiddens, grad_nears = tie(hiddens, grad_nears)
    grad_parts = far_scatter(grad_nears, fsdp)
    terms_ffn = call(
        "feed_forward_weights", functools.partial(ffn_weight_kernel, ctx, fsdp),
        [shape((lines + lines // 2, 2 * hidden))] * half
        + [shape(((lines + lines // 2) // 2, 2 * hidden))] * 2
        + [shape((lines + lines // 2, 2 * hidden))] * (half - 1),
        [table] + ffns + cots + hiddens + grads,
        scratch=[pltpu.VMEM((shard, 2 * hidden), jnp.bfloat16), pltpu.VMEM((shard, hidden), jnp.bfloat16)],
        time=12,
    )
    terms_ffn, grad_parts = tie(terms_ffn, grad_parts)
    ffn_sums = Scatter(terms_ffn, ring)
    grad_resid, branch, *grad_attn = call(
        "branch", functools.partial(branch_kernel, ctx, fsdp, len(grad_parts)),
        [shape((rows, width), f32), shape((rows, width))] + [shape((rows, own_width))] * ctx,
        [table, resid, cotangent] + grad_parts + outs + slices,
        scratch=[gain_scratch, square_scratch, pltpu.VMEM((8, 128), f32)],
        time=5,
    )
    grad_slots = ring_exchange(grad_attn, ring)
    out_sides = call(
        "out_weights", functools.partial(out_weight_kernel, ctx, fsdp),
        [shape((ctx, shard, own_width))] * fsdp, [table, branch] + attn_parts,
        scratch=[square_scratch],
        time=3.3,
    )
    if not aligned:
        out_sides = [by_slot(array, table, ctx) for array in out_sides]
    out_nears = near_scatter(out_sides, fsdp)

    out_parts = far_scatter(out_nears, fsdp)
    part_out = low(total_of(out_parts))
    grad_slots, part_out = ffn_sums.advance(grad_slots, part_out)
    grad_qkv = attention_backward(
        table, lengths, block_order, qkv, grad_slots, part_out, out_t, log_total, own_heads, depth, TILE
    )
    (grad_qkv,) = ffn_sums.advance(grad_qkv)
    qkv_halves, unused = tie(qkv_halves, grad_qkv[0])
    qkv_nears += [far_gather(piece, fsdp) for piece in qkv_halves[1:]]
    grad_back = ring_exchange(grad_qkv, ring)
    qkv_sides = call(
        "qkv_weights", functools.partial(qkv_weight_kernel, len(attn_slots), ctx, fsdp),
        [shape((shard, 3 * own_width))] * fsdp, [table] + attn_slots + grad_qkv,
        time=6,
    )
    qkv_sum_nears = near_scatter(qkv_sides, fsdp)
    third = max(1, (ctx - 1) * 3 // 7)
    grad_back[-third:], qkv_sum_nears = ffn_sums.advance(grad_back[-third:], qkv_sum_nears)
    qkv_sum = far_scatter(qkv_sum_nears, fsdp)
    weights = [near_gather(nears, fsdp) for nears in qkv_nears]
    weights = [pieces[slot] for slot in range(fsdp) for pieces in weights]

    own_sum, ffn_up, ffn_down = ffn_sums.sums()
    second = third + max(1, (ctx - 1) * 2 // 7)
    ffn_up, ffn_down, qkv_sum, grad_back[-second:-third] = tie(ffn_up, ffn_down, qkv_sum, grad_back[-second:-third])
    *gate_sides, rest = call(
        "cut", functools.partial(cut_kernel, ctx),
        [shape((sub, 2 * hidden))] * fsdp + [shape((lines // 2, 2 * hidden))],
        [table, own_sum, ffn_up, ffn_down],
        scratch=[pltpu.VMEM((lines + lines // 2, 2 * hidden), jnp.bfloat16)],
        time=3,
    )
    gate_sides = side_exchange(gate_sides, fsdp)
    gate_sides, grad_back[1:-second], weights = tie(gate_sides, grad_back[1:-second], weights)
    (packed,) = call(
        "pack", functools.partial(pack_kernel, ctx),
        [shape((lines + lines // 2, 2 * hidden))], [table, rest] + gate_sides,
        time=2,
    )
    ffn_going = Gather(packed, ring)
    (grad_tokens,) = call(
        "tail", functools.partial(tail_kernel, ctx, fsdp, aligned),
        [shape((rows, width))], [table, tokens, grad_resid] + grad_back + weights + slices,
        scratch=[gain_scratch, pltpu.VMEM((rows, width), f32), pltpu.VMEM((rows, 3 * width), jnp.bfloat16)],
        time=8,
    )
    (joined,) = call(
        "join", functools.partial(join_kernel, len(qkv_sum)),
        [shape((shard, 4 * own_width))], [table] + qkv_sum + grad_back,
        time=2.5,
    )
    joined, grad_tokens = ffn_going.advance(joined, grad_tokens)
    ffn_going.advance()
    joined, unused = tie(joined, ffn_going.behind[-1])
    attn_going = Gather(joined, ring)
    grad_w_gate_up, grad_w_down, grad_gain_ffn = call(
        "feed_forward_final", functools.partial(ffn_final_kernel, ctx, fsdp, factor),
        [shape((shard, 2 * hidden * fsdp), f32), shape((hidden, width), f32), shape((1, shard), f32)],
        [table, w_gate_up, gain_two] + ffn_going.slots(),
        scratch=[pltpu.VMEM((width, hidden), f32)],
        time=8,
    )
    grad_w_qkv, grad_w_out, grad_gain_attn = call(
        "attention_final", functools.partial(attn_final_kernel, ctx, factor, aligned),
        [shape((shard, 3 * width), f32), shape((shard, width), f32), shape((1, shard), f32)],
        [table, w_qkv if aligned else unmixed(relative(w_qkv, table, ctx), ctx, own_width), gain_one] + attn_going.slots(),
        time=4.6,
    )
    if not aligned:
        grad_w_qkv, grad_w_out = ordered(grad_w_qkv, table, 3, ctx), ordered(grad_w_out, table, 1, ctx)
    output = low(resid + total_of(far_scatter(near_scatter(out_terms, fsdp), fsdp)))
    return (
        output,
        grad_tokens,
        grad_gain_attn.reshape(shard),
        grad_w_qkv,
        grad_w_out,
        grad_gain_ffn.reshape(shard),
        grad_w_gate_up,
        grad_w_down,
    )


def relative(weight, table, ctx):
    rows = weight.shape[0]
    parts = weight.reshape(rows, 3, ctx, -1)
    slots = [lax.dynamic_index_in_dim(parts, table[0, k], 2, keepdims=False) for k in range(ctx)]
    return jnp.concatenate([slot.reshape(rows, -1) for slot in slots], axis=1)


def by_slot(array, table, ctx):
    return jnp.stack([lax.dynamic_index_in_dim(array, table[0, k], 0, keepdims=False) for k in range(ctx)])


def unmixed(weight, ctx, own_width):
    rows = weight.shape[0]
    return weight.reshape(rows, ctx, 3, own_width).transpose(0, 2, 1, 3).reshape(rows, -1)


def ordered(array, table, parts, ctx):
    rows = array.shape[0]
    split = array.reshape(rows, parts, ctx, -1)
    result = jnp.zeros_like(split)
    for k in range(ctx):
        result = lax.dynamic_update_slice(result, split[:, :, k : k + 1], (0, 0, table[0, k], 0))
    return result.reshape(rows, -1)


def solution(mesh):
    in_specs = (
        P(("fsdp", "ctx"), None),
        P(("fsdp", "ctx"), None),
        P("fsdp"),
        P("fsdp", None),
        P("fsdp", None),
        P("fsdp"),
        P("fsdp", None),
        P("fsdp", None),
        P("fsdp", None),
        P("fsdp", None),
    )
    out_specs = (
        P(("fsdp", "ctx"), None),
        P(("fsdp", "ctx"), None),
        P("fsdp"),
        P("fsdp", None),
        P("fsdp", None),
        P("fsdp"),
        P("fsdp", None),
        P("fsdp", None),
    )
    return jax.shard_map(body, mesh=mesh, in_specs=in_specs, out_specs=out_specs, check_vma=False)
```

time: 629 us -> 418 us (0.66)
  local copies, waits for them, and re-layouts: 187 us -> 15.6 us
  Pallas kernels: 39.9 us -> 146 us
  starting transfers between devices: 132 us -> 78.6 us
  matrix products: 46.7 us -> 0 us
  other arithmetic: 51.8 us -> 11.8 us
  between operations: 22.4 us -> 1.61 us
  waiting for transfers between devices: 140 us -> 157 us
    pallas_call x0 -> x24, Pallas kernels: none -> 107 us  [call(): pl.pallas_call(kernel, out_shape=list(out), in_specs=[SM] + [VM] * (len(i...]
    dynamic_slice x16 -> x1, local copies, waits for them, and re-layouts: 55.6 us -> 1.21 us  [body(): lax.dynamic_slice_in_dim(jnp.asarray(entries, jnp.int32), device, 1, 0)]
    unnamed x175 -> x190, local copies, waits for them, and re-layouts: 58.1 us -> 10.9 us
    dot_general x19 -> x0, matrix products: 46.7 us -> none  [the longest x4 15.3 us: against_rows(): lax.dot_general(left, right, (((1,), (1,)), ((), ())), preferred_element_...]
    ppermute x85 -> x53, starting transfers between devices: 109 us -> 64.9 us  [ring_shift(): lax.ppermute(value, 'ctx', [(ring[i], ring[(i + step) % count]) for i in...]
    dynamic_update_slice x42 -> x0, local copies, waits for them, and re-layouts: 30.2 us -> none  [the longest x19 25.3 us: stack_sides(): whole = lax.dynamic_update_slice_in_dim(whole, slot[None], side, 0)]
    broadcast_in_dim x17 -> x0, local copies, waits for them, and re-layouts: 23.4 us -> none  [the longest x6 10.7 us: stack_sides(): whole = lax.dynamic_update_slice_in_dim(whole, slot[None], side, 0)]
    dynamic_update_slice x25 -> x0, other arithmetic: 22.2 us -> none  [the longest x20 20.6 us: gather_rows(): lax.dynamic_update_slice(whole, (slots[k].astype(jnp.float32) * factor)[N...]
  transfers between devices with their start and end apart: 121 -> 89, of which waited for: 43 -> 42; matrix products, arithmetic and copies ran while one was open for 46% -> 4% of each run, Pallas kernels for 6% -> 32%
where the time goes in v2:
time: 418 us; the launch traced here: 410 us
  waiting for transfers between devices  157 us (38%)
  Pallas kernels  146 us (35%)
  starting transfers between devices  78.6 us (19%)
  local copies, waits for them, and re-layouts  15.6 us (4%)
  other arithmetic  11.8 us (3%)
    ppermute x53, waiting for transfers between devices, ring_shift(): lax.ppermute(value, 'ctx', [(ring[i], ring[(i + step) % count]) for i in...  121 us
    pallas_call x24, Pallas kernels, call(): pl.pallas_call(kernel, out_shape=list(out), in_specs=[SM] + [VM] * (len(i...  107 us
    ppermute x53, starting transfers between devices, ring_shift(): lax.ppermute(value, 'ctx', [(ring[i], ring[(i + step) % count]) for i in...  64.9 us
    ppermute x10, waiting for transfers between devices, chip_shift(): lax.ppermute(value, 'fsdp', [(i, (i + 2 * step) % count) for i in range(c...  21.6 us
    pallas_call x1, Pallas kernels, attention_backward(): pl.pallas_call(functools.partial(bwd_kernel, meta), out_shape=[jax.ShapeD...  20.1 us
    pallas_call x1, Pallas kernels, attention_forward(): pl.pallas_call(functools.partial(fwd_kernel, meta), out_shape=[jax.ShapeD...  18.9 us
    convert_element_type x14, other arithmetic, low(): return value.astype(jnp.bfloat16)  11.8 us
    unnamed x190, local copies, waits for them, and re-layouts  10.9 us
  transfers between devices with their start and end apart: 89, of which 42 were waited for; matrix products, arithmetic and copies ran while one was open for 4% of the time, Pallas kernels for 32%

profile of v2, /device:TPU:0, one launch (start us, length us, event | category | flops | bytes accessed | tf_op | source)
XLA Modules:
  0.0 410.2 jit_solution(7974401847907283335)
XLA Ops:
  0.6 3.0 collective-permute-start
  11.4 3.9 split.1
  23.9 2.6 project.9
  26.6 2.6 project.10
  29.2 2.6 project.11
  40.2 2.6 project.12
  42.8 2.7 project.13
  45.5 6.0 %collective-permute-done.9.rows_ref = bf16[256,1024]{1,0:T(8,128)(2,1)S(1)} collective-permute-done((bf16[256,1024]{1,0:T(8,128)(2,1)}, bf16[256,1024]{1,0:T(8,128)(2,1)S(1)}, u32[]{:S(2)}, u32[]{:S(2)}) %collective-permute-start.9) | collective-permute-done | bytes 524320 | tf_op jit(solution)/shard_map/ppermute | solution.py:569
  59.1 2.7 project.14
  61.8 2.6 project.15
  65.6 2.5 project.16
  68.1 2.4 project.17
  70.5 18.9 %attention_forward.1 = (bf16[256,128]{1,0:T(8,128)(2,1)}, bf16[256,128]{1,0:T(8,128)(2,1)}, bf16[256,128]{1,0:T(8,128)(2,1)}, bf16[256,128]{1,0:T(8,128)(2,1)}, ...) custom-call(s32[1,12]{1,0:T(1,128)} %constant_dynamic-slice_fusion.t, ...), custom_call_target="tpu_custom_call" | custom-call | bytes 57800000 | tf_op jit(solution)/shard_map/attention_forward/pallas_call | solution.py:196
  98.4 3.7 collective-permute-start.19
  102.1 2.6 collective-permute-done.18.refs_3_
  107.5 4.2 %collective-permute-done.20.refs_5_ = bf16[256,128]{1,0:T(8,128)(2,1)S(1)} collective-permute-done((bf16[256,128]{1,0:T(8,128)(2,1)}, bf16[256,128]{1,0:T(8,128)(2,1)S(1)}, u32[]{:S(2)}, u32[]{:S(2)}) %collective-permute-start.20) | collective-permute-done | bytes 65568 | tf_op jit(solution)/shard_map/ppermute | solution.py:569
  113.3 3.0 collective-permute-done.22.refs_7_
  118.0 4.3 %leave.1 = (f32[256,1024]{1,0:T(8,128)}, bf16[256,1024]{1,0:T(8,128)(2,1)}) custom-call(s32[1,12]{1,0:T(1,128)} %constant_dynamic-slice_fusion.table, bf16[256,1024]{1,0:T(8,128)(2,1)} %tokens_ref.3, bf16[256,128]{1,0:T(8,128)(2,1)} %get-tuple-element.365.refs_0_, bf16[256,128]{1,0:T(8,128)(2,1)} %copy-done.54, bf16[256,128]{1,0:T(8,128)(2,1)} %copy-done.55, ...), custom_call_target="tpu_custom_call" | custom-call | bytes 13939999 | tf_op jit(solution)/shard_map/leave/pallas_call | solution.py:239
  124.6 9.5 %feed_forward.2 = (bf16[256,1024]{1,0:T(8,128)(2,1)}, bf16[256,1024]{1,0:T(8,128)(2,1)}, bf16[256,1024]{1,0:T(8,128)(2,1)}, bf16[256,1024]{1,0:T(8,128)(2,1)}, b...) custom-call(s32[1,12]{1,0:T(1,128)} %constant_dynamic-slice_fusion.table, ...), custom_call_target="tpu_custom_call" | custom-call | bytes 32300000 | tf_op jit(solution)/shard_map/feed_forward/pallas_call | solution.py:239
  134.1 2.9 collective-permute-done.28.refs_0_.refs_2_
  140.6 9.5 %feed_forward.3 = (bf16[256,1024]{1,0:T(8,128)(2,1)}, bf16[256,1024]{1,0:T(8,128)(2,1)}, bf16[256,1024]{1,0:T(8,128)(2,1)}, bf16[256,1024]{1,0:T(8,128)(2,1)}, b...) custom-call(s32[1,12]{1,0:T(1,128)} %constant_dynamic-slice_fusion.table, ...), custom_call_target="tpu_custom_call" | custom-call | bytes 32300000 | tf_op jit(solution)/shard_map/feed_forward/pallas_call | solution.py:239
  153.1 11.0 %feed_forward_weights.1 = (bf16[192,1408]{1,0:T(8,128)(2,1)}, bf16[192,1408]{1,0:T(8,128)(2,1)}, bf16[192,1408]{1,0:T(8,128)(2,1)}, bf16[192,1408]{1,0:T(8,128)(...) custom-call(s32[1,12]{1,0:T(1,128)} %constant_dynamic-slice_fusion.t, ...), custom_call_target="tpu_custom_call" | custom-call | bytes 40800000 | tf_op jit(solution)/shard_map/feed_forward_weights/pallas_call | solution.py:239
  164.1 2.9 collective-permute-done.36.refs_1_
  167.8 5.0 %branch.1 = (f32[256,1024]{1,0:T(8,128)}, bf16[256,1024]{1,0:T(8,128)(2,1)}, bf16[256,128]{1,0:T(8,128)(2,1)}, bf16[256,128]{1,0:T(8,128)(2,1)}, bf16[256,128]{1...) custom-call(s32[1,12]{1,0:T(1,128)} %constant_dynamic-slice_fusion.t, ...), custom_call_target="tpu_custom_call" | custom-call | bytes 17000000 | tf_op jit(solution)/shard_map/branch/pallas_call | solution.py:239
  172.9 3.5 out_weights.1
  182.1 6.2 %collective-permute-done.37 = bf16[96,1408]{1,0:T(8,128)(2,1)S(1)} collective-permute-done((bf16[96,1408]{1,0:T(8,128)(2,1)S(1)}, bf16[96,1408]{1,0:T(8,128)(2,1)S(1)}, u32[]{:S(2)}, u32[]{:S(2)}) %collective-permute-start.37) | collective-permute-done | bytes 270368 | tf_op jit(solution)/shard_map/ppermute | solution.py:569
  191.2 2.5 collective-permute-start.42
  193.7 2.5 collective-permute-done.40.refs_11_
  196.6 3.9 collective-permute-start.44
  209.5 20.1 %attention_backward.1 = (bf16[256,512]{1,0:T(8,128)(2,1)}, bf16[256,512]{1,0:T(8,128)(2,1)}, bf16[256,512]{1,0:T(8,128)(2,1)}, bf16[256,512]{1,0:T(8,128)(2,1)},...) custom-call(s32[1,12]{1,0:T(1,128)} %constant_dynamic-slice_fusion.ta, ...), custom_call_target="tpu_custom_call" | custom-call | bytes 61200000 | tf_op jit(solution)/shard_map/attention_backward/pallas_call | solution.py:208
  231.0 5.9 %qkv_weights.1 = (bf16[256,384]{1,0:T(8,128)(2,1)}, bf16[256,384]{1,0:T(8,128)(2,1)}, bf16[256,384]{1,0:T(8,128)(2,1)}, bf16[256,384]{1,0:T(8,128)(2,1)}) custom-call(s32[1,12]{1,0:T(1,128)} %constant_dynamic-slice_fusion.table, bf16[256,1024]{1,0:T(8,128)(2,1)} %get-tuple-element.470.refs_0_, bf16[256,1024]{1,0:T(8,128)(2,1)} %get-tuple-element.471.refs_1_, ...), custom_call_target="tpu_custom_call" | custom-call | bytes 20400000 | tf_op jit(solution)/shard_map/qkv_weights/pallas_call | solution.py:239
  244.1 8.4 %collective-permute-done.52 = bf16[192,1408]{1,0:T(8,128)(2,1)S(1)} collective-permute-done((bf16[192,1408]{1,0:T(8,128)(2,1)S(1)}, bf16[192,1408]{1,0:T(8,128)(2,1)S(1)}, u32[]{:S(2)}, u32[]{:S(2)}) %collective-permute-start.52) | collective-permute-done | bytes 540704 | tf_op jit(solution)/shard_map/ppermute | solution.py:569
  253.4 4.7 %collective-permute-done.53.refs_7_.refs_5_ = bf16[256,512]{1,0:T(8,128)(2,1)S(1)} collective-permute-done((bf16[256,512]{1,0:T(8,128)(2,1)S(1)}, bf16[256,512]{1,0:T(8,128)(2,1)S(1)}, u32[]{:S(2)}, u32[]{:S(2)}) %collective-permute-start.53) | collective-permute-done | bytes 262176 | tf_op jit(solution)/shard_map/ppermute | solution.py:569
  259.8 17.8 %collective-permute-done.54.refs_8_.refs_6_ = bf16[256,512]{1,0:T(8,128)(2,1)S(1)} collective-permute-done((bf16[256,512]{1,0:T(8,128)(2,1)S(1)}, bf16[256,512]{1,0:T(8,128)(2,1)S(1)}, u32[]{:S(2)}, u32[]{:S(2)}) %collective-permute-start.54) | collective-permute-done | bytes 262176 | tf_op jit(solution)/shard_map/ppermute | solution.py:569
  280.0 4.6 %collective-permute-start.59 = (bf16[192,1408]{1,0:T(8,128)(2,1)S(1)}, bf16[192,1408]{1,0:T(8,128)(2,1)S(1)}, u32[]{:S(2)}, u32[]{:S(2)}) collective-permute-start(bf16[192,1408]{1,0:T(8,128)(2,1)S(1)} %add_convert_fusion), channel_id=1, source_target_pairs={{4,0},{12,4},{20,12},{28,20},{24,28},{16,24},{8,16},{0,8},{5,1},{1... | collective-permute-start | bytes 1622024 | tf_op jit(solution)/shard_map/ppermute | solution.py:569
  284.7 15.7 %collective-permute-done.60.refs_1_ = bf16[256,384]{1,0:T(8,128)(2,1)S(1)} collective-permute-done((bf16[256,384]{1,0:T(8,128)(2,1)S(1)}, bf16[256,384]{1,0:T(8,128)(2,1)S(1)}, u32[]{:S(2)}, u32[]{:S(2)}) %collective-permute-start.60) | collective-permute-done | bytes 196640 | tf_op jit(solution)/shard_map/ppermute | solution.py:644
  301.9 2.6 cut.1
  304.7 10.4 %collective-permute-done.66.refs_3_.refs_1_ = bf16[256,512]{1,0:T(8,128)(2,1)S(1)} collective-permute-done((bf16[256,512]{1,0:T(8,128)(2,1)}, bf16[256,512]{1,0:T(8,128)(2,1)S(1)}, u32[]{:S(2)}, u32[]{:S(2)}) %collective-permute-start.66) | collective-permute-done | bytes 262176 | tf_op jit(solution)/shard_map/ppermute | solution.py:569
  315.4 4.9 %collective-permute-done.64.refs_2_ = bf16[32,1408]{1,0:T(8,128)(2,1)S(1)} collective-permute-done((bf16[32,1408]{1,0:T(8,128)(2,1)}, bf16[32,1408]{1,0:T(8,128)(2,1)S(1)}, u32[]{:S(2)}, u32[]{:S(2)}) %collective-permute-start.64) | collective-permute-done | bytes 90144 | tf_op jit(solution)/shard_map/ppermute | solution.py:674
  323.0 4.9 %collective-permute-start.73 = (bf16[192,1408]{1,0:T(8,128)(2,1)}, bf16[192,1408]{1,0:T(8,128)(2,1)S(1)}, u32[]{:S(2)}, u32[]{:S(2)}) collective-permute-start(bf16[192,1408]{1,0:T(8,128)(2,1)} %pack.1.refs_0_), channel_id=1, source_target_pairs={{4,12},{12,20},{20,28},{28,24},{24,16},{16,8},{8,0},{0,4},{5,13},{... | collective-permute-start | bytes 1622024 | tf_op jit(solution)/shard_map/ppermute | solution.py:569
  327.9 2.5 join.1.refs_0_
  330.4 9.1 %tail.1 = bf16[256,1024]{1,0:T(8,128)(2,1)} custom-call(s32[1,12]{1,0:T(1,128)} %constant_dynamic-slice_fusion.table, bf16[256,1024]{1,0:T(8,128)(2,1)} %tokens_ref.3, f32[256,1024]{1,0:T(8,128)} %get-tuple-element.520.grad_ref, bf16[256,512]{1,0:T(8,128)(2,1)} %get-tuple-element.479.refs_9_.refs_2_.refs_0_, bf16[256,512]{1,0:T(8,128)(2,1)} %copy-done.27, ...), custom_call_target="tpu_custom_call" | custom-call | bytes 27200000 | tf_op jit(solution)/shard_map/tail/pallas_call | solution.py:239
  344.1 11.1 %collective-permute-done.75.refs_7_ = bf16[192,1408]{1,0:T(8,128)(2,1)S(1)} collective-permute-done((bf16[192,1408]{1,0:T(8,128)(2,1)S(1)}, bf16[192,1408]{1,0:T(8,128)(2,1)S(1)}, u32[]{:S(2)}, u32[]{:S(2)}) %collective-permute-start.75) | collective-permute-done | bytes 540704 | tf_op jit(solution)/shard_map/ppermute | solution.py:569
  358.2 6.6 %collective-permute-done.77.refs_8_ = bf16[256,512]{1,0:T(8,128)(2,1)S(1)} collective-permute-done((bf16[256,512]{1,0:T(8,128)(2,1)S(1)}, bf16[256,512]{1,0:T(8,128)(2,1)S(1)}, u32[]{:S(2)}, u32[]{:S(2)}) %collective-permute-start.77) | collective-permute-done | bytes 262176 | tf_op jit(solution)/shard_map/ppermute | solution.py:569
  369.5 9.7 %collective-permute-done.79.refs_7_ = bf16[256,512]{1,0:T(8,128)(2,1)S(1)} collective-permute-done((bf16[256,512]{1,0:T(8,128)(2,1)S(1)}, bf16[256,512]{1,0:T(8,128)(2,1)S(1)}, u32[]{:S(2)}, u32[]{:S(2)}) %collective-permute-start.79) | collective-permute-done | bytes 262176 | tf_op jit(solution)/shard_map/ppermute | solution.py:569
  382.6 6.4 %collective-permute-done.81.refs_6_ = bf16[256,512]{1,0:T(8,128)(2,1)S(1)} collective-permute-done((bf16[256,512]{1,0:T(8,128)(2,1)S(1)}, bf16[256,512]{1,0:T(8,128)(2,1)S(1)}, u32[]{:S(2)}, u32[]{:S(2)}) %collective-permute-start.81) | collective-permute-done | bytes 262176 | tf_op jit(solution)/shard_map/ppermute | solution.py:569
  396.2 8.0 %feed_forward_final.1 = (f32[256,5632]{1,0:T(8,128)}, f32[704,1024]{1,0:T(8,128)}, f32[1,256]{1,0:T(1,128)}) custom-call(s32[1,12]{1,0:T(1,128)} %constant_dynamic-slice_fusion.table, bf16[256,5632]{1,0:T(8,128)(2,1)} %w_ref.7, bf16[1,256]{1,0:T(2,128)(2,1)} %reshape.29.two_ref.gain_ref, bf16[192,1408]{1,0:T(8,128)(2,1)} %pack.1.refs_0_, ...), custom_call_target="tpu_custom_call" | custom-call | bytes 27200000 | tf_op jit(solution)/shard_map/feed_forward_final/pallas_call | solution.py:239
  405.5 4.5 %attention_final.1 = (f32[256,3072]{1,0:T(8,128)}, f32[256,1024]{1,0:T(8,128)}, f32[1,256]{1,0:T(1,128)}) custom-call(s32[1,12]{1,0:T(1,128)} %constant_dynamic-slice_fusion.table, bf16[256,3072]{1,0:T(8,128)(2,1)} %w_ref.6, bf16[1,256]{1,0:T(2,128)(2,1)} %reshape.28.one_ref.gain_ref, bf16[256,512]{1,0:T(8,128)(2,1)} %join.1.refs_0_, ...), custom_call_target="tpu_custom_call" | custom-call | bytes 15639999 | tf_op jit(solution)/shard_map/attention_final/pallas_call | solution.py:239
  (370 shorter events, 117.9 us)
Async XLA Ops:
  0.6 15.2 %collective-permute-start = (bf16[256,1024]{1,0:T(8,128)(2,1)}, bf16[256,1024]{1,0:T(8,128)(2,1)S(1)}, u32[]{:S(2)}, u32[]{:S(2)}) collective-permute-start(bf16[256,1024]{1,0:T(8,128)(2,1)} %tokens_ref.3), channel_id=1, source_target_pairs={{4,12},{12,20},{20,28},{28,24},{24,16},{16,8},{8,0},{0,4},{5,13},{... | collective-permute-start | bytes 1572872 | tf_op jit(solution)/shard_map/ppermute | solution.py:569
  3.7 13.6 %collective-permute-start.1 = (bf16[256,1024]{1,0:T(8,128)(2,1)}, bf16[256,1024]{1,0:T(8,128)(2,1)S(1)}, u32[]{:S(2)}, u32[]{:S(2)}) collective-permute-start(bf16[256,1024]{1,0:T(8,128)(2,1)} %tokens_ref.3), channel_id=1, source_target_pairs={{4,0},{12,4},{20,12},{28,20},{24,28},{16,24},{8,16},{0,8},{5,1},{1... | collective-permute-start | bytes 1572872 | tf_op jit(solution)/shard_map/ppermute | solution.py:569
  18.0 17.5 %collective-permute-start.7 = (bf16[256,1408]{1,0:T(8,128)(2,1)}, bf16[256,1408]{1,0:T(8,128)(2,1)S(1)}, u32[]{:S(2)}, u32[]{:S(2)}) collective-permute-start(bf16[256,1408]{1,0:T(8,128)(2,1)} %get-tuple-element.304), channel_id=1, source_target_pairs={{0,1},{1,0},{2,3},{3,2},{4,5},{5,4},{6,7},{7,6},{8,9},{9,8},{10,11... | collective-permute-start | bytes 2162696 | tf_op jit(solution)/shard_map/ppermute | solution.py:674
  18.0 19.1 %collective-permute-start.8 = (bf16[256,1408]{1,0:T(8,128)(2,1)}, bf16[256,1408]{1,0:T(8,128)(2,1)S(1)}, u32[]{:S(2)}, u32[]{:S(2)}) collective-permute-start(bf16[256,1408]{1,0:T(8,128)(2,1)} %get-tuple-element.305), channel_id=1, source_target_pairs={{0,2},{1,3},{2,0},{3,1},{4,6},{5,7},{6,4},{7,5},{8,10},{9,11},{10,... | collective-permute-start | bytes 2162696 | tf_op jit(solution)/shard_map/ppermute | solution.py:674
  19.8 14.2 %collective-permute-start.3 = (bf16[256,1024]{1,0:T(8,128)(2,1)S(1)}, bf16[256,1024]{1,0:T(8,128)(2,1)}, u32[]{:S(2)}, u32[]{:S(2)}) collective-permute-start(bf16[256,1024]{1,0:T(8,128)(2,1)S(1)} %collective-permute-done.rows_ref), channel_id=1, source_target_pairs={{4,12},{12,20},{20,28},{28,24},{24,16},{16,8},{8,0},{0,4},{5,13},{... | collective-permute-start | bytes 1572872 | tf_op jit(solution)/shard_map/ppermute | solution.py:569
  21.3 14.1 %collective-permute-start.4 = (bf16[256,1024]{1,0:T(8,128)(2,1)}, bf16[256,1024]{1,0:T(8,128)(2,1)}, u32[]{:S(2)}, u32[]{:S(2)}) collective-permute-start(bf16[256,1024]{1,0:T(8,128)(2,1)} %copy-done.46), channel_id=1, source_target_pairs={{4,0},{12,4},{20,12},{28,20},{24,28},{16,24},{8,16},{0,8},{5,1},{1... | collective-permute-start | bytes 1572872 | tf_op jit(solution)/shard_map/ppermute | solution.py:569
  23.3 29.7 %collective-permute-start.11 = (bf16[256,1408]{1,0:T(8,128)(2,1)}, bf16[256,1408]{1,0:T(8,128)(2,1)S(1)}, u32[]{:S(2)}, u32[]{:S(2)}) collective-permute-start(bf16[256,1408]{1,0:T(8,128)(2,1)} %get-tuple-element.315), channel_id=1, source_target_pairs={{0,3},{1,2},{2,1},{3,0},{4,7},{5,6},{6,5},{7,4},{8,11},{9,10},{10,... | collective-permute-start | bytes 2162696 | tf_op jit(solution)/shard_map/ppermute | solution.py:674
  38.1 13.4 %collective-permute-start.9 = (bf16[256,1024]{1,0:T(8,128)(2,1)}, bf16[256,1024]{1,0:T(8,128)(2,1)S(1)}, u32[]{:S(2)}, u32[]{:S(2)}) collective-permute-start(bf16[256,1024]{1,0:T(8,128)(2,1)} %collective-permute-done.3.rows_ref), channel_id=1, source_target_pairs={{4,12},{12,20},{20,28},{28,24},{24,16},{16,8},{8,0},{0,4},{5,13},{... | collective-permute-start | bytes 1572872 | tf_op jit(solution)/shard_map/ppermute | solution.py:569
  39.7 13.2 %collective-permute-start.10 = (bf16[256,1024]{1,0:T(8,128)(2,1)}, bf16[256,1024]{1,0:T(8,128)(2,1)}, u32[]{:S(2)}, u32[]{:S(2)}) collective-permute-start(bf16[256,1024]{1,0:T(8,128)(2,1)} %collective-permute-done.4.rows_ref), channel_id=1, source_target_pairs={{4,0},{12,4},{20,12},{28,20},{24,28},{16,24},{8,16},{0,8},{5,1},{1... | collective-permute-start | bytes 1572872 | tf_op jit(solution)/shard_map/ppermute | solution.py:569
  53.9 35.5 %collective-permute-start.14 = (bf16[128,3072]{1,0:T(8,128)(2,1)S(1)}, bf16[128,3072]{1,0:T(8,128)(2,1)}, u32[]{:S(2)}, u32[]{:S(2)}) collective-permute-start(bf16[128,3072]{1,0:T(8,128)(2,1)S(1)} %get-tuple-element.521.refs_8_), channel_id=1, source_target_pairs={{0,2},{1,3},{2,0},{3,1},{4,6},{5,7},{6,4},{7,5},{8,10},{9,11},{10,... | collective-permute-start | bytes 2359304 | tf_op jit(solution)/shard_map/ppermute | solution.py:644
  55.5 33.9 %collective-permute-start.15 = (bf16[256,1024]{1,0:T(8,128)(2,1)}, bf16[256,1024]{1,0:T(8,128)(2,1)}, u32[]{:S(2)}, u32[]{:S(2)}) collective-permute-start(bf16[256,1024]{1,0:T(8,128)(2,1)} %refs_2_.1), channel_id=1, source_target_pairs={{0,2},{1,3},{2,0},{3,1},{4,6},{5,7},{6,4},{7,5},{8,10},{9,11},{10,... | collective-permute-start | bytes 1572872 | tf_op jit(solution)/shard_map/ppermute | solution.py:644
  89.4 26.9 %collective-permute-start.23 = (bf16[256,1024]{1,0:T(8,128)(2,1)}, bf16[256,1024]{1,0:T(8,128)(2,1)S(1)}, u32[]{:S(2)}, u32[]{:S(2)}) collective-permute-start(bf16[256,1024]{1,0:T(8,128)(2,1)} %refs_2_.1), channel_id=1, source_target_pairs={{0,1},{1,0},{2,3},{3,2},{4,5},{5,4},{6,7},{7,6},{8,9},{9,8},{10,11... | collective-permute-start | bytes 1572872 | tf_op jit(solution)/shard_map/ppermute | solution.py:640
  89.5 27.7 %collective-permute-start.24 = (bf16[256,1024]{1,0:T(8,128)(2,1)}, bf16[256,1024]{1,0:T(8,128)(2,1)S(1)}, u32[]{:S(2)}, u32[]{:S(2)}) collective-permute-start(bf16[256,1024]{1,0:T(8,128)(2,1)} %collective-permute-done.15.refs_10_.refs_4_), channel_id=1, source_target_pairs={{0,1},{1,0},{2,3},{3,2},{4,5},{5,4},{6,7},{7,6},{8,9},{9,8},{10,11... | collective-permute-start | bytes 1572872 | tf_op jit(solution)/shard_map/ppermute | solution.py:640
  90.0 28.0 %collective-permute-start.25 = (bf16[256,1024]{1,0:T(8,128)(2,1)S(1)}, bf16[256,1024]{1,0:T(8,128)(2,1)S(1)}, u32[]{:S(2)}, u32[]{:S(2)}) collective-permute-start(bf16[256,1024]{1,0:T(8,128)(2,1)S(1)} %copy-done.5), channel_id=1, source_target_pairs={{0,2},{1,3},{2,0},{3,1},{4,6},{5,7},{6,4},{7,5},{8,10},{9,11},{10,... | collective-permute-start | bytes 1572872 | tf_op jit(solution)/shard_map/ppermute | solution.py:644
  122.3 14.6 %collective-permute-start.28 = (bf16[256,1024]{1,0:T(8,128)(2,1)}, bf16[256,1024]{1,0:T(8,128)(2,1)}, u32[]{:S(2)}, u32[]{:S(2)}) collective-permute-start(bf16[256,1024]{1,0:T(8,128)(2,1)} %get-tuple-element.378.refs_0_), channel_id=1, source_target_pairs={{0,2},{1,3},{2,0},{3,1},{4,6},{5,7},{6,4},{7,5},{8,10},{9,11},{10,... | collective-permute-start | bytes 1572872 | tf_op jit(solution)/shard_map/ppermute | solution.py:644
  122.4 15.1 %collective-permute-start.31 = (bf16[256,1024]{1,0:T(8,128)(2,1)S(1)}, bf16[256,1024]{1,0:T(8,128)(2,1)}, u32[]{:S(2)}, u32[]{:S(2)}) collective-permute-start(bf16[256,1024]{1,0:T(8,128)(2,1)S(1)} %collective-permute-done.25.refs_2_.refs_6_), channel_id=1, source_target_pairs={{0,1},{1,0},{2,3},{3,2},{4,5},{5,4},{6,7},{7,6},{8,9},{9,8},{10,11... | collective-permute-start | bytes 1572872 | tf_op jit(solution)/shard_map/ppermute | solution.py:640
  137.0 13.3 %collective-permute-start.34 = (bf16[256,1024]{1,0:T(8,128)(2,1)}, bf16[256,1024]{1,0:T(8,128)(2,1)}, u32[]{:S(2)}, u32[]{:S(2)}) collective-permute-start(bf16[256,1024]{1,0:T(8,128)(2,1)} %get-tuple-element.397), channel_id=1, source_target_pairs={{0,1},{1,0},{2,3},{3,2},{4,5},{5,4},{6,7},{7,6},{8,9},{9,8},{10,11... | collective-permute-start | bytes 1572872 | tf_op jit(solution)/shard_map/ppermute | solution.py:640
  152.8 14.3 %collective-permute-start.36 = (bf16[256,1024]{1,0:T(8,128)(2,1)S(1)}, bf16[256,1024]{1,0:T(8,128)(2,1)S(1)}, u32[]{:S(2)}, u32[]{:S(2)}) collective-permute-start(bf16[256,1024]{1,0:T(8,128)(2,1)S(1)} %add_convert_fusion.9), channel_id=1, source_target_pairs={{0,2},{1,3},{2,0},{3,1},{4,6},{5,7},{6,4},{7,5},{8,10},{9,11},{10,... | collective-permute-start | bytes 1572872 | tf_op jit(solution)/shard_map/ppermute | solution.py:644
  176.4 20.2 %collective-permute-start.46 = (bf16[8,256,128]{2,1,0:T(8,128)(2,1)}, bf16[8,256,128]{2,1,0:T(8,128)(2,1)S(1)}, u32[]{:S(2)}, u32[]{:S(2)}) collective-permute-start(bf16[8,256,128]{2,1,0:T(8,128)(2,1)} %get-tuple-element.435), channel_id=1, source_target_pairs={{0,1},{1,0},{2,3},{3,2},{4,5},{5,4},{6,7},{7,6},{8,9},{9,8},{10,11... | collective-permute-start | bytes 1572872 | tf_op jit(solution)/shard_map/ppermute | solution.py:640
  179.7 20.9 %collective-permute-start.48 = (bf16[8,256,128]{2,1,0:T(8,128)(2,1)S(1)}, bf16[8,256,128]{2,1,0:T(8,128)(2,1)S(1)}, u32[]{:S(2)}, u32[]{:S(2)}) collective-permute-start(bf16[8,256,128]{2,1,0:T(8,128)(2,1)S(1)} %add_convert_fusion.7), channel_id=1, source_target_pairs={{0,2},{1,3},{2,0},{3,1},{4,6},{5,7},{6,4},{7,5},{8,10},{9,11},{10,... | collective-permute-start | bytes 1572872 | tf_op jit(solution)/shard_map/ppermute | solution.py:644
  206.5 23.1 %collective-permute-start.49 = (bf16[192,1408]{1,0:T(8,128)(2,1)}, bf16[192,1408]{1,0:T(8,128)(2,1)S(1)}, u32[]{:S(2)}, u32[]{:S(2)}) collective-permute-start(bf16[192,1408]{1,0:T(8,128)(2,1)} %add_convert_fusion.5), channel_id=1, source_target_pairs={{4,12},{12,20},{20,28},{28,24},{24,16},{16,8},{8,0},{0,4},{5,13},{... | collective-permute-start | bytes 1622024 | tf_op jit(solution)/shard_map/ppermute | solution.py:569
  207.5 22.1 %collective-permute-start.50 = (bf16[192,1408]{1,0:T(8,128)(2,1)}, bf16[192,1408]{1,0:T(8,128)(2,1)S(1)}, u32[]{:S(2)}, u32[]{:S(2)}) collective-permute-start(bf16[192,1408]{1,0:T(8,128)(2,1)} %add_convert_fusion.4), channel_id=1, source_target_pairs={{4,0},{12,4},{20,12},{28,20},{24,28},{16,24},{8,16},{0,8},{5,1},{1... | collective-permute-start | bytes 1622024 | tf_op jit(solution)/shard_map/ppermute | solution.py:569
  237.8 14.7 %collective-permute-start.52 = (bf16[192,1408]{1,0:T(8,128)(2,1)S(1)}, bf16[192,1408]{1,0:T(8,128)(2,1)S(1)}, u32[]{:S(2)}, u32[]{:S(2)}) collective-permute-start(bf16[192,1408]{1,0:T(8,128)(2,1)S(1)} %add_convert_fusion.2), channel_id=1, source_target_pairs={{4,0},{12,4},{20,12},{28,20},{24,28},{16,24},{8,16},{0,8},{5,1},{1... | collective-permute-start | bytes 1622024 | tf_op jit(solution)/shard_map/ppermute | solution.py:569
  239.8 38.4 %collective-permute-start.68 = (bf16[128,3072]{1,0:T(8,128)(2,1)S(1)}, bf16[128,3072]{1,0:T(8,128)(2,1)S(1)}, u32[]{:S(2)}, u32[]{:S(2)}) collective-permute-start(bf16[128,3072]{1,0:T(8,128)(2,1)S(1)} %get-tuple-element.521.refs_8_), channel_id=1, source_target_pairs={{0,1},{1,0},{2,3},{3,2},{4,5},{5,4},{6,7},{7,6},{8,9},{9,8},{10,11... | collective-permute-start | bytes 2359304 | tf_op jit(solution)/shard_map/ppermute | solution.py:640
  239.8 18.3 %collective-permute-start.53 = (bf16[256,512]{1,0:T(8,128)(2,1)S(1)}, bf16[256,512]{1,0:T(8,128)(2,1)S(1)}, u32[]{:S(2)}, u32[]{:S(2)}) collective-permute-start(bf16[256,512]{1,0:T(8,128)(2,1)S(1)} %copy-done.67), channel_id=1, source_target_pairs={{4,28},{12,24},{20,16},{28,8},{24,0},{16,4},{8,12},{0,20},{5,29},{... | collective-permute-start | bytes 786440 | tf_op jit(solution)/shard_map/ppermute | solution.py:569
  240.9 36.7 %collective-permute-start.54 = (bf16[256,512]{1,0:T(8,128)(2,1)S(1)}, bf16[256,512]{1,0:T(8,128)(2,1)S(1)}, u32[]{:S(2)}, u32[]{:S(2)}) collective-permute-start(bf16[256,512]{1,0:T(8,128)(2,1)S(1)} %copy-done.66), channel_id=1, source_target_pairs={{4,20},{12,28},{20,24},{28,16},{24,8},{16,0},{8,4},{0,12},{5,21},{... | collective-permute-start | bytes 786440 | tf_op jit(solution)/shard_map/ppermute | solution.py:569
  242.3 35.7 %collective-permute-start.55 = (bf16[256,512]{1,0:T(8,128)(2,1)S(1)}, bf16[256,512]{1,0:T(8,128)(2,1)S(1)}, u32[]{:S(2)}, u32[]{:S(2)}) collective-permute-start(bf16[256,512]{1,0:T(8,128)(2,1)S(1)} %copy-done.65), channel_id=1, source_target_pairs={{4,12},{12,20},{20,28},{28,24},{24,16},{16,8},{8,0},{0,4},{5,13},{... | collective-permute-start | bytes 786440 | tf_op jit(solution)/shard_map/ppermute | solution.py:569
  252.4 27.6 %collective-permute-start.61 = (bf16[256,512]{1,0:T(8,128)(2,1)S(1)}, bf16[256,512]{1,0:T(8,128)(2,1)S(1)}, u32[]{:S(2)}, u32[]{:S(2)}) collective-permute-start(bf16[256,512]{1,0:T(8,128)(2,1)S(1)} %copy-done.62), channel_id=1, source_target_pairs={{4,16},{12,8},{20,0},{28,4},{24,12},{16,20},{8,28},{0,24},{5,17},{... | collective-permute-start | bytes 786440 | tf_op jit(solution)/shard_map/ppermute | solution.py:569
  258.1 26.6 %collective-permute-start.62 = (bf16[256,512]{1,0:T(8,128)(2,1)S(1)}, bf16[256,512]{1,0:T(8,128)(2,1)S(1)}, u32[]{:S(2)}, u32[]{:S(2)}) collective-permute-start(bf16[256,512]{1,0:T(8,128)(2,1)S(1)} %copy-done.61), channel_id=1, source_target_pairs={{4,24},{12,16},{20,8},{28,0},{24,4},{16,12},{8,20},{0,28},{5,25},{... | collective-permute-start | bytes 786440 | tf_op jit(solution)/shard_map/ppermute | solution.py:569
  277.5 22.9 %collective-permute-start.70 = (bf16[128,3072]{1,0:T(8,128)(2,1)S(1)}, bf16[128,3072]{1,0:T(8,128)(2,1)}, u32[]{:S(2)}, u32[]{:S(2)}) collective-permute-start(bf16[128,3072]{1,0:T(8,128)(2,1)S(1)} %get-tuple-element.522.refs_9_), channel_id=1, source_target_pairs={{0,2},{1,3},{2,0},{3,1},{4,6},{5,7},{6,4},{7,5},{8,10},{9,11},{10,... | collective-permute-start | bytes 2359304 | tf_op jit(solution)/shard_map/ppermute | solution.py:644
  278.1 22.8 %collective-permute-start.58 = (bf16[192,1408]{1,0:T(8,128)(2,1)S(1)}, bf16[192,1408]{1,0:T(8,128)(2,1)S(1)}, u32[]{:S(2)}, u32[]{:S(2)}) collective-permute-start(bf16[192,1408]{1,0:T(8,128)(2,1)S(1)} %add_convert_fusion.1), channel_id=1, source_target_pairs={{4,12},{12,20},{20,28},{28,24},{24,16},{16,8},{8,0},{0,4},{5,13},{... | collective-permute-start | bytes 1622024 | tf_op jit(solution)/shard_map/ppermute | solution.py:569
  278.2 22.2 %collective-permute-start.60 = (bf16[256,384]{1,0:T(8,128)(2,1)S(1)}, bf16[256,384]{1,0:T(8,128)(2,1)S(1)}, u32[]{:S(2)}, u32[]{:S(2)}) collective-permute-start(bf16[256,384]{1,0:T(8,128)(2,1)S(1)} %add_convert_fusion.14), channel_id=1, source_target_pairs={{0,2},{1,3},{2,0},{3,1},{4,6},{5,7},{6,4},{7,5},{8,10},{9,11},{10,... | collective-permute-start | bytes 589832 | tf_op jit(solution)/shard_map/ppermute | solution.py:644
  280.0 20.9 %collective-permute-start.59 = (bf16[192,1408]{1,0:T(8,128)(2,1)S(1)}, bf16[192,1408]{1,0:T(8,128)(2,1)S(1)}, u32[]{:S(2)}, u32[]{:S(2)}) collective-permute-start(bf16[192,1408]{1,0:T(8,128)(2,1)S(1)} %add_convert_fusion), channel_id=1, source_target_pairs={{4,0},{12,4},{20,12},{28,20},{24,28},{16,24},{8,16},{0,8},{5,1},{1... | collective-permute-start | bytes 1622024 | tf_op jit(solution)/shard_map/ppermute | solution.py:569
  284.7 19.8 %collective-permute-start.71 = (bf16[128,3072]{1,0:T(8,128)(2,1)}, bf16[128,3072]{1,0:T(8,128)(2,1)S(1)}, u32[]{:S(2)}, u32[]{:S(2)}) collective-permute-start(bf16[128,3072]{1,0:T(8,128)(2,1)} %collective-permute-done.14.refs_12_), channel_id=1, source_target_pairs={{0,1},{1,0},{2,3},{3,2},{4,5},{5,4},{6,7},{7,6},{8,9},{9,8},{10,11... | collective-permute-start | bytes 2359304 | tf_op jit(solution)/shard_map/ppermute | solution.py:640
  300.4 15.0 %collective-permute-start.69 = (bf16[128,3072]{1,0:T(8,128)(2,1)S(1)}, bf16[128,3072]{1,0:T(8,128)(2,1)}, u32[]{:S(2)}, u32[]{:S(2)}) collective-permute-start(bf16[128,3072]{1,0:T(8,128)(2,1)S(1)} %get-tuple-element.522.refs_9_), channel_id=1, source_target_pairs={{0,1},{1,0},{2,3},{3,2},{4,5},{5,4},{6,7},{7,6},{8,9},{9,8},{10,11... | collective-permute-start | bytes 2359304 | tf_op jit(solution)/shard_map/ppermute | solution.py:640
  300.4 19.8 %collective-permute-start.72 = (bf16[128,3072]{1,0:T(8,128)(2,1)}, bf16[128,3072]{1,0:T(8,128)(2,1)}, u32[]{:S(2)}, u32[]{:S(2)}) collective-permute-start(bf16[128,3072]{1,0:T(8,128)(2,1)} %collective-permute-done.70.refs_13_), channel_id=1, source_target_pairs={{0,1},{1,0},{2,3},{3,2},{4,5},{5,4},{6,7},{7,6},{8,9},{9,8},{10,11... | collective-permute-start | bytes 2359304 | tf_op jit(solution)/shard_map/ppermute | solution.py:640
  300.9 14.1 %collective-permute-start.66 = (bf16[256,512]{1,0:T(8,128)(2,1)}, bf16[256,512]{1,0:T(8,128)(2,1)S(1)}, u32[]{:S(2)}, u32[]{:S(2)}) collective-permute-start(bf16[256,512]{1,0:T(8,128)(2,1)} %get-tuple-element.483.refs_16_), channel_id=1, source_target_pairs={{4,0},{12,4},{20,12},{28,20},{24,28},{16,24},{8,16},{0,8},{5,1},{1... | collective-permute-start | bytes 786440 | tf_op jit(solution)/shard_map/ppermute | solution.py:569
  301.8 13.2 %collective-permute-start.67 = (bf16[256,512]{1,0:T(8,128)(2,1)}, bf16[256,512]{1,0:T(8,128)(2,1)S(1)}, u32[]{:S(2)}, u32[]{:S(2)}) collective-permute-start(bf16[256,512]{1,0:T(8,128)(2,1)} %get-tuple-element.482.refs_15_), channel_id=1, source_target_pairs={{4,8},{12,0},{20,4},{28,12},{24,20},{16,28},{8,24},{0,16},{5,9},{1... | collective-permute-start | bytes 786440 | tf_op jit(solution)/shard_map/ppermute | solution.py:569
  323.0 17.0 %collective-permute-start.73 = (bf16[192,1408]{1,0:T(8,128)(2,1)}, bf16[192,1408]{1,0:T(8,128)(2,1)S(1)}, u32[]{:S(2)}, u32[]{:S(2)}) collective-permute-start(bf16[192,1408]{1,0:T(8,128)(2,1)} %pack.1.refs_0_), channel_id=1, source_target_pairs={{4,12},{12,20},{20,28},{28,24},{24,16},{16,8},{8,0},{0,4},{5,13},{... | collective-permute-start | bytes 1622024 | tf_op jit(solution)/shard_map/ppermute | solution.py:569
  327.9 14.2 %collective-permute-start.74 = (bf16[192,1408]{1,0:T(8,128)(2,1)}, bf16[192,1408]{1,0:T(8,128)(2,1)S(1)}, u32[]{:S(2)}, u32[]{:S(2)}) collective-permute-start(bf16[192,1408]{1,0:T(8,128)(2,1)} %pack.1.refs_0_), channel_id=1, source_target_pairs={{4,0},{12,4},{20,12},{28,20},{24,28},{16,24},{8,16},{0,8},{5,1},{1... | collective-permute-start | bytes 1622024 | tf_op jit(solution)/shard_map/ppermute | solution.py:569
  342.1 13.1 %collective-permute-start.75 = (bf16[192,1408]{1,0:T(8,128)(2,1)S(1)}, bf16[192,1408]{1,0:T(8,128)(2,1)S(1)}, u32[]{:S(2)}, u32[]{:S(2)}) collective-permute-start(bf16[192,1408]{1,0:T(8,128)(2,1)S(1)} %collective-permute-done.73.refs_8_), channel_id=1, source_target_pairs={{4,12},{12,20},{20,28},{28,24},{24,16},{16,8},{8,0},{0,4},{5,13},{... | collective-permute-start | bytes 1622024 | tf_op jit(solution)/shard_map/ppermute | solution.py:569
  342.4 13.2 %collective-permute-start.76 = (bf16[192,1408]{1,0:T(8,128)(2,1)S(1)}, bf16[192,1408]{1,0:T(8,128)(2,1)S(1)}, u32[]{:S(2)}, u32[]{:S(2)}) collective-permute-start(bf16[192,1408]{1,0:T(8,128)(2,1)S(1)} %collective-permute-done.74.refs_1_), channel_id=1, source_target_pairs={{4,0},{12,4},{20,12},{28,20},{24,28},{16,24},{8,16},{0,8},{5,1},{1... | collective-permute-start | bytes 1622024 | tf_op jit(solution)/shard_map/ppermute | solution.py:569
  344.1 22.8 %collective-permute-start.32 = (bf16[256,1024]{1,0:T(8,128)(2,1)}, bf16[256,1024]{1,0:T(8,128)(2,1)S(1)}, u32[]{:S(2)}, u32[]{:S(2)}) collective-permute-start(bf16[256,1024]{1,0:T(8,128)(2,1)} %get-tuple-element.393), channel_id=1, source_target_pairs={{0,1},{1,0},{2,3},{3,2},{4,5},{5,4},{6,7},{7,6},{8,9},{9,8},{10,11... | collective-permute-start | bytes 1572872 | tf_op jit(solution)/shard_map/ppermute | solution.py:640
  357.6 22.8 %collective-permute-start.85 = (bf16[192,1408]{1,0:T(8,128)(2,1)S(1)}, bf16[192,1408]{1,0:T(8,128)(2,1)S(1)}, u32[]{:S(2)}, u32[]{:S(2)}) collective-permute-start(bf16[192,1408]{1,0:T(8,128)(2,1)S(1)} %collective-permute-done.75.refs_7_), channel_id=1, source_target_pairs={{4,12},{12,20},{20,28},{28,24},{24,16},{16,8},{8,0},{0,4},{5,13},{... | collective-permute-start | bytes 1622024 | tf_op jit(solution)/shard_map/ppermute | solution.py:569
  358.2 32.9 %collective-permute-start.29 = (bf16[256,1024]{1,0:T(8,128)(2,1)}, bf16[256,1024]{1,0:T(8,128)(2,1)S(1)}, u32[]{:S(2)}, u32[]{:S(2)}) collective-permute-start(bf16[256,1024]{1,0:T(8,128)(2,1)} %get-tuple-element.389), channel_id=1, source_target_pairs={{0,1},{1,0},{2,3},{3,2},{4,5},{5,4},{6,7},{7,6},{8,9},{9,8},{10,11... | collective-permute-start | bytes 1572872 | tf_op jit(solution)/shard_map/ppermute | solution.py:640
  364.9 17.0 %collective-permute-start.86 = (bf16[192,1408]{1,0:T(8,128)(2,1)S(1)}, bf16[192,1408]{1,0:T(8,128)(2,1)S(1)}, u32[]{:S(2)}, u32[]{:S(2)}) collective-permute-start(bf16[192,1408]{1,0:T(8,128)(2,1)S(1)} %collective-permute-done.76.refs_2_), channel_id=1, source_target_pairs={{4,0},{12,4},{20,12},{28,20},{24,28},{16,24},{8,16},{0,8},{5,1},{1... | collective-permute-start | bytes 1622024 | tf_op jit(solution)/shard_map/ppermute | solution.py:569
  379.2 13.2 %collective-permute-start.33 = (bf16[256,1024]{1,0:T(8,128)(2,1)S(1)}, bf16[256,1024]{1,0:T(8,128)(2,1)S(1)}, u32[]{:S(2)}, u32[]{:S(2)}) collective-permute-start(bf16[256,1024]{1,0:T(8,128)(2,1)S(1)} %add_convert_fusion.12), channel_id=1, source_target_pairs={{0,2},{1,3},{2,0},{3,1},{4,6},{5,7},{6,4},{7,5},{8,10},{9,11},{10,... | collective-permute-start | bytes 1572872 | tf_op jit(solution)/shard_map/ppermute | solution.py:644
  390.1 14.1 %collective-permute-start.83 = (bf16[128,512]{1,0:T(8,128)(2,1)S(1)}, bf16[128,512]{1,0:T(8,128)(2,1)S(1)}, u32[]{:S(2)}, u32[]{:S(2)}) collective-permute-start(bf16[128,512]{1,0:T(8,128)(2,1)S(1)} %slice.29), channel_id=1, source_target_pairs={{4,12},{12,20},{20,28},{28,24},{24,16},{16,8},{8,0},{0,4},{5,13},{... | collective-permute-start | bytes 393224 | tf_op jit(solution)/shard_map/ppermute | solution.py:569
  (136 other events, 1835.7 us)

commit v3 on v2

--- a/solution.py
+++ b/solution.py
@@ -10,6 +10,8 @@
 
 HEADS = 16
 TILE = 256
+VMEM_FWD = 24 << 20
+VMEM_BWD = 32 << 20
 
 
 EPS = 1e-05
@@ -56,6 +58,12 @@
             position = order_ref[0, table[0, number // per] * per + number % per] * block
             yield slot, pl.ds(row, block), pl.ds(pl.multiple_of(position, block), block)
             number += 1
+
+def stored(owners, block, order_ref, per):
+    for owner in range(owners):
+        for b in range(per):
+            position = order_ref[0, owner * per + b] * block
+            yield owner, pl.ds(b * block, block), pl.ds(pl.multiple_of(position, block), block)
 
 def fwd_kernel(meta, table, lengths_ref, order_ref, *refs):
     given, n, heads, depth, tile, block = meta
@@ -110,15 +118,13 @@
 def bwd_kernel(meta, table, lengths_ref, order_ref, *refs):
     given, n, heads, depth, tile, block = meta
     qkv_refs, grad_refs = refs[:given], refs[given:given+n]
-    part_out_ref = refs[given+n]
-    refs = refs[given-n:]
-    out_t_ref, lse_ref = refs[2*n+1], refs[2*n+2]
-    dqkv_refs = refs[2*n+3:3*n+3]
+    refs = refs[n:]
+    part_out_ref, out_t_ref, lse_ref, dqkv_ref = refs[given:given+4]
     ends = ends_of(lengths_ref)
-    q_ref, k_ref, v_ref, g_ref, k_t_ref, delta_ref, dq_t_ref, dq_ref, dk_ref, dv_ref = refs[3*n+3:]
+    q_ref, k_ref, v_ref, g_ref, k_t_ref, delta_ref, dq_t_ref, dq_ref, dk_ref, dv_ref = refs[given+4:]
     width = heads*depth
     scale = depth ** (-0.5)
-    per = dqkv_refs[0].shape[0] // block
+    per = dqkv_ref.shape[1] // block
     total = k_ref.shape[0]
     for slot, src, dst in placed(qkv_refs, block, table, order_ref, per):
         q = slot[src, 0:width].astype(jnp.float32)*scale
@@ -177,15 +183,16 @@
         dq_ref[rows, :] = (jnp.transpose(dq_t_ref[:, rows])*scale).astype(jnp.bfloat16)
         return 0
     lax.fori_loop(0, tiles, finish, 0)
-    for slot, dst, src in placed(dqkv_refs, block, table, order_ref, per):
-        slot[dst, 0:width] = dq_ref[src, :]
-        slot[dst, width:2*width] = dk_ref[src, :].astype(jnp.bfloat16)
-        slot[dst, 2*width:3*width] = dv_ref[src, :].astype(jnp.bfloat16)
+    for owner, dst, src in stored(n, block, order_ref, per):
+        dqkv_ref[owner, dst, 0:width] = dq_ref[src, :]
+        dqkv_ref[owner, dst, width:2*width] = dk_ref[src, :].astype(jnp.bfloat16)
+        dqkv_ref[owner, dst, 2*width:3*width] = dv_ref[src, :].astype(jnp.bfloat16)
     shard = part_out_ref.shape[1]
-    for k in range(n):
-        dqkv_refs[k][0:shard, 3*width:] = part_out_ref[k]
-        if shard < dqkv_refs[k].shape[0]:
-            dqkv_refs[k][shard:, 3*width:] = jnp.zeros((dqkv_refs[k].shape[0]-shard, width), jnp.bfloat16)
+    rows = dqkv_ref.shape[1]
+    for owner in range(n):
+        dqkv_ref[owner, 0:shard, 3*width:] = part_out_ref[owner]
+        if shard < rows:
+            dqkv_ref[owner, shard:, 3*width:] = jnp.zeros((rows-shard, width), jnp.bfloat16)
 
 SM=pl.BlockSpec(memory_space=pltpu.SMEM)
 VM=pl.BlockSpec(memory_space=pltpu.VMEM)
@@ -198,6 +205,7 @@
         in_specs=[SM,SM,SM]+[VM]*len(qkv), out_specs=[VM]*(n+2),
         scratch_shapes=[pltpu.VMEM((heads,total,width),jnp.bfloat16)]+[pltpu.VMEM((total,width),jnp.bfloat16)]*3,
         cost_estimate=cost(17),
+        compiler_params=pltpu.CompilerParams(vmem_limit_bytes=VMEM_FWD),
         name="attention_forward")(table,lengths,order,*qkv)
     return list(res[:n]),res[n],res[n+1]
 def attention_backward(table, lengths, order, qkv, grads, part_out, out_t, lse, heads, depth, tile):
@@ -205,13 +213,14 @@
     block=total//order.shape[1]
     meta=(len(qkv),n,heads,depth,tile,block)
     f32=jnp.float32; b16=jnp.bfloat16
-    return list(pl.pallas_call(functools.partial(bwd_kernel,meta),
-        out_shape=[jax.ShapeDtypeStruct((rows,4*width),b16)]*n,
-        in_specs=[SM,SM,SM]+[VM]*(len(qkv)+n+3), out_specs=[VM]*n,
+    return pl.pallas_call(functools.partial(bwd_kernel,meta),
+        out_shape=jax.ShapeDtypeStruct((n,rows,4*width),b16),
+        in_specs=[SM,SM,SM]+[VM]*(len(qkv)+n+3), out_specs=VM,
         scratch_shapes=[pltpu.VMEM((heads,total,width),b16),pltpu.VMEM((total,width),b16),pltpu.VMEM((total,width),b16),pltpu.VMEM((heads,total,width),b16),
           pltpu.VMEM((width,total),b16),pltpu.VMEM((heads,total),f32),pltpu.VMEM((width,total),f32),pltpu.VMEM((total,width),b16),pltpu.VMEM((total,width),f32),pltpu.VMEM((total,width),f32)],
         cost_estimate=cost(18),
-        name="attention_backward")(table,lengths,order,*qkv,*grads,part_out,out_t,lse))
+        compiler_params=pltpu.CompilerParams(vmem_limit_bytes=VMEM_BWD),
+        name="attention_backward")(table,lengths,order,*qkv,*grads,part_out,out_t,lse)
 
 
 def tn(left, right):
@@ -234,7 +243,16 @@
     return pl.CostEstimate(flops=0, bytes_accessed=int(microseconds * 3.4e6), transcendentals=0)
 
 
-def call(name, kernel, out, inputs, scratch=(), time=2.0):
+def room(arrays, extra):
+    total = 0
+    for array in arrays:
+        dims = [1, 1] + list(array.shape)
+        rows, lanes = -(-dims[-2] // 16) * 16, -(-dims[-1] // 128) * 128
+        total += math.prod(dims[:-2]) * rows * lanes * jnp.dtype(array.dtype).itemsize
+    return pltpu.CompilerParams(vmem_limit_bytes=min(60 << 20, total + (extra << 20)))
+
+
+def call(name, kernel, out, inputs, scratch=(), time=2.0, extra=8):
     return list(
         pl.pallas_call(
             kernel,
@@ -243,6 +261,7 @@
             out_specs=[VM] * len(out),
             scratch_shapes=list(scratch),
             cost_estimate=cost(time),
+            compiler_params=room(list(inputs[1:]) + list(out) + list(scratch), extra),
             name=name,
         )(*inputs)
     )
@@ -309,7 +328,7 @@
 
 def leave_kernel(n, count, table, tokens_ref, *refs):
     parts, outs, slices = refs[:n], refs[n : n + count], refs[n + count : n + 2 * count]
-    resid_ref, ffn_ref, gain_ref, weight_ref, sum_ref = refs[n + 2 * count :]
+    resid_ref, ffn_ref, gain_ref, weight_ref = refs[n + 2 * count :]
     own_width = parts[0].shape[1]
     full_gain(table, n, slices, 1, gain_ref)
     stage_rows(table, n, outs, weight_ref)
@@ -391,7 +410,7 @@
     terms, outs, slices = refs[:got], refs[got : got + count], refs[got + count : got + 2 * count]
     rest = refs[got + 2 * count :]
     grad_ref, branch_ref, parts = rest[0], rest[1], rest[2 : 2 + n]
-    gain_ref, weight_ref, scratch_ref = rest[2 + n :]
+    gain_ref, weight_ref = rest[2 + n :]
     own_width = parts[0].shape[1]
     full_gain(table, n, slices, 1, gain_ref)
     stage_rows(table, n, outs, weight_ref)
@@ -419,45 +438,35 @@
     for k in range(n):
         whole_ref[at(table[0, k] * own_width, own_width), :] = low(tn(parts[k][...], branch))
     for slot in range(count):
-        lines = at(table[0, n + slot] * shard, shard)
-        for k in range(n):
-            if own_width % 128 == 0:
-                outs[slot][k] = whole_ref[lines, at(table[0, k] * own_width, own_width)]
-            else:
-                outs[slot][k] = whole_ref[lines, k * own_width : (k + 1) * own_width]
+        lines = whole_ref[at(table[0, n + slot] * shard, shard), :]
+        for owner in range(n):
+            outs[slot][owner] = lines[:, owner * own_width : (owner + 1) * own_width]
 
 
 def qkv_weight_kernel(given, n, count, table, *refs):
-    attn, grads, outs = refs[:given], refs[given : given + n], refs[given + n :]
+    attn, grads_ref, outs = refs[:given], refs[given], refs[given + 1 :]
     shard = outs[0].shape[0]
-    grad_all = jnp.concatenate([r[:, 0 : outs[0].shape[1]] for r in grads], axis=0)
+    used = outs[0].shape[1]
+    grad_all = jnp.concatenate([grads_ref[table[0, k], :, 0:used] for k in range(n)], axis=0)
     for slot in range(count):
         lanes = at(table[0, n + slot] * shard, shard)
         attn_all = jnp.concatenate([r[:, lanes] for r in attn], axis=0)
         outs[slot][...] = low(tn(attn_all, grad_all))
 
 
-def tail_kernel(n, count, aligned, table, tokens_ref, grad_ref, *refs):
-    parts, weights, slices = refs[:n], refs[n : -4 - count], refs[-4 - count : -4]
-    out_ref, gain_ref, sum_ref, grads_ref = refs[-4:]
-    pieces = len(weights) // count
-    own_width = parts[0].shape[1] // 4
+def tail_kernel(n, count, table, tokens_ref, grad_ref, parts_ref, *refs):
+    weights, slices = refs[:count], refs[count : 2 * count]
+    out_ref, gain_ref, sum_ref, grads_ref = refs[2 * count :]
+    own_width = parts_ref.shape[2] // 4
     width = tokens_ref.shape[1]
     shard = width // count
     full_gain(table, n, slices, 0, gain_ref)
-    for k in range(n):
+    for owner in range(n):
         for part in range(3):
-            value = parts[k][:, part * own_width : (part + 1) * own_width]
-            if aligned:
-                grads_ref[:, at(part * width + table[0, k] * own_width, own_width)] = value
-            else:
-                start = (k * 3 + part) * own_width
-                grads_ref[:, start : start + own_width] = value
+            start = part * width + owner * own_width
+            grads_ref[:, start : start + own_width] = parts_ref[owner, :, part * own_width : (part + 1) * own_width]
     for slot in range(count):
-        for piece in range(pieces):
-            size = shard // pieces
-            place = at(table[0, n + slot] * shard + piece * size, size)
-            sum_ref[:, place] = nt(grads_ref[...], weights[slot * pieces + piece][...])
+        sum_ref[:, at(table[0, n + slot] * shard, shard)] = nt(grads_ref[...], weights[slot][...])
     value = wide(tokens_ref[...])
     inverse = lax.rsqrt(jnp.mean(value * value, axis=1, keepdims=True) + EPS)
     normed = value * inverse
@@ -540,16 +549,16 @@
 
 
 def join_kernel(terms, table, *refs):
-    qkv, back, out_ref = refs[:terms], refs[terms:-1], refs[-1]
+    qkv, back_ref, out_ref = refs[:terms], refs[terms], refs[-1]
     total = wide(qkv[0][...])
     for term in qkv[1:]:
         total = total + wide(term[...])
     start = total.shape[1]
     out_ref[:, 0:start] = low(total)
     shard = out_ref.shape[0]
-    other = wide(back[0][0:shard, start:])
-    for term in back[1:]:
-        other = other + wide(term[0:shard, start:])
+    other = wide(back_ref[0, 0:shard, start:])
+    for owner in range(1, back_ref.shape[0]):
+        other = other + wide(back_ref[owner, 0:shard, start:])
     out_ref[:, start:] = low(other)
 
 
@@ -634,6 +643,10 @@
     for k in range(1, count):
         result[count - k] = ring_shift(slots[k], ring, k)
     return result
+
+
+def exchange(array):
+    return lax.all_to_all(array, "ctx", 0, 0, tiled=True)
 
 
 def partner(value, count):
@@ -762,8 +775,8 @@
         behind.append(project(going.behind[step]))
         if going.step < half:
             ahead[step], behind[step], gate_pieces[3:] = going.advance(ahead[step], behind[step], gate_pieces[3:])
-    later_out, later_cot, later_qkv, unused = tie(w_out, cotangent, w_qkv, gate_pieces[-1])
-    outs = far_gather(later_out, fsdp)
+    later_out, later_cot, unused = tie(w_out, cotangent, gate_pieces[-1])
+    outs, cots = far_gather(later_out, fsdp), far_gather(later_cot, fsdp)
     *far, ahead, behind = tie(going.up, going.down, ahead, behind)
     pairs = [first] + ahead + [project(far[0]), project(far[1])] + behind[::-1]
     attn_slots, qkv = [pair[0] for pair in pairs], [pair[1] for pair in pairs]
@@ -771,18 +784,14 @@
     out_slots, out_t, log_total = attention_forward(
         table, lengths, block_order, qkv, ctx, own_heads, depth, TILE
     )
-    qkv_halves = [later_qkv[: shard // 2], later_qkv[shard // 2 :]] if aligned else [relative(later_qkv, table, ctx)]
-    qkv_nears = [far_gather(qkv_halves[0], fsdp)]
-    out_slots, qkv_nears[0], outs = tie(out_slots, qkv_nears[0], outs)
+    out_slots, outs, cots = tie(out_slots, outs, cots)
     attn_parts = ring_exchange(out_slots, ring)
-    later_cot, unused = tie(later_cot, out_slots[0])
-    outs, cots = near_gather(outs, fsdp), near_gather(far_gather(later_cot, fsdp), fsdp)
-    attn_parts, outs, cots[2::2] = tie(attn_parts, outs, cots[2::2])
+    outs, cots = near_gather(outs, fsdp), near_gather(cots, fsdp)
     resid, ffn_in = call(
         "leave", functools.partial(leave_kernel, ctx, fsdp),
         [shape((rows, width), f32), shape((rows, width))],
         [table, tokens] + attn_parts + outs + slices,
-        scratch=[gain_scratch, square_scratch, pltpu.VMEM((8, 128), f32)],
+        scratch=[gain_scratch, square_scratch],
         time=4.1,
     )
 
@@ -822,9 +831,10 @@
         "branch", functools.partial(branch_kernel, ctx, fsdp, len(grad_parts)),
         [shape((rows, width), f32), shape((rows, width))] + [shape((rows, own_width))] * ctx,
         [table, resid, cotangent] + grad_parts + outs + slices,
-        scratch=[gain_scratch, square_scratch, pltpu.VMEM((8, 128), f32)],
+        scratch=[gain_scratch, square_scratch],
         time=5,
     )
+    grad_attn, branch, ffn_sums.up, ffn_sums.down = tie(grad_attn, branch, ffn_sums.up, ffn_sums.down)
     grad_slots = ring_exchange(grad_attn, ring)
     out_sides = call(
         "out_weights", functools.partial(out_weight_kernel, ctx, fsdp),
@@ -832,8 +842,6 @@
         scratch=[square_scratch],
         time=3.3,
     )
-    if not aligned:
-        out_sides = [by_slot(array, table, ctx) for array in out_sides]
     out_nears = near_scatter(out_sides, fsdp)
 
     out_parts = far_scatter(out_nears, fsdp)
@@ -842,25 +850,20 @@
     grad_qkv = attention_backward(
         table, lengths, block_order, qkv, grad_slots, part_out, out_t, log_total, own_heads, depth, TILE
     )
-    (grad_qkv,) = ffn_sums.advance(grad_qkv)
-    qkv_halves, unused = tie(qkv_halves, grad_qkv[0])
-    qkv_nears += [far_gather(piece, fsdp) for piece in qkv_halves[1:]]
-    grad_back = ring_exchange(grad_qkv, ring)
     qkv_sides = call(
         "qkv_weights", functools.partial(qkv_weight_kernel, len(attn_slots), ctx, fsdp),
-        [shape((shard, 3 * own_width))] * fsdp, [table] + attn_slots + grad_qkv,
+        [shape((shard, 3 * own_width))] * fsdp, [table] + attn_slots + [grad_qkv],
         time=6,
     )
-    qkv_sum_nears = near_scatter(qkv_sides, fsdp)
-    third = max(1, (ctx - 1) * 3 // 7)
-    grad_back[-third:], qkv_sum_nears = ffn_sums.advance(grad_back[-third:], qkv_sum_nears)
-    qkv_sum = far_scatter(qkv_sum_nears, fsdp)
-    weights = [near_gather(nears, fsdp) for nears in qkv_nears]
-    weights = [pieces[slot] for slot in range(fsdp) for pieces in weights]
-
+    grad_qkv, qkv_sides = tie(grad_qkv, qkv_sides)
+    grad_back = exchange(grad_qkv)
+    qkv_sides, unused = ffn_sums.advance(qkv_sides, grad_qkv)
+    later_qkv, unused = tie(w_qkv, qkv_sides[0])
+    qkv_nears = far_gather(later_qkv, fsdp)
+    qkv_sum = far_scatter(near_scatter(qkv_sides, fsdp), fsdp)
+
+    qkv_sum = ffn_sums.advance(qkv_sum)[0] if ffn_sums.step > 1 else qkv_sum
     own_sum, ffn_up, ffn_down = ffn_sums.sums()
-    second = third + max(1, (ctx - 1) * 2 // 7)
-    ffn_up, ffn_down, qkv_sum, grad_back[-second:-third] = tie(ffn_up, ffn_down, qkv_sum, grad_back[-second:-third])
     *gate_sides, rest = call(
         "cut", functools.partial(cut_kernel, ctx),
         [shape((sub, 2 * hidden))] * fsdp + [shape((lines // 2, 2 * hidden))],
@@ -868,29 +871,29 @@
         scratch=[pltpu.VMEM((lines + lines // 2, 2 * hidden), jnp.bfloat16)],
         time=3,
     )
+    (joined,) = call(
+        "join", functools.partial(join_kernel, len(qkv_sum)),
+        [shape((shard, 4 * own_width))], [table] + qkv_sum + [grad_back],
+        time=2.5,
+    )
     gate_sides = side_exchange(gate_sides, fsdp)
-    gate_sides, grad_back[1:-second], weights = tie(gate_sides, grad_back[1:-second], weights)
+    gate_sides, joined = tie(gate_sides, joined)
     (packed,) = call(
         "pack", functools.partial(pack_kernel, ctx),
         [shape((lines + lines // 2, 2 * hidden))], [table, rest] + gate_sides,
         time=2,
     )
     ffn_going = Gather(packed, ring)
+    attn_going = Gather(joined, ring)
+    weights = near_gather(qkv_nears, fsdp)
     (grad_tokens,) = call(
-        "tail", functools.partial(tail_kernel, ctx, fsdp, aligned),
-        [shape((rows, width))], [table, tokens, grad_resid] + grad_back + weights + slices,
+        "tail", functools.partial(tail_kernel, ctx, fsdp),
+        [shape((rows, width))], [table, tokens, grad_resid, grad_back] + weights + slices,
         scratch=[gain_scratch, pltpu.VMEM((rows, width), f32), pltpu.VMEM((rows, 3 * width), jnp.bfloat16)],
         time=8,
     )
-    (joined,) = call(
-        "join", functools.partial(join_kernel, len(qkv_sum)),
-        [shape((shard, 4 * own_width))], [table] + qkv_sum + grad_back,
-        time=2.5,
-    )
-    joined, grad_tokens = ffn_going.advance(joined, grad_tokens)
     ffn_going.advance()
-    joined, unused = tie(joined, ffn_going.behind[-1])
-    attn_going = Gather(joined, ring)
+    (grad_tokens,) = ffn_going.advance(grad_tokens)
     grad_w_gate_up, grad_w_down, grad_gain_ffn = call(
         "feed_forward_final", functools.partial(ffn_final_kernel, ctx, fsdp, factor),
         [shape((shard, 2 * hidden * fsdp), f32), shape((hidden, width), f32), shape((1, shard), f32)],
@@ -926,10 +929,6 @@
     return jnp.concatenate([slot.reshape(rows, -1) for slot in slots], axis=1)
 
 
-def by_slot(array, table, ctx):
-    return jnp.stack([lax.dynamic_index_in_dim(array, table[0, k], 0, keepdims=False) for k in range(ctx)])
-
-
 def unmixed(weight, ctx, own_width):
     rows = weight.shape[0]
     return weight.reshape(rows, ctx, 3, own_width).transpose(0, 2, 1, 3).reshape(rows, -1)

time: 418 us -> 377 us (0.902)
  Pallas kernels: 146 us -> 100 us
  starting transfers between devices: 78.6 us -> 87.6 us
  waiting for transfers between devices: 157 us -> 163 us
  local copies, waits for them, and re-layouts: 15.6 us -> 10.8 us
    pallas_call x24, Pallas kernels: 107 us -> 60.8 us  [call(): pl.pallas_call(kernel, out_shape=list(out), in_specs=[SM] + [VM] * (len(i...]
    ppermute x53 -> x46, waiting for transfers between devices: 121 us -> 132 us  [ring_shift(): lax.ppermute(value, 'ctx', [(ring[i], ring[(i + step) % count]) for i in...]
    ppermute x10 -> x9, waiting for transfers between devices: 21.6 us -> 17.1 us  [chip_shift(): lax.ppermute(value, 'fsdp', [(i, (i + 2 * step) % count) for i in range(c...]
    ppermute x53 -> x46, starting transfers between devices: 64.9 us -> 69.1 us  [ring_shift(): lax.ppermute(value, 'ctx', [(ring[i], ring[(i + step) % count]) for i in...]
    unnamed x190 -> x82, local copies, waits for them, and re-layouts: 10.9 us -> 8.72 us
  transfers between devices with their start and end apart: 89 -> 80, of which waited for: 42 -> 42; matrix products, arithmetic and copies ran while one was open for 4% -> 2% of each run, Pallas kernels for 32% -> 25%
where the time goes in v3:
time: 377 us; the launch traced here: 372 us
  waiting for transfers between devices  163 us (43%)
  Pallas kernels  100 us (27%)
  starting transfers between devices  87.6 us (23%)
  local copies, waits for them, and re-layouts  10.8 us (3%)
  other arithmetic  7.68 us (2%)
    ppermute x46, waiting for transfers between devices, ring_shift(): lax.ppermute(value, 'ctx', [(ring[i], ring[(i + step) % count]) for i in...  132 us
    ppermute x46, starting transfers between devices, ring_shift(): lax.ppermute(value, 'ctx', [(ring[i], ring[(i + step) % count]) for i in...  69.1 us
    pallas_call x24, Pallas kernels, call(): pl.pallas_call(kernel, out_shape=list(out), in_specs=[SM] + [VM] * (len(i...  60.8 us
    pallas_call x1, Pallas kernels, attention_backward(): pl.pallas_call(functools.partial(bwd_kernel, meta), out_shape=jax.ShapeDt...  20.5 us
    pallas_call x1, Pallas kernels, attention_forward(): pl.pallas_call(functools.partial(fwd_kernel, meta), out_shape=[jax.ShapeD...  19 us
    ppermute x9, waiting for transfers between devices, chip_shift(): lax.ppermute(value, 'fsdp', [(i, (i + 2 * step) % count) for i in range(c...  17.1 us
    unnamed x82, local copies, waits for them, and re-layouts  8.72 us
    ppermute x9, starting transfers between devices, chip_shift(): lax.ppermute(value, 'fsdp', [(i, (i + 2 * step) % count) for i in range(c...  7.71 us
  transfers between devices with their start and end apart: 80, of which 42 were waited for; matrix products, arithmetic and copies ran while one was open for 2% of the time, Pallas kernels for 25%

profile of v3, /device:TPU:0, one launch (start us, length us, event | category | flops | bytes accessed | tf_op | source)
XLA Modules:
  0.0 371.6 jit_solution(6901486900830105971)
XLA Ops:
  0.6 3.1 collective-permute-start.1
  7.2 2.0 collective-permute-start.2
  9.2 1.8 copy-done
  12.3 3.5 collective-permute-done.1.rows_ref
  26.2 7.0 %collective-permute-done.3.rows_ref = bf16[256,1024]{1,0:T(8,128)(2,1)S(1)} collective-permute-done((bf16[256,1024]{1,0:T(8,128)(2,1)S(1)}, bf16[256,1024]{1,0:T(8,128)(2,1)S(1)}, u32[]{:S(2)}, u32[]{:S(2)}) %collective-permute-start.3) | collective-permute-done | bytes 524320 | tf_op jit(solution)/shard_map/ppermute | solution.py:578
  33.4 2.9 collective-permute-done.8.refs_6_
  40.7 8.7 %collective-permute-done.9.rows_ref = bf16[256,1024]{1,0:T(8,128)(2,1)S(1)} collective-permute-done((bf16[256,1024]{1,0:T(8,128)(2,1)S(1)}, bf16[256,1024]{1,0:T(8,128)(2,1)S(1)}, u32[]{:S(2)}, u32[]{:S(2)}) %collective-permute-start.9) | collective-permute-done | bytes 524320 | tf_op jit(solution)/shard_map/ppermute | solution.py:578
  57.3 3.6 collective-permute-done.13.rows_ref
  64.2 19.0 %attention_forward.1 = (bf16[256,128]{1,0:T(8,128)(2,1)S(1)}, bf16[256,128]{1,0:T(8,128)(2,1)S(1)}, bf16[256,128]{1,0:T(8,128)(2,1)S(1)}, bf16[256,128]{1,0:T(8,...) custom-call(s32[1,12]{1,0:T(1,128)S(1)} %constant_dynamic-slice_fusi, ...), custom_call_target="tpu_custom_call" | custom-call | bytes 57800000 | tf_op jit(solution)/shard_map/attention_forward/pallas_call | solution.py:203
  88.1 3.6 collective-permute-start.19
  91.7 3.2 collective-permute-done.17.refs_2_
  94.9 2.0 collective-permute-done.18.refs_3_
  96.8 3.2 collective-permute-start.21
  108.0 6.2 %feed_forward.2 = (bf16[256,1024]{1,0:T(8,128)(2,1)S(1)}, bf16[256,1024]{1,0:T(8,128)(2,1)S(1)}, bf16[256,1024]{1,0:T(8,128)(2,1)S(1)}, bf16[256,1024]{1,0:T(8,1...) custom-call(s32[1,12]{1,0:T(1,128)S(1)} %constant_dynamic-slice_fusion.table, ...), custom_call_target="tpu_custom_call" | custom-call | bytes 32300000 | tf_op jit(solution)/shard_map/feed_forward/pallas_call | solution.py:257
  115.0 5.4 %collective-permute-done.27.refs_0_.refs_2_ = bf16[256,1024]{1,0:T(8,128)(2,1)S(1)} collective-permute-done((bf16[256,1024]{1,0:T(8,128)(2,1)S(1)}, bf16[256,1024]{1,0:T(8,128)(2,1)S(1)}, u32[]{:S(2)}, u32[]{:S(2)}) %collective-permute-start.27) | collective-permute-done | bytes 524320 | tf_op jit(solution)/shard_map/ppermute | solution.py:657
  122.3 6.2 %feed_forward.3 = (bf16[256,1024]{1,0:T(8,128)(2,1)S(1)}, bf16[256,1024]{1,0:T(8,128)(2,1)S(1)}, bf16[256,1024]{1,0:T(8,128)(2,1)S(1)}, bf16[256,1024]{1,0:T(8,1...) custom-call(s32[1,12]{1,0:T(1,128)S(1)} %constant_dynamic-slice_fusion.table, ...), custom_call_target="tpu_custom_call" | custom-call | bytes 32300000 | tf_op jit(solution)/shard_map/feed_forward/pallas_call | solution.py:257
  131.3 6.2 %feed_forward_weights.1 = (bf16[192,1408]{1,0:T(8,128)(2,1)S(1)}, bf16[192,1408]{1,0:T(8,128)(2,1)S(1)}, bf16[192,1408]{1,0:T(8,128)(2,1)S(1)}, bf16[192,1408]{1...) custom-call(s32[1,12]{1,0:T(1,128)S(1)} %constant_dynamic-slice_fusi, ...), custom_call_target="tpu_custom_call" | custom-call | bytes 40800000 | tf_op jit(solution)/shard_map/feed_forward_weights/pallas_call | solution.py:257
  137.5 7.5 %collective-permute-done.35.refs_1_ = bf16[256,1024]{1,0:T(8,128)(2,1)S(1)} collective-permute-done((bf16[256,1024]{1,0:T(8,128)(2,1)S(1)}, bf16[256,1024]{1,0:T(8,128)(2,1)S(1)}, u32[]{:S(2)}, u32[]{:S(2)}) %collective-permute-start.35) | collective-permute-done | bytes 524320 | tf_op jit(solution)/shard_map/ppermute | solution.py:657
  145.0 2.0 collective-permute-start.37
  147.0 2.4 branch.1
  149.5 3.2 collective-permute-done.36
  158.5 2.7 collective-permute-start.40
  161.2 2.3 collective-permute-start.41
  163.5 3.0 collective-permute-done.39.refs_11_
  166.5 1.8 collective-permute-start.42
  172.6 3.0 collective-permute-done.43.refs_15_
  180.1 20.5 %attention_backward.1.refs_9_ = bf16[8,256,512]{2,1,0:T(8,128)(2,1)} custom-call(s32[1,12]{1,0:T(1,128)S(1)} %constant_dynamic-slice_fusion.table, s32[1,4]{1,0:T(1,128)S(1)} %copy-done.32, s32[1,32]{1,0:T(1,128)S(1)} %copy-done.33, bf16[256,384]{1,0:T(8,128)(2,1)S(1)} %get-tuple-element.275.refs_0_, bf16[256,384]{1,0:T(8,128)(2,1)S(1)} %get-tuple-element.301.refs_1_, ...), custom_call_target="tpu_custom_call" | custom-call | bytes 61200000 | tf_op jit(solution)/shard_map/attention_backward/pallas_call | solution.py:216
  200.6 4.1 %qkv_weights.1 = (bf16[256,384]{1,0:T(8,128)(2,1)S(1)}, bf16[256,384]{1,0:T(8,128)(2,1)S(1)}, bf16[256,384]{1,0:T(8,128)(2,1)S(1)}, bf16[256,384]{1,0:T(8,128)(2,1)S(1)}) custom-call(s32[1,12]{1,0:T(1,128)S(1)} %constant_dynamic-slice_fusion.table, bf16[256,1024]{1,0:T(8,128)(2,1)S(1)} %get-tuple-element.421.refs_0_, ...), custom_call_target="tpu_custom_call" | custom-call | bytes 20400000 | tf_op jit(solution)/shard_map/qkv_weights/pallas_call | solution.py:257
  207.4 3.7 all-to-all-start
  212.7 2.1 collective-permute-start.51
  216.4 2.1 collective-permute-start.54
  219.3 34.7 %collective-permute-done.51 = bf16[192,1408]{1,0:T(8,128)(2,1)S(1)} collective-permute-done((bf16[192,1408]{1,0:T(8,128)(2,1)S(1)}, bf16[192,1408]{1,0:T(8,128)(2,1)S(1)}, u32[]{:S(2)}, u32[]{:S(2)}) %collective-permute-start.51) | collective-permute-done | bytes 540704 | tf_op jit(solution)/shard_map/ppermute | solution.py:578
  254.0 3.4 collective-permute-done.54.refs_1_
  258.2 11.4 %collective-permute-start.56 = (bf16[192,1408]{1,0:T(8,128)(2,1)S(1)}, bf16[192,1408]{1,0:T(8,128)(2,1)S(1)}, u32[]{:S(2)}, u32[]{:S(2)}) collective-permute-start(bf16[192,1408]{1,0:T(8,128)(2,1)S(1)} %add_convert_fusion), channel_id=1, source_target_pairs={{4,0},{12,4},{20,12},{28,20},{24,28},{16,24},{8,16},{0,8},{5,1},{1... | collective-permute-start | bytes 1622024 | tf_op jit(solution)/shard_map/ppermute | solution.py:578
  270.5 7.3 %collective-permute-done.56.down_ref = bf16[192,1408]{1,0:T(8,128)(2,1)S(1)} collective-permute-done((bf16[192,1408]{1,0:T(8,128)(2,1)S(1)}, bf16[192,1408]{1,0:T(8,128)(2,1)S(1)}, u32[]{:S(2)}, u32[]{:S(2)}) %collective-permute-start.56) | collective-permute-done | bytes 540704 | tf_op jit(solution)/shard_map/ppermute | solution.py:578
  277.8 3.1 collective-permute-done.55.up_ref
  283.3 1.8 collective-permute-start.58
  295.2 11.4 %collective-permute-done.61.refs_1_ = bf16[192,1408]{1,0:T(8,128)(2,1)S(1)} collective-permute-done((bf16[192,1408]{1,0:T(8,128)(2,1)S(1)}, bf16[192,1408]{1,0:T(8,128)(2,1)S(1)}, u32[]{:S(2)}, u32[]{:S(2)}) %collective-permute-start.61) | collective-permute-done | bytes 540704 | tf_op jit(solution)/shard_map/ppermute | solution.py:578
  307.4 2.0 collective-permute-start.62
  309.4 1.9 collective-permute-done.68.refs_1_
  313.1 2.7 collective-permute-done.67.refs_8_
  317.9 6.0 %tail.1 = bf16[256,1024]{1,0:T(8,128)(2,1)} custom-call(s32[1,12]{1,0:T(1,128)S(1)} %constant_dynamic-slice_fusion.table, bf16[256,1024]{1,0:T(8,128)(2,1)S(1)} %copy-done.3, f32[256,1024]{1,0:T(8,128)S(1)} %copy-done.9, bf16[8,256,512]{2,1,0:T(8,128)(2,1)S(1)} %all-to-all-done.refs_2_.parts_ref, bf16[256,3072]{1,0:T(8,128)(2,1)} %w_ref.6, ...), custom_call_target="tpu_custom_call" | custom-call | bytes 27200000 | tf_op jit(solution)/shard_map/tail/pallas_call | solution.py:257
  323.9 6.5 %collective-permute-done.69.refs_7_ = bf16[256,512]{1,0:T(8,128)(2,1)S(1)} collective-permute-done((bf16[256,512]{1,0:T(8,128)(2,1)S(1)}, bf16[256,512]{1,0:T(8,128)(2,1)S(1)}, u32[]{:S(2)}, u32[]{:S(2)}) %collective-permute-start.69) | collective-permute-done | bytes 262176 | tf_op jit(solution)/shard_map/ppermute | solution.py:578
  335.3 4.3 %collective-permute-done.71.refs_6_ = bf16[256,512]{1,0:T(8,128)(2,1)S(1)} collective-permute-done((bf16[256,512]{1,0:T(8,128)(2,1)S(1)}, bf16[256,512]{1,0:T(8,128)(2,1)S(1)}, u32[]{:S(2)}, u32[]{:S(2)}) %collective-permute-start.71) | collective-permute-done | bytes 262176 | tf_op jit(solution)/shard_map/ppermute | solution.py:578
  341.4 12.4 %collective-permute-done.72.refs_3_ = bf16[256,512]{1,0:T(8,128)(2,1)S(1)} collective-permute-done((bf16[256,512]{1,0:T(8,128)(2,1)S(1)}, bf16[256,512]{1,0:T(8,128)(2,1)S(1)}, u32[]{:S(2)}, u32[]{:S(2)}) %collective-permute-start.72) | collective-permute-done | bytes 262176 | tf_op jit(solution)/shard_map/ppermute | solution.py:578
  356.2 2.0 collective-permute-start.77
  360.5 4.3 %attention_final.1 = (f32[256,3072]{1,0:T(8,128)}, f32[256,1024]{1,0:T(8,128)}, f32[1,256]{1,0:T(1,128)}) custom-call(s32[1,12]{1,0:T(1,128)S(1)} %constant_dynamic-slice_fusion.table, bf16[256,3072]{1,0:T(8,128)(2,1)} %w_ref.6, bf16[1,256]{1,0:T(2,128)(2,1)S(1)} %reshape.28.one_ref.gain_ref, bf16[256,512]{1,0:T(8,128)(2,1)S(1)} %join.1.refs_0_, ...), custom_call_target="tpu_custom_call" | custom-call | bytes 15639999 | tf_op jit(solution)/shard_map/attention_final/pallas_call | solution.py:257
  364.7 6.4 %feed_forward_final.1 = (f32[256,5632]{1,0:T(8,128)}, f32[704,1024]{1,0:T(8,128)}, f32[1,256]{1,0:T(1,128)}) custom-call(s32[1,12]{1,0:T(1,128)S(1)} %constant_dynamic-slice_fusion.table, bf16[256,5632]{1,0:T(8,128)(2,1)S(1)} %copy-done.1, bf16[1,256]{1,0:T(2,128)(2,1)S(1)} %reshape.29.two_ref.gain_ref, bf16[192,1408]{1,0:T(8,128)(2,1)S(1)} %pack.1.refs_0_, ...), custom_call_target="tpu_custom_call" | custom-call | bytes 27200000 | tf_op jit(solution)/shard_map/feed_forward_final/pallas_call | solution.py:257
  (243 shorter events, 100.1 us)
Async XLA Ops:
  0.6 15.2 %collective-permute-start.1 = (bf16[256,1024]{1,0:T(8,128)(2,1)}, bf16[256,1024]{1,0:T(8,128)(2,1)S(1)}, u32[]{:S(2)}, u32[]{:S(2)}) collective-permute-start(bf16[256,1024]{1,0:T(8,128)(2,1)} %tokens_ref.3), channel_id=1, source_target_pairs={{4,0},{12,4},{20,12},{28,20},{24,28},{16,24},{8,16},{0,8},{5,1},{1... | collective-permute-start | bytes 1572872 | tf_op jit(solution)/shard_map/ppermute | solution.py:578
  3.7 13.6 %collective-permute-start = (bf16[256,1024]{1,0:T(8,128)(2,1)}, bf16[256,1024]{1,0:T(8,128)(2,1)S(1)}, u32[]{:S(2)}, u32[]{:S(2)}) collective-permute-start(bf16[256,1024]{1,0:T(8,128)(2,1)} %tokens_ref.3), channel_id=1, source_target_pairs={{4,12},{12,20},{20,28},{28,24},{24,16},{16,8},{8,0},{0,4},{5,13},{... | collective-permute-start | bytes 1572872 | tf_op jit(solution)/shard_map/ppermute | solution.py:578
  7.2 10.1 %collective-permute-start.2 = (bf16[264,384]{1,0:T(8,128)(2,1)S(1)}, bf16[264,384]{1,0:T(8,128)(2,1)S(1)}, u32[]{:S(2)}, u32[]{:S(2)}) collective-permute-start(bf16[264,384]{1,0:T(8,128)(2,1)S(1)} %slice.25.refs_0_.refs_12_.refs_6_.refs_4_), channel_id=1, source_target_pairs={{0,2},{1,3},{2,0},{3,1},{4,6},{5,7},{6,4},{7,5},{8,10},{9,11},{10,... | collective-permute-start | bytes 608264 | tf_op jit(solution)/shard_map/ppermute | solution.py:657
  17.3 16.1 %collective-permute-start.7 = (bf16[256,1408]{1,0:T(8,128)(2,1)S(1)}, bf16[256,1408]{1,0:T(8,128)(2,1)S(1)}, u32[]{:S(2)}, u32[]{:S(2)}) collective-permute-start(bf16[256,1408]{1,0:T(8,128)(2,1)S(1)} %get-tuple-element.273), channel_id=1, source_target_pairs={{0,1},{1,0},{2,3},{3,2},{4,5},{5,4},{6,7},{7,6},{8,9},{9,8},{10,11... | collective-permute-start | bytes 2162696 | tf_op jit(solution)/shard_map/ppermute | solution.py:687
  17.3 19.0 %collective-permute-start.8 = (bf16[256,1408]{1,0:T(8,128)(2,1)S(1)}, bf16[256,1408]{1,0:T(8,128)(2,1)S(1)}, u32[]{:S(2)}, u32[]{:S(2)}) collective-permute-start(bf16[256,1408]{1,0:T(8,128)(2,1)S(1)} %get-tuple-element.274), channel_id=1, source_target_pairs={{0,2},{1,3},{2,0},{3,1},{4,6},{5,7},{6,4},{7,5},{8,10},{9,11},{10,... | collective-permute-start | bytes 2162696 | tf_op jit(solution)/shard_map/ppermute | solution.py:687
  19.0 14.2 %collective-permute-start.3 = (bf16[256,1024]{1,0:T(8,128)(2,1)S(1)}, bf16[256,1024]{1,0:T(8,128)(2,1)S(1)}, u32[]{:S(2)}, u32[]{:S(2)}) collective-permute-start(bf16[256,1024]{1,0:T(8,128)(2,1)S(1)} %collective-permute-done.rows_ref), channel_id=1, source_target_pairs={{4,12},{12,20},{20,28},{28,24},{24,16},{16,8},{8,0},{0,4},{5,13},{... | collective-permute-start | bytes 1572872 | tf_op jit(solution)/shard_map/ppermute | solution.py:578
  19.5 13.9 %collective-permute-start.4 = (bf16[256,1024]{1,0:T(8,128)(2,1)S(1)}, bf16[256,1024]{1,0:T(8,128)(2,1)S(1)}, u32[]{:S(2)}, u32[]{:S(2)}) collective-permute-start(bf16[256,1024]{1,0:T(8,128)(2,1)S(1)} %collective-permute-done.1.rows_ref), channel_id=1, source_target_pairs={{4,0},{12,4},{20,12},{28,20},{24,28},{16,24},{8,16},{0,8},{5,1},{1... | collective-permute-start | bytes 1572872 | tf_op jit(solution)/shard_map/ppermute | solution.py:578
  22.5 28.3 %collective-permute-start.11 = (bf16[256,1408]{1,0:T(8,128)(2,1)S(1)}, bf16[256,1408]{1,0:T(8,128)(2,1)S(1)}, u32[]{:S(2)}, u32[]{:S(2)}) collective-permute-start(bf16[256,1408]{1,0:T(8,128)(2,1)S(1)} %get-tuple-element.284), channel_id=1, source_target_pairs={{0,3},{1,2},{2,1},{3,0},{4,7},{5,6},{6,5},{7,4},{8,11},{9,10},{10,... | collective-permute-start | bytes 2162696 | tf_op jit(solution)/shard_map/ppermute | solution.py:687
  36.3 13.0 %collective-permute-start.9 = (bf16[256,1024]{1,0:T(8,128)(2,1)S(1)}, bf16[256,1024]{1,0:T(8,128)(2,1)S(1)}, u32[]{:S(2)}, u32[]{:S(2)}) collective-permute-start(bf16[256,1024]{1,0:T(8,128)(2,1)S(1)} %collective-permute-done.3.rows_ref), channel_id=1, source_target_pairs={{4,12},{12,20},{20,28},{28,24},{24,16},{16,8},{8,0},{0,4},{5,13},{... | collective-permute-start | bytes 1572872 | tf_op jit(solution)/shard_map/ppermute | solution.py:578
  36.6 12.8 %collective-permute-start.10 = (bf16[256,1024]{1,0:T(8,128)(2,1)S(1)}, bf16[256,1024]{1,0:T(8,128)(2,1)S(1)}, u32[]{:S(2)}, u32[]{:S(2)}) collective-permute-start(bf16[256,1024]{1,0:T(8,128)(2,1)S(1)} %collective-permute-done.4.rows_ref), channel_id=1, source_target_pairs={{4,0},{12,4},{20,12},{28,20},{24,28},{16,24},{8,16},{0,8},{5,1},{1... | collective-permute-start | bytes 1572872 | tf_op jit(solution)/shard_map/ppermute | solution.py:578
  50.8 32.4 %collective-permute-start.14 = (bf16[256,1024]{1,0:T(8,128)(2,1)S(1)}, bf16[256,1024]{1,0:T(8,128)(2,1)S(1)}, u32[]{:S(2)}, u32[]{:S(2)}) collective-permute-start(bf16[256,1024]{1,0:T(8,128)(2,1)S(1)} %copy-done.7), channel_id=1, source_target_pairs={{0,2},{1,3},{2,0},{3,1},{4,6},{5,7},{6,4},{7,5},{8,10},{9,11},{10,... | collective-permute-start | bytes 1572872 | tf_op jit(solution)/shard_map/ppermute | solution.py:657
  52.3 30.9 %collective-permute-start.15 = (bf16[256,1024]{1,0:T(8,128)(2,1)S(1)}, bf16[256,1024]{1,0:T(8,128)(2,1)S(1)}, u32[]{:S(2)}, u32[]{:S(2)}) collective-permute-start(bf16[256,1024]{1,0:T(8,128)(2,1)S(1)} %copy-done.4), channel_id=1, source_target_pairs={{0,2},{1,3},{2,0},{3,1},{4,6},{5,7},{6,4},{7,5},{8,10},{9,11},{10,... | collective-permute-start | bytes 1572872 | tf_op jit(solution)/shard_map/ppermute | solution.py:657
  83.3 21.2 %collective-permute-start.23 = (bf16[256,1024]{1,0:T(8,128)(2,1)S(1)}, bf16[256,1024]{1,0:T(8,128)(2,1)S(1)}, u32[]{:S(2)}, u32[]{:S(2)}) collective-permute-start(bf16[256,1024]{1,0:T(8,128)(2,1)S(1)} %copy-done.7), channel_id=1, source_target_pairs={{0,1},{1,0},{2,3},{3,2},{4,5},{5,4},{6,7},{7,6},{8,9},{9,8},{10,11... | collective-permute-start | bytes 1572872 | tf_op jit(solution)/shard_map/ppermute | solution.py:653
  83.3 21.1 %collective-permute-start.24 = (bf16[256,1024]{1,0:T(8,128)(2,1)S(1)}, bf16[256,1024]{1,0:T(8,128)(2,1)S(1)}, u32[]{:S(2)}, u32[]{:S(2)}) collective-permute-start(bf16[256,1024]{1,0:T(8,128)(2,1)S(1)} %collective-permute-done.14.refs_10_.refs_4_), channel_id=1, source_target_pairs={{0,1},{1,0},{2,3},{3,2},{4,5},{5,4},{6,7},{7,6},{8,9},{9,8},{10,11... | collective-permute-start | bytes 1572872 | tf_op jit(solution)/shard_map/ppermute | solution.py:653
  85.4 9.4 %collective-permute-start.17 = (bf16[256,128]{1,0:T(8,128)(2,1)S(1)}, bf16[256,128]{1,0:T(8,128)(2,1)S(1)}, u32[]{:S(2)}, u32[]{:S(2)}) collective-permute-start(bf16[256,128]{1,0:T(8,128)(2,1)S(1)} %get-tuple-element.324), channel_id=1, source_target_pairs={{4,8},{12,0},{20,4},{28,12},{24,20},{16,28},{8,24},{0,16},{5,9},{1... | collective-permute-start | bytes 196616 | tf_op jit(solution)/shard_map/ppermute | solution.py:578
  86.8 10.0 %collective-permute-start.18 = (bf16[256,128]{1,0:T(8,128)(2,1)S(1)}, bf16[256,128]{1,0:T(8,128)(2,1)S(1)}, u32[]{:S(2)}, u32[]{:S(2)}) collective-permute-start(bf16[256,128]{1,0:T(8,128)(2,1)S(1)} %get-tuple-element.325), channel_id=1, source_target_pairs={{4,16},{12,8},{20,0},{28,4},{24,12},{16,20},{8,28},{0,24},{5,17},{... | collective-permute-start | bytes 196616 | tf_op jit(solution)/shard_map/ppermute | solution.py:578
  88.1 11.9 %collective-permute-start.19 = (bf16[256,128]{1,0:T(8,128)(2,1)S(1)}, bf16[256,128]{1,0:T(8,128)(2,1)S(1)}, u32[]{:S(2)}, u32[]{:S(2)}) collective-permute-start(bf16[256,128]{1,0:T(8,128)(2,1)S(1)} %get-tuple-element.326), channel_id=1, source_target_pairs={{4,24},{12,16},{20,8},{28,0},{24,4},{16,12},{8,20},{0,28},{5,25},{... | collective-permute-start | bytes 196616 | tf_op jit(solution)/shard_map/ppermute | solution.py:578
  106.1 14.3 %collective-permute-start.27 = (bf16[256,1024]{1,0:T(8,128)(2,1)S(1)}, bf16[256,1024]{1,0:T(8,128)(2,1)S(1)}, u32[]{:S(2)}, u32[]{:S(2)}) collective-permute-start(bf16[256,1024]{1,0:T(8,128)(2,1)S(1)} %get-tuple-element.333.refs_0_), channel_id=1, source_target_pairs={{0,2},{1,3},{2,0},{3,1},{4,6},{5,7},{6,4},{7,5},{8,10},{9,11},{10,... | collective-permute-start | bytes 1572872 | tf_op jit(solution)/shard_map/ppermute | solution.py:657
  106.1 14.8 %collective-permute-start.30 = (bf16[256,1024]{1,0:T(8,128)(2,1)S(1)}, bf16[256,1024]{1,0:T(8,128)(2,1)S(1)}, u32[]{:S(2)}, u32[]{:S(2)}) collective-permute-start(bf16[256,1024]{1,0:T(8,128)(2,1)S(1)} %collective-permute-done.15.refs_2_.refs_6_), channel_id=1, source_target_pairs={{0,1},{1,0},{2,3},{3,2},{4,5},{5,4},{6,7},{7,6},{8,9},{9,8},{10,11... | collective-permute-start | bytes 1572872 | tf_op jit(solution)/shard_map/ppermute | solution.py:653
  131.0 14.0 %collective-permute-start.35 = (bf16[256,1024]{1,0:T(8,128)(2,1)S(1)}, bf16[256,1024]{1,0:T(8,128)(2,1)S(1)}, u32[]{:S(2)}, u32[]{:S(2)}) collective-permute-start(bf16[256,1024]{1,0:T(8,128)(2,1)S(1)} %add_convert_fusion.9), channel_id=1, source_target_pairs={{0,2},{1,3},{2,0},{3,1},{4,6},{5,7},{6,4},{7,5},{8,10},{9,11},{10,... | collective-permute-start | bytes 1572872 | tf_op jit(solution)/shard_map/ppermute | solution.py:657
  154.4 14.0 %collective-permute-start.45 = (bf16[8,256,128]{2,1,0:T(8,128)(2,1)S(1)}, bf16[8,256,128]{2,1,0:T(8,128)(2,1)S(1)}, u32[]{:S(2)}, u32[]{:S(2)}) collective-permute-start(bf16[8,256,128]{2,1,0:T(8,128)(2,1)S(1)} %get-tuple-element.402), channel_id=1, source_target_pairs={{0,1},{1,0},{2,3},{3,2},{4,5},{5,4},{6,7},{7,6},{8,9},{9,8},{10,11... | collective-permute-start | bytes 1572872 | tf_op jit(solution)/shard_map/ppermute | solution.py:653
  156.4 14.0 %collective-permute-start.47 = (bf16[8,256,128]{2,1,0:T(8,128)(2,1)S(1)}, bf16[8,256,128]{2,1,0:T(8,128)(2,1)S(1)}, u32[]{:S(2)}, u32[]{:S(2)}) collective-permute-start(bf16[8,256,128]{2,1,0:T(8,128)(2,1)S(1)} %add_convert_fusion.7), channel_id=1, source_target_pairs={{0,2},{1,3},{2,0},{3,1},{4,6},{5,7},{6,4},{7,5},{8,10},{9,11},{10,... | collective-permute-start | bytes 1572872 | tf_op jit(solution)/shard_map/ppermute | solution.py:657
  158.5 13.6 %collective-permute-start.40 = (bf16[256,128]{1,0:T(8,128)(2,1)S(1)}, bf16[256,128]{1,0:T(8,128)(2,1)S(1)}, u32[]{:S(2)}, u32[]{:S(2)}) collective-permute-start(bf16[256,128]{1,0:T(8,128)(2,1)S(1)} %get-tuple-element.395), channel_id=1, source_target_pairs={{4,16},{12,8},{20,0},{28,4},{24,12},{16,20},{8,28},{0,24},{5,17},{... | collective-permute-start | bytes 196616 | tf_op jit(solution)/shard_map/ppermute | solution.py:578
  161.2 11.0 %collective-permute-start.41 = (bf16[256,128]{1,0:T(8,128)(2,1)S(1)}, bf16[256,128]{1,0:T(8,128)(2,1)S(1)}, u32[]{:S(2)}, u32[]{:S(2)}) collective-permute-start(bf16[256,128]{1,0:T(8,128)(2,1)S(1)} %get-tuple-element.396), channel_id=1, source_target_pairs={{4,24},{12,16},{20,8},{28,0},{24,4},{16,12},{8,20},{0,28},{5,25},{... | collective-permute-start | bytes 196616 | tf_op jit(solution)/shard_map/ppermute | solution.py:578
  176.9 34.2 %collective-permute-start.49 = (bf16[192,1408]{1,0:T(8,128)(2,1)}, bf16[192,1408]{1,0:T(8,128)(2,1)}, u32[]{:S(2)}, u32[]{:S(2)}) collective-permute-start(bf16[192,1408]{1,0:T(8,128)(2,1)} %add_convert_fusion.4), channel_id=1, source_target_pairs={{4,0},{12,4},{20,12},{28,20},{24,28},{16,24},{8,16},{0,8},{5,1},{1... | collective-permute-start | bytes 1622024 | tf_op jit(solution)/shard_map/ppermute | solution.py:578
  178.5 32.6 %collective-permute-start.48 = (bf16[192,1408]{1,0:T(8,128)(2,1)}, bf16[192,1408]{1,0:T(8,128)(2,1)}, u32[]{:S(2)}, u32[]{:S(2)}) collective-permute-start(bf16[192,1408]{1,0:T(8,128)(2,1)} %add_convert_fusion.5), channel_id=1, source_target_pairs={{4,12},{12,20},{20,28},{28,24},{24,16},{16,8},{8,0},{0,4},{5,13},{... | collective-permute-start | bytes 1622024 | tf_op jit(solution)/shard_map/ppermute | solution.py:578
  207.4 77.8 %all-to-all-start = ((bf16[8,256,512]{2,1,0:T(8,128)(2,1)}), bf16[8,256,512]{2,1,0:T(8,128)(2,1)S(1)}, u32[]{:S(2)}, u32[]{:S(2)}) async-start(bf16[8,256,512]{2,1,0:T(8,128)(2,1)} %attention_backward.1.refs_9_), calls=%async_computation | async-start | bytes 4194304 | tf_op jit(solution)/shard_map/all_to_all | solution.py:649
  212.7 41.3 %collective-permute-start.51 = (bf16[192,1408]{1,0:T(8,128)(2,1)S(1)}, bf16[192,1408]{1,0:T(8,128)(2,1)S(1)}, u32[]{:S(2)}, u32[]{:S(2)}) collective-permute-start(bf16[192,1408]{1,0:T(8,128)(2,1)S(1)} %add_convert_fusion.2), channel_id=1, source_target_pairs={{4,0},{12,4},{20,12},{28,20},{24,28},{16,24},{8,16},{0,8},{5,1},{1... | collective-permute-start | bytes 1622024 | tf_op jit(solution)/shard_map/ppermute | solution.py:578
  215.9 38.1 %collective-permute-start.50 = (bf16[192,1408]{1,0:T(8,128)(2,1)S(1)}, bf16[192,1408]{1,0:T(8,128)(2,1)S(1)}, u32[]{:S(2)}, u32[]{:S(2)}) collective-permute-start(bf16[192,1408]{1,0:T(8,128)(2,1)S(1)} %add_convert_fusion.3), channel_id=1, source_target_pairs={{4,12},{12,20},{20,28},{28,24},{24,16},{16,8},{8,0},{0,4},{5,13},{... | collective-permute-start | bytes 1622024 | tf_op jit(solution)/shard_map/ppermute | solution.py:578
  216.3 53.6 %collective-permute-start.65 = (bf16[256,3072]{1,0:T(8,128)(2,1)}, bf16[256,3072]{1,0:T(8,128)(2,1)}, u32[]{:S(2)}, u32[]{:S(2)}) collective-permute-start(bf16[256,3072]{1,0:T(8,128)(2,1)} %w_ref.6), channel_id=1, source_target_pairs={{0,2},{1,3},{2,0},{3,1},{4,6},{5,7},{6,4},{7,5},{8,10},{9,11},{10,... | collective-permute-start | bytes 4718600 | tf_op jit(solution)/shard_map/ppermute | solution.py:657
  216.4 41.0 %collective-permute-start.54 = (bf16[256,384]{1,0:T(8,128)(2,1)S(1)}, bf16[256,384]{1,0:T(8,128)(2,1)S(1)}, u32[]{:S(2)}, u32[]{:S(2)}) collective-permute-start(bf16[256,384]{1,0:T(8,128)(2,1)S(1)} %add_convert_fusion.14), channel_id=1, source_target_pairs={{0,2},{1,3},{2,0},{3,1},{4,6},{5,7},{6,4},{7,5},{8,10},{9,11},{10,... | collective-permute-start | bytes 589832 | tf_op jit(solution)/shard_map/ppermute | solution.py:657
  258.2 19.6 %collective-permute-start.56 = (bf16[192,1408]{1,0:T(8,128)(2,1)S(1)}, bf16[192,1408]{1,0:T(8,128)(2,1)S(1)}, u32[]{:S(2)}, u32[]{:S(2)}) collective-permute-start(bf16[192,1408]{1,0:T(8,128)(2,1)S(1)} %add_convert_fusion), channel_id=1, source_target_pairs={{4,0},{12,4},{20,12},{28,20},{24,28},{16,24},{8,16},{0,8},{5,1},{1... | collective-permute-start | bytes 1622024 | tf_op jit(solution)/shard_map/ppermute | solution.py:578
  269.8 11.1 %collective-permute-start.55 = (bf16[192,1408]{1,0:T(8,128)(2,1)S(1)}, bf16[192,1408]{1,0:T(8,128)(2,1)S(1)}, u32[]{:S(2)}, u32[]{:S(2)}) collective-permute-start(bf16[192,1408]{1,0:T(8,128)(2,1)S(1)} %add_convert_fusion.1), channel_id=1, source_target_pairs={{4,12},{12,20},{20,28},{28,24},{24,16},{16,8},{8,0},{0,4},{5,13},{... | collective-permute-start | bytes 1622024 | tf_op jit(solution)/shard_map/ppermute | solution.py:578
  269.9 45.9 %collective-permute-start.64 = (bf16[256,3072]{1,0:T(8,128)(2,1)}, bf16[256,3072]{1,0:T(8,128)(2,1)}, u32[]{:S(2)}, u32[]{:S(2)}) collective-permute-start(bf16[256,3072]{1,0:T(8,128)(2,1)} %w_ref.6), channel_id=1, source_target_pairs={{0,1},{1,0},{2,3},{3,2},{4,5},{5,4},{6,7},{7,6},{8,9},{9,8},{10,11... | collective-permute-start | bytes 4718600 | tf_op jit(solution)/shard_map/ppermute | solution.py:653
  270.0 46.7 %collective-permute-start.66 = (bf16[256,3072]{1,0:T(8,128)(2,1)}, bf16[256,3072]{1,0:T(8,128)(2,1)}, u32[]{:S(2)}, u32[]{:S(2)}) collective-permute-start(bf16[256,3072]{1,0:T(8,128)(2,1)} %collective-permute-done.65.refs_2_), channel_id=1, source_target_pairs={{0,1},{1,0},{2,3},{3,2},{4,5},{5,4},{6,7},{7,6},{8,9},{9,8},{10,11... | collective-permute-start | bytes 4718600 | tf_op jit(solution)/shard_map/ppermute | solution.py:653
  291.4 15.2 %collective-permute-start.61 = (bf16[192,1408]{1,0:T(8,128)(2,1)S(1)}, bf16[192,1408]{1,0:T(8,128)(2,1)S(1)}, u32[]{:S(2)}, u32[]{:S(2)}) collective-permute-start(bf16[192,1408]{1,0:T(8,128)(2,1)S(1)} %pack.1.refs_0_), channel_id=1, source_target_pairs={{4,0},{12,4},{20,12},{28,20},{24,28},{16,24},{8,16},{0,8},{5,1},{1... | collective-permute-start | bytes 1622024 | tf_op jit(solution)/shard_map/ppermute | solution.py:578
  293.2 14.2 %collective-permute-start.60 = (bf16[192,1408]{1,0:T(8,128)(2,1)S(1)}, bf16[192,1408]{1,0:T(8,128)(2,1)S(1)}, u32[]{:S(2)}, u32[]{:S(2)}) collective-permute-start(bf16[192,1408]{1,0:T(8,128)(2,1)S(1)} %pack.1.refs_0_), channel_id=1, source_target_pairs={{4,12},{12,20},{20,28},{28,24},{24,16},{16,8},{8,0},{0,4},{5,13},{... | collective-permute-start | bytes 1622024 | tf_op jit(solution)/shard_map/ppermute | solution.py:578
  293.5 17.9 %collective-permute-start.68 = (bf16[256,512]{1,0:T(8,128)(2,1)S(1)}, bf16[256,512]{1,0:T(8,128)(2,1)S(1)}, u32[]{:S(2)}, u32[]{:S(2)}) collective-permute-start(bf16[256,512]{1,0:T(8,128)(2,1)S(1)} %join.1.refs_0_), channel_id=1, source_target_pairs={{4,0},{12,4},{20,12},{28,20},{24,28},{16,24},{8,16},{0,8},{5,1},{1... | collective-permute-start | bytes 786440 | tf_op jit(solution)/shard_map/ppermute | solution.py:578
  307.4 24.9 %collective-permute-start.62 = (bf16[192,1408]{1,0:T(8,128)(2,1)S(1)}, bf16[192,1408]{1,0:T(8,128)(2,1)S(1)}, u32[]{:S(2)}, u32[]{:S(2)}) collective-permute-start(bf16[192,1408]{1,0:T(8,128)(2,1)S(1)} %collective-permute-done.60.refs_8_), channel_id=1, source_target_pairs={{4,12},{12,20},{20,28},{28,24},{24,16},{16,8},{8,0},{0,4},{5,13},{... | collective-permute-start | bytes 1622024 | tf_op jit(solution)/shard_map/ppermute | solution.py:578
  311.4 20.9 %collective-permute-start.63 = (bf16[192,1408]{1,0:T(8,128)(2,1)S(1)}, bf16[192,1408]{1,0:T(8,128)(2,1)S(1)}, u32[]{:S(2)}, u32[]{:S(2)}) collective-permute-start(bf16[192,1408]{1,0:T(8,128)(2,1)S(1)} %collective-permute-done.61.refs_1_), channel_id=1, source_target_pairs={{4,0},{12,4},{20,12},{28,20},{24,28},{16,24},{8,16},{0,8},{5,1},{1... | collective-permute-start | bytes 1622024 | tf_op jit(solution)/shard_map/ppermute | solution.py:578
  315.8 18.5 %collective-permute-start.31 = (bf16[256,1024]{1,0:T(8,128)(2,1)S(1)}, bf16[256,1024]{1,0:T(8,128)(2,1)S(1)}, u32[]{:S(2)}, u32[]{:S(2)}) collective-permute-start(bf16[256,1024]{1,0:T(8,128)(2,1)S(1)} %copy-done.37), channel_id=1, source_target_pairs={{0,1},{1,0},{2,3},{3,2},{4,5},{5,4},{6,7},{7,6},{8,9},{9,8},{10,11... | collective-permute-start | bytes 1572872 | tf_op jit(solution)/shard_map/ppermute | solution.py:653
  315.8 14.6 %collective-permute-start.69 = (bf16[256,512]{1,0:T(8,128)(2,1)S(1)}, bf16[256,512]{1,0:T(8,128)(2,1)S(1)}, u32[]{:S(2)}, u32[]{:S(2)}) collective-permute-start(bf16[256,512]{1,0:T(8,128)(2,1)S(1)} %collective-permute-done.67.refs_8_), channel_id=1, source_target_pairs={{4,12},{12,20},{20,28},{28,24},{24,16},{16,8},{8,0},{0,4},{5,13},{... | collective-permute-start | bytes 786440 | tf_op jit(solution)/shard_map/ppermute | solution.py:578
  316.7 13.8 %collective-permute-start.70 = (bf16[256,512]{1,0:T(8,128)(2,1)S(1)}, bf16[256,512]{1,0:T(8,128)(2,1)S(1)}, u32[]{:S(2)}, u32[]{:S(2)}) collective-permute-start(bf16[256,512]{1,0:T(8,128)(2,1)S(1)} %collective-permute-done.68.refs_1_), channel_id=1, source_target_pairs={{4,0},{12,4},{20,12},{28,20},{24,28},{16,24},{8,16},{0,8},{5,1},{1... | collective-permute-start | bytes 786440 | tf_op jit(solution)/shard_map/ppermute | solution.py:578
  330.4 25.8 %collective-permute-start.28 = (bf16[256,1024]{1,0:T(8,128)(2,1)S(1)}, bf16[256,1024]{1,0:T(8,128)(2,1)S(1)}, u32[]{:S(2)}, u32[]{:S(2)}) collective-permute-start(bf16[256,1024]{1,0:T(8,128)(2,1)S(1)} %copy-done.35), channel_id=1, source_target_pairs={{0,1},{1,0},{2,3},{3,2},{4,5},{5,4},{6,7},{7,6},{8,9},{9,8},{10,11... | collective-permute-start | bytes 1572872 | tf_op jit(solution)/shard_map/ppermute | solution.py:653
  332.3 21.8 %collective-permute-start.75 = (bf16[192,1408]{1,0:T(8,128)(2,1)S(1)}, bf16[192,1408]{1,0:T(8,128)(2,1)S(1)}, u32[]{:S(2)}, u32[]{:S(2)}) collective-permute-start(bf16[192,1408]{1,0:T(8,128)(2,1)S(1)} %collective-permute-done.62.refs_7_), channel_id=1, source_target_pairs={{4,12},{12,20},{20,28},{28,24},{24,16},{16,8},{8,0},{0,4},{5,13},{... | collective-permute-start | bytes 1622024 | tf_op jit(solution)/shard_map/ppermute | solution.py:578
  334.0 21.8 %collective-permute-start.76 = (bf16[192,1408]{1,0:T(8,128)(2,1)S(1)}, bf16[192,1408]{1,0:T(8,128)(2,1)S(1)}, u32[]{:S(2)}, u32[]{:S(2)}) collective-permute-start(bf16[192,1408]{1,0:T(8,128)(2,1)S(1)} %collective-permute-done.63.refs_2_), channel_id=1, source_target_pairs={{4,0},{12,4},{20,12},{28,20},{24,28},{16,24},{8,16},{0,8},{5,1},{1... | collective-permute-start | bytes 1622024 | tf_op jit(solution)/shard_map/ppermute | solution.py:578
  334.5 23.7 %collective-permute-start.32 = (bf16[256,1024]{1,0:T(8,128)(2,1)S(1)}, bf16[256,1024]{1,0:T(8,128)(2,1)S(1)}, u32[]{:S(2)}, u32[]{:S(2)}) collective-permute-start(bf16[256,1024]{1,0:T(8,128)(2,1)S(1)} %add_convert_fusion.12), channel_id=1, source_target_pairs={{0,2},{1,3},{2,0},{3,1},{4,6},{5,7},{6,4},{7,5},{8,10},{9,11},{10,... | collective-permute-start | bytes 1572872 | tf_op jit(solution)/shard_map/ppermute | solution.py:657
  339.6 14.1 %collective-permute-start.72 = (bf16[256,512]{1,0:T(8,128)(2,1)S(1)}, bf16[256,512]{1,0:T(8,128)(2,1)S(1)}, u32[]{:S(2)}, u32[]{:S(2)}) collective-permute-start(bf16[256,512]{1,0:T(8,128)(2,1)S(1)} %collective-permute-done.70.refs_2_), channel_id=1, source_target_pairs={{4,0},{12,4},{20,12},{28,20},{24,28},{16,24},{8,16},{0,8},{5,1},{1... | collective-permute-start | bytes 786440 | tf_op jit(solution)/shard_map/ppermute | solution.py:578
  (73 other events, 673.5 us)
